TPU v7x, 256 devices: a whole 4x4x8 slice. The times are simulated.
256 devices in a mesh: dom: 64 (over y, z, core), sub: 4 (over x).
Axes of the slice: x: 4, y: 4, z: 8, core: 2. Of those that a mesh axis runs over, the one named last changes fastest.
Arguments:
- displacement: float32 [3, 1048576], P(None, 'dom'), may hold values from -6 to 6
- connect: int32 [20, 196608], P(None, ('dom', 'sub')), may hold values from 0 to 20479
- shear: float32 [196608], P(('dom', 'sub')), may hold values from 0.3 to 3
- bulk: float32 [196608], P(('dom', 'sub')), may hold values from 0.3 to 3
- stiff_shear: float32 [60, 60], replicated, may hold values from -0.75 to 0.75
- stiff_bulk: float32 [60, 60], replicated, may hold values from -0.75 to 0.75
- seg_slave: int32 [8, 65536], P(None, ('dom', 'sub')), may hold values from 0 to 16383
- seg_part: int32 [65536, 1], P(('dom', 'sub')), may hold values from 0 to 63; in each aligned block of 256 rows (0 to 255, 256 to 511, ...) at most 8 rows name the same one
- seg_face: int32 [65536], P(('dom', 'sub')), may hold values from 0 to 2047
- face_nodes: int32 [8, 131072], P(None, 'dom'), may hold values from 0 to 16383
- dual: float32 [8, 65536], P(None, ('dom', 'sub')), may hold values from 0.2 to 2
- mortar: float32 [64, 65536], P(None, ('dom', 'sub')), may hold values from -4 to 4
- seg_count: int32 [256], P(('dom', 'sub')), may hold values from 128 to 256
Outputs:
- product: float32 [3, 1048576], P(None, ('dom', 'sub'))
Inputs may be any that keep to these rules, and one draw needn't show every extreme that they name: `seg_part`: among the 256 segment slots of one device (live or not) no partition is named more than 8 times, a bound that some block reaches.
All inputs are finite; a program needn't handle non-finite values.
Results may differ from a plain program's by a relative error of at most 0.000067.
Values sent between devices are 32-bit elements; how exact they have to be, the bound alone decides.
No kernel may reach another device: no remote copies, remote signals or barrier semaphores. Data moves between devices by JAX's collectives and lax.ppermute only.
A program may use at most 128 MiB of HBM per device.

v0:
```python
import jax
import jax.numpy as jnp
from jax import lax
from jax.sharding import PartitionSpec as P

GHOST = 2048


penalty = 2.0


def with_halo(x, sides, width):
    for axis, dim in sides:
        count, length = (lax.axis_size(axis), x.shape[dim])
        up = [(i, (i + 1) % count) for i in range(count - 1)]
        down = [(j, i) for i, j in up]
        last = lax.slice_in_dim(x, length - width, length, axis=dim)
        first = lax.slice_in_dim(x, 0, width, axis=dim)
        before = lax.ppermute(last, axis, up)
        after = lax.ppermute(first, axis, down)
        x = jnp.concatenate([before, x, after], axis=dim)
    return x


def from_behind(block, axis, distance):
    devices = range(lax.axis_size(axis))
    route = [(i - distance, i) for i in devices if i - distance in devices]
    return lax.ppermute(block, axis, route)


def place_slots(values, slot_index, width):
    return jnp.zeros((values.shape[0], width), jnp.float32).at[:, slot_index].set(values)


def on_device(
    displacement,
    connect,
    shear,
    bulk,
    stiff_shear,
    stiff_bulk,
    seg_slave,
    seg_part,
    seg_face,
    face_nodes,
    dual,
    mortar,
    seg_count,
):
    highest = lax.Precision.HIGHEST
    nodes = displacement.shape[1]
    extended = with_halo(displacement, (("dom", 1),), GHOST)
    element_dofs = extended[:, connect].reshape(60, -1)
    forces = shear * jnp.dot(stiff_shear.T, element_dofs, precision=highest) + bulk * jnp.dot(
        stiff_bulk.T, element_dofs, precision=highest
    )
    partial_ext = (
        jnp.zeros(extended.shape, jnp.float32).at[:, connect].add(forces.reshape(3, 20, -1))
    )
    from_upper = from_behind(partial_ext[:, :GHOST], "dom", -1)
    from_lower = from_behind(partial_ext[:, GHOST + nodes :], "dom", 1)
    segs = seg_face.shape[0]
    n_dom = lax.axis_size("dom")
    capacity = 2 * segs // n_dom
    width = n_dom * capacity
    target = seg_part[:, 0]
    hits = (target[:, None] == jnp.arange(n_dom, dtype=jnp.int32)[None, :]).astype(jnp.int32)
    running = jnp.cumsum(hits, axis=0) - 1
    slot_index = target * capacity + jnp.sum(running * hits, axis=1)
    live = (jnp.arange(segs, dtype=jnp.int32) < seg_count[0]).astype(jnp.float32)
    slave_vals = displacement[:, seg_slave]
    slave_part = (dual * live)[None] * slave_vals
    matrix = (mortar * live).reshape(8, 8, segs)
    face_float = seg_face.astype(jnp.float32)[None]
    payload = jnp.concatenate(
        [slave_part.reshape(24, segs), matrix.reshape(64, segs), face_float], axis=0
    )
    outgoing = place_slots(payload, slot_index, width).reshape(89, n_dom, capacity)
    incoming = lax.all_to_all(outgoing, "dom", split_axis=1, concat_axis=1, tiled=True).reshape(
        89, width
    )
    master_nodes = face_nodes[:, incoming[88].astype(jnp.int32)]
    master_vals = displacement[:, master_nodes]
    matrix_in = incoming[24:88].reshape(8, 8, width)
    gap_in = incoming[:24].reshape(3, 8, width) - jnp.einsum(
        "ijs,cjs->cis", matrix_in, master_vals, precision=highest
    )
    mult_in = penalty * gap_in
    master_force = -jnp.einsum("ijs,cis->cjs", matrix_in, mult_in, precision=highest)
    returned = lax.all_to_all(
        mult_in.reshape(24, n_dom, capacity), "dom", split_axis=1, concat_axis=1, tiled=True
    )
    mult_own = returned.reshape(24, width)[:, slot_index].reshape(3, 8, segs)
    slave_force = dual[None] * mult_own
    owned = partial_ext[:, GHOST : GHOST + nodes]
    owned = owned.at[:, nodes - GHOST :].add(from_upper).at[:, :GHOST].add(from_lower)
    owned = owned.at[:, seg_slave].add(slave_force).at[:, master_nodes].add(master_force)
    return lax.psum_scatter(owned, "sub", scatter_dimension=1, tiled=True)


def solution(mesh):
    placed = (
        P(None, "dom"),
        P(None, ("dom", "sub")),
        P(("dom", "sub")),
        P(("dom", "sub")),
        P(),
        P(),
        P(None, ("dom", "sub")),
        P(("dom", "sub"), None),
        P(("dom", "sub")),
        P(None, "dom"),
        P(None, ("dom", "sub")),
        P(None, ("dom", "sub")),
        P(("dom", "sub")),
    )
    return jax.shard_map(
        on_device, mesh=mesh, in_specs=placed, out_specs=P(None, ("dom", "sub")), check_vma=False
    )
```

profile of v0, /device:TPU:8, one launch (start us, length us, event | category | flops | bytes accessed | tf_op | source)
XLA Modules:
  0.0 418.3 jit_solution(17357392237123456167)
XLA Ops:
  6.6 0.9 fusion.18
  7.4 1.9 collective-permute-start
  9.4 7.1 %collective-permute-start.1 = (f32[3,2048]{1,0:T(4,128)S(1)}, f32[3,2048]{1,0:T(4,128)S(1)}, u32[]{:S(2)}, u32[]{:S(2)}) collective-permute-start(f32[3,2048]{1,0:T(4,128)S(1)} %get-tuple-element.33), channel_id=1, source_target_pairs={{4,0},{8,4},{12,8},{16,12},{20,16},{24,20},{28,24},{32,28},{36,32}... | collective-permute-start | bytes 73736 | tf_op jit(solution)/shard_map/ppermute | solution.py:20
  16.5 5.7 %copy.88 = f32[3,16384]{0,1:T(8,128)} copy(f32[3,16384]{1,0:T(4,128)} %param.17) | data formatting | bytes 393216 | tf_op args[0]
  22.9 8.8 %gather_fusion.1 = f32[2048,3]{1,0:T(8,128)S(1)} fusion(f32[3,16384]{0,1:T(8,128)} %copy.88, s32[2048]{0:T(1024)S(1)} %broadcast_clamp_fusion.2), kind=kCustom, calls=%fused_computation.1 | custom fusion | bytes 57344 | tf_op jit(solution)/shard_map/gather | solution.py:71
  31.7 0.3 multiply_bitcast_fusion
  32.1 0.3 copy.89
  32.5 0.1 copy.90
  32.6 0.6 reduce-window.6
  33.2 0.2 slice_reduce_fusion
  33.4 0.1 fusion.12
  33.6 1.8 scatter_custom_fusion.1
  35.4 9.9 %all-to-all-start = ((f32[89,64,8]{0,2,1:T(8,128)}), f32[89,64,8]{0,2,1:T(8,128)S(1)}, u32[]{:S(2)}, u32[]{:S(2)}) async-start(f32[89,64,8]{0,2,1:T(8,128)} %bitcast.16), calls=%async_computation | async-start | bytes 524288 | tf_op jit(solution)/shard_map/all_to_all | solution.py:79
  45.5 5.5 %copy.79 = f32[3,20480]{0,1:T(8,128)} copy(f32[3,20480]{1,0:T(4,128)S(1)} %pad_maximum_fusion) | data formatting | bytes 491520 | tf_op jit(solution)/shard_map/concatenate | solution.py:21
  51.0 55.1 %gather_fusion = f32[15360,3]{1,0:T(8,128)} fusion(f32[3,20480]{0,1:T(8,128)} %copy.79, s32[15360]{0:T(1024)S(1)} %broadcast_clamp_fusion), kind=kCustom, calls=%fused_computation | custom fusion | bytes 430080 | tf_op jit(solution)/shard_map/gather | solution.py:53
  106.1 5.3 %copy.80 = f32[20,768,3]{1,0,2:T(8,128)S(1)} copy(f32[20,768,3]{2,1,0:T(8,128)} %bitcast.80) | data formatting | bytes 368640 | tf_op jit(solution)/shard_map/gather | solution.py:53
  111.5 0.4 convolution_multiply_fusion.1
  111.9 0.4 fusion.4
  112.3 4.7 %copy.81 = f32[20,768,3]{2,1,0:T(8,128)} copy(f32[20,768,3]{1,0,2:T(8,128)S(1)} %bitcast.89) | data formatting | bytes 368640 | tf_op jit(solution)/shard_map/reshape | solution.py:58
  116.9 86.8 %scatter_custom_fusion = f32[3,20480]{0,1:T(8,128)} fusion(s32[15360]{0:T(1024)S(1)} %reshape.196, f32[15360,3]{1,0:T(8,128)} %bitcast.81, f32[]{:T(128)} %constant.74.clone.1), kind=kCustom, calls=%fused_computation.9 | custom fusion | flops 46080 | bytes 246272 | tf_op jit(solution)/shard_map/scatter-add | solution.py:58
  203.8 2.1 fusion.17
  205.8 0.9 copy.82
  206.8 4.3 %collective-permute-start.2 = (f32[3,2048]{1,0:T(4,128)}, f32[3,2048]{1,0:T(4,128)}, u32[]{:S(2)}, u32[]{:S(2)}) collective-permute-start(f32[3,2048]{1,0:T(4,128)} %copy.82), channel_id=1, source_target_pairs={{4,0},{8,4},{12,8},{16,12},{20,16},{24,20},{28,24},{32,28},{36,32}... | collective-permute-start | bytes 73736 | tf_op jit(solution)/shard_map/ppermute | solution.py:28
  211.1 0.3 copy.92
  211.5 0.7 compare_reduce_fusion
  212.2 5.8 %slice.94 = f32[3,16384]{0,1:T(8,128)} slice(f32[3,20480]{0,1:T(8,128)} %scatter_custom_fusion), slice={[0:3], [2048:18432]} | slice | bytes 393216 | tf_op jit(solution)/shard_map/slice | solution.py:95
  218.0 0.3 copy.83
  218.3 0.3 copy.85
  218.6 2.1 collective-permute-start.3
  220.8 0.8 add.75
  221.5 0.4 copy.84
  221.9 1.0 constant_dynamic-update-slice_fusion
  223.0 3.0 collective-permute-done.3
  226.0 0.4 copy.86
  226.4 2.9 fusion.5
  229.3 1.2 fusion.8
  230.7 1.0 gather_fusion.2
  231.8 0.1 copy.93
  231.9 14.2 %gather_fusion.3 = f32[4096,3]{1,0:T(8,128)S(1)} fusion(f32[3,16384]{0,1:T(8,128)} %copy.88, s32[4096]{0:T(1024)S(1)} %broadcast_clamp_fusion.1), kind=kCustom, calls=%fused_computation.3 | custom fusion | bytes 114688 | tf_op jit(solution)/shard_map/gather | solution.py:83
  246.0 3.4 copy.95
  249.4 0.8 slice.102
  250.3 1.6 reshape.236
  251.9 4.5 %fusion.6 = f32[512,3,8]{2,1,0:T(4,128)} fusion(f32[8,8,512]{1,0,2:T(8,128)S(1)} %reshape.236, f32[8,512,3]{0,2,1:T(4,128)S(1)} %copy.95), kind=kOutput, calls=%fused_computation.19 | convolution fusion | flops 1179648 | bytes 229376 | tf_op jit(solution)/shard_map/ijs,cjs->cis/dot_general | solution.py:85
  256.4 1.4 copy.98
  257.9 0.7 copy.91
  258.6 0.4 reshape.149
  259.0 0.4 reshape.151
  259.5 1.3 copy.102
  260.8 0.4 copy.99
  261.2 0.9 reshape.243
  262.1 7.3 %all-to-all-start.1 = ((f32[64,1,192]{2,1,0:T(1,128)}), f32[64,1,192]{2,1,0:T(1,128)S(1)}, u32[]{:S(2)}, u32[]{:S(2)}) async-start(f32[64,1,192]{2,1,0:T(1,128)} %reshape.243), calls=%async_computation.1 | async-start | bytes 131072 | tf_op jit(solution)/shard_map/all_to_all | solution.py:90
  269.4 0.3 reduce-scatter.2.cloned.1.call-start
  269.7 4.7 %fusion.2 = f32[8,512,3]{0,2,1:T(4,128)S(1)} fusion(f32[3,8,512]{1,0,2:T(4,128)} %copy.102, f32[8,8,512]{1,0,2:T(8,128)S(1)} %reshape.236), kind=kOutput, calls=%fused_computation.13 | convolution fusion | flops 1191936 | bytes 229376 | tf_op jit(solution)/shard_map/ijs,cis->cjs/dot_general | solution.py:89
  274.3 3.3 copy.109
  277.6 0.6 all-to-all-done.1
  278.2 0.5 broadcast.178
  278.7 0.8 reduce.14
  279.5 0.1 reshape.244
  279.7 0.7 gather_fusion.4
  280.5 0.4 copy.108
  280.9 17.1 %scatter_fusion = f32[3,16384]{0,1:T(8,128)} fusion(f32[3,16384]{0,1:T(8,128)} %fusion.5, s32[2048]{0:T(1024)S(1)} %bitcast.95, f32[2048,3]{1,0:T(8,128)S(1)} %bitcast.85), kind=kCustom, calls=%fused_computation.7 | custom fusion | flops 6144 | bytes 81920 | tf_op jit(solution)/shard_map/scatter-add | solution.py:97
  297.9 27.1 %scatter_fusion.1 = f32[3,16384]{0,1:T(8,128)} fusion(f32[3,16384]{0,1:T(8,128)} %scatter_fusion, s32[4096]{0:T(1024)S(1)} %bitcast.92, f32[4096,3]{1,0:T(8,128)S(1)} %bitcast.82), kind=kCustom, calls=%fused_computation.8 | custom fusion | flops 12288 | bytes 163840 | tf_op jit(solution)/shard_map/scatter-add | solution.py:97
  325.1 83.5 %reduce-scatter.2.cloned.1.call-done = f32[3,4096]{0,1:T(8,128)} async-done(((f32[3,16384]{0,1:T(8,128)}), f32[3,4096]{0,1:T(8,128)}) %reduce-scatter.2.cloned.1.call-update) | async-done | bytes 49168 | tf_op jit(solution)/shard_map/reduce_scatter | solution.py:98
  408.6 2.8 copy.106
  (60 shorter events, 0.6 us)
Async XLA Ops:
  6.5 104.9 %copy-start = (f32[60,60]{1,0:T(8,128)S(1)}, f32[60,60]{1,0:T(8,128)}, u32[]{:S(2)}) copy-start(f32[60,60]{1,0:T(8,128)} %param.21) | copy-start | bytes 43204
  6.5 38.8 %copy-start.2 = (f32[3,16384]{1,0:T(4,128)S(1)}, f32[3,16384]{1,0:T(4,128)}, u32[]{:S(2)}) copy-start(f32[3,16384]{1,0:T(4,128)} %param.17) | copy-start | bytes 589828
  6.5 15.6 %copy-start.9 = (s32[8,256]{1,0:T(8,128)S(1)}, s32[8,256]{1,0:T(8,128)}, u32[]{:S(2)}) copy-start(s32[8,256]{1,0:T(8,128)} %param.23) | copy-start | bytes 24580
  6.5 25.2 %copy-start.7 = (f32[8,256]{1,0:T(8,128)S(1)}, f32[8,256]{1,0:T(8,128)}, u32[]{:S(2)}) copy-start(f32[8,256]{1,0:T(8,128)} %param.27) | copy-start | bytes 24580
  6.5 25.9 %copy-start.5 = (f32[64,256]{1,0:T(8,128)S(1)}, f32[64,256]{1,0:T(8,128)}, u32[]{:S(2)}) copy-start(f32[64,256]{1,0:T(8,128)} %param.28) | copy-start | bytes 196612
  6.5 25.9 %copy-start.12 = (s32[256]{0:T(256)S(1)}, s32[256]{0:T(256)}, u32[]{:S(2)}) copy-start(s32[256]{0:T(256)} %param.25) | copy-start | bytes 3076
  6.6 26.0 %copy-start.8 = (s32[256,1]{0,1:T(1,128)S(1)}, s32[256,1]{0,1:T(1,128)}, u32[]{:S(2)}) copy-start(s32[256,1]{0,1:T(1,128)} %param.24) | copy-start | bytes 3076
  6.6 38.7 %copy-start.3 = (s32[20,768]{1,0:T(8,128)S(1)}, s32[20,768]{1,0:T(8,128)}, u32[]{:S(2)}) copy-start(s32[20,768]{1,0:T(8,128)} %param.18) | copy-start | bytes 184324
  7.4 37.9 %collective-permute-start = (f32[3,2048]{1,0:T(4,128)S(1)}, f32[3,2048]{1,0:T(4,128)S(1)}, u32[]{:S(2)}, u32[]{:S(2)}) collective-permute-start(f32[3,2048]{1,0:T(4,128)S(1)} %get-tuple-element.32), channel_id=1, source_target_pairs={{0,4},{4,8},{8,12},{12,16},{16,20},{20,24},{24,28},{28,32},{32,36}... | collective-permute-start | bytes 73736 | tf_op jit(solution)/shard_map/ppermute | solution.py:19
  9.4 36.0 %collective-permute-start.1 = (f32[3,2048]{1,0:T(4,128)S(1)}, f32[3,2048]{1,0:T(4,128)S(1)}, u32[]{:S(2)}, u32[]{:S(2)}) collective-permute-start(f32[3,2048]{1,0:T(4,128)S(1)} %get-tuple-element.33), channel_id=1, source_target_pairs={{4,0},{8,4},{12,8},{16,12},{20,16},{24,20},{28,24},{32,28},{36,32}... | collective-permute-start | bytes 73736 | tf_op jit(solution)/shard_map/ppermute | solution.py:20
  35.4 193.9 %all-to-all-start = ((f32[89,64,8]{0,2,1:T(8,128)}), f32[89,64,8]{0,2,1:T(8,128)S(1)}, u32[]{:S(2)}, u32[]{:S(2)}) async-start(f32[89,64,8]{0,2,1:T(8,128)} %bitcast.16), calls=%async_computation | async-start | bytes 524288 | tf_op jit(solution)/shard_map/all_to_all | solution.py:79
  45.4 66.0 %copy-start.10 = (f32[768]{0:T(1024)S(1)}, f32[768]{0:T(1024)}, u32[]{:S(2)}) copy-start(f32[768]{0:T(1024)} %param.19) | copy-start | bytes 9220
  45.5 66.4 %copy-start.6 = (f32[60,60]{1,0:T(8,128)S(1)}, f32[60,60]{1,0:T(8,128)}, u32[]{:S(2)}) copy-start(f32[60,60]{1,0:T(8,128)} %param.22) | copy-start | bytes 43204
  45.5 66.4 %copy-start.11 = (f32[768]{0:T(1024)S(1)}, f32[768]{0:T(1024)}, u32[]{:S(2)}) copy-start(f32[768]{0:T(1024)} %param.20) | copy-start | bytes 9220
  116.9 94.2 %copy-start.4 = (s32[8,2048]{1,0:T(8,128)S(1)}, s32[8,2048]{1,0:T(8,128)}, u32[]{:S(2)}) copy-start(s32[8,2048]{1,0:T(8,128)} %param.26) | copy-start | bytes 196612
  206.8 14.0 %collective-permute-start.2 = (f32[3,2048]{1,0:T(4,128)}, f32[3,2048]{1,0:T(4,128)}, u32[]{:S(2)}, u32[]{:S(2)}) collective-permute-start(f32[3,2048]{1,0:T(4,128)} %copy.82), channel_id=1, source_target_pairs={{4,0},{8,4},{12,8},{16,12},{20,16},{24,20},{28,24},{32,28},{36,32}... | collective-permute-start | bytes 73736 | tf_op jit(solution)/shard_map/ppermute | solution.py:28
  218.6 7.3 %collective-permute-start.3 = (f32[3,2048]{1,0:T(4,128)S(1)}, f32[3,2048]{1,0:T(4,128)S(1)}, u32[]{:S(2)}, u32[]{:S(2)}) collective-permute-start(f32[3,2048]{1,0:T(4,128)S(1)} %copy.85), channel_id=1, source_target_pairs={{0,4},{4,8},{8,12},{12,16},{16,20},{20,24},{24,28},{28,32},{32,36}... | collective-permute-start | bytes 73736 | tf_op jit(solution)/shard_map/ppermute | solution.py:28
  262.1 16.1 %all-to-all-start.1 = ((f32[64,1,192]{2,1,0:T(1,128)}), f32[64,1,192]{2,1,0:T(1,128)S(1)}, u32[]{:S(2)}, u32[]{:S(2)}) async-start(f32[64,1,192]{2,1,0:T(1,128)} %reshape.243), calls=%async_computation.1 | async-start | bytes 131072 | tf_op jit(solution)/shard_map/all_to_all | solution.py:90
  269.4 139.2 %reduce-scatter.2.cloned.1.call-start = ((), (), s32[]{:S(2)}) async-start(), calls=%async_computation.3 | async-start | bytes 10485760 | tf_op jit(solution)/shard_map/reduce_scatter | solution.py:98
  297.9 113.5 %copy-start.1 = (f32[60,60]{1,0:T(8,128)S(1)}, f32[60,60]{1,0:T(8,128)}, u32[]{:S(2)}) copy-start(f32[60,60]{1,0:T(8,128)} %param.21) | copy-start | bytes 43204
Sparse Core Ops, SparseCore 0:
  325.2 83.3 reduce-scatter.1
where the time goes:
time: 420 us; the launch traced here: 418 us
  other arithmetic  139 us (33%)
  local copies, waits for them, and re-layouts  135 us (32%)
  waiting for transfers between devices  87.2 us (21%)
  starting transfers between devices  32.8 us (8%)
  between operations  14.6 us (3%)
  matrix products  9.91 us (2%)
    scatter-add x1, other arithmetic, on_device(): jnp.zeros(extended.shape, jnp.float32).at[:, connect]  86.8 us
    reduce_scatter x1, waiting for transfers between devices, on_device(): return lax.psum_scatter(owned, 'sub', scatter_dimension=1, tiled=True)  83.5 us
    gather x2, local copies, waits for them, and re-layouts, on_device(): element_dofs = extended[:, connect].reshape(60, -1)  60.4 us
    scatter-add x2, other arithmetic, on_device(): owned.at[:, seg_slave].add(slave_force).at[:, master_nodes]  44.2 us
    gather x2, local copies, waits for them, and re-layouts, on_device(): master_vals = displacement[:, master_nodes]  17.6 us
    all_to_all x1, starting transfers between devices, on_device(): lax.all_to_all(outgoing, 'dom', split_axis=1, concat_axis=1, tiled=True)  9.87 us
    gather x1, local copies, waits for them, and re-layouts, on_device(): slave_vals = displacement[:, seg_slave]  8.84 us
  transfers between devices with their start and end apart: 7, of which 3 were waited for; matrix products, arithmetic and copies ran while one was open for 48% of the time, Pallas kernels for 0%

commit v1 on v0

v1 whole, which is shorter than its diff:
```python
import jax
import jax.numpy as jnp
from jax import lax
from jax.experimental import pallas as pl
from jax.experimental.pallas import tpu as pltpu
from jax.sharding import PartitionSpec as P

GHOST = 2048
LO = 256
penalty = 2.0
F32 = jnp.float32
BF16 = jnp.bfloat16


def pieces(x):
    first = x.astype(BF16)
    second = (x - first.astype(F32)).astype(BF16)
    return first, second


def one_hot_lo(index):
    n = index.shape[1]
    rows = lax.broadcasted_iota(jnp.int32, (LO, n), 0)
    return jnp.where(rows == (index & (LO - 1)), 1.0, 0.0).astype(BF16)


def hi_mask(index, rows):
    n = index.shape[1]
    return lax.broadcasted_iota(jnp.int32, (rows, n), 0) == (index >> 8)


def to_rows(source, offset, count, target, first_row, stride):
    for c in range(3):
        for h in range(count):
            row = c * stride + first_row + h
            target[row : row + 1, :] = source[c : c + 1, offset + h * LO : offset + (h + 1) * LO]


def gather_column(table, index, rows):
    hot = one_hot_lo(index)
    picked = jnp.dot(table, jnp.concatenate([hot, hot], axis=0), preferred_element_type=F32)
    mask = hi_mask(index, rows)
    return [
        jnp.sum(jnp.where(mask, picked[c * rows : (c + 1) * rows], 0.0), axis=0, keepdims=True)
        for c in range(3)
    ]


def scatter_column(values, index, rows):
    hot = one_hot_lo(index)
    mask = hi_mask(index, rows)
    firsts, seconds = [], []
    for c in range(3):
        first, second = pieces(values[c])
        firsts.append(jnp.where(mask, first.astype(F32), 0.0).astype(BF16))
        seconds.append(jnp.where(mask, second.astype(F32), 0.0).astype(BF16))
    spread = jnp.concatenate(
        [jnp.concatenate(firsts, axis=0), jnp.concatenate(seconds, axis=0)], axis=1
    )
    return lax.dot_general(
        spread,
        jnp.concatenate([hot, hot], axis=1),
        (((1,), (1,)), ((), ())),
        preferred_element_type=F32,
    )


def forces_kernel(disp, before, after, connect, shear, bulk, k_shear, k_bulk, out, rows, table, dofs):
    nodes = disp.shape[1]
    ghost = GHOST // LO
    total = nodes // LO + 2 * ghost
    to_rows(before, 0, ghost, rows, 0, total)
    to_rows(disp, 0, nodes // LO, rows, ghost, total)
    to_rows(after, 0, ghost, rows, total - ghost, total)
    first, second = pieces(rows[...])
    table[:, :LO] = first
    table[:, LO:] = second
    dofs[...] = jnp.zeros_like(dofs)

    def step(a, carry):
        got = gather_column(table[...], connect[pl.ds(a, 1), :], total)
        for c in range(3):
            dofs[pl.ds(20 * c + a, 1), :] = got[c]
        return carry

    lax.fori_loop(0, 20, step, 0)
    g_first, g_second = pieces(dofs[...])
    g = jnp.concatenate([g_first, g_first, g_second, g_second], axis=0)

    def product(k):
        k_first, k_second = pieces(k[...])
        wide = jnp.concatenate([k_first, k_second, k_first, k_second], axis=1)
        return jnp.dot(wide, g, preferred_element_type=F32)

    out[...] = shear[...] * product(k_shear) + bulk[...] * product(k_bulk)


def element_scatter_kernel(forces, connect, owned, low, high, total):
    ghost = GHOST // LO
    all_rows = total.shape[0] // 3
    total[...] = jnp.zeros_like(total)

    def step(a, carry):
        values = [forces[pl.ds(20 * c + a, 1), :] for c in range(3)]
        total[...] += scatter_column(values, connect[pl.ds(a, 1), :], all_rows)
        return carry

    lax.fori_loop(0, 20, step, 0)
    own = all_rows - 2 * ghost
    for c in range(3):
        base = c * all_rows
        low[c * ghost : (c + 1) * ghost, :] = total[base : base + ghost, :]
        owned[c * own : (c + 1) * own, :] = total[base + ghost : base + ghost + own, :]
        high[c * ghost : (c + 1) * ghost, :] = total[base + ghost + own : base + all_rows, :]


def pack_kernel(disp, slave, dual, mortar, face, part, count, out, slot_out, rows, table):
    segs = slave.shape[1]
    own = disp.shape[1] // LO
    to_rows(disp, 0, own, rows, 0, own)
    first, second = pieces(rows[...])
    packed = jnp.concatenate([first, second], axis=1)
    cap = 8
    width = out.shape[0]
    n_dom = width // cap
    lanes = lax.broadcasted_iota(jnp.int32, (1, segs), 1)
    live = jnp.where(lanes < count[0, 0], 1.0, 0.0)
    vals = []
    for i in range(8):
        vals.append(gather_column(packed, slave[i : i + 1, :], own))
    slave_part = [
        (dual[i : i + 1, :] * live) * vals[i][c] for c in range(3) for i in range(8)
    ]
    payload = jnp.concatenate(
        slave_part
        + [mortar[...] * live, face[...].astype(F32), jnp.zeros((39, segs), F32)],
        axis=0,
    )
    hits = lax.broadcasted_iota(jnp.int32, (n_dom, segs), 0) == part[...]
    hits_b = jnp.where(hits, 1.0, 0.0).astype(BF16)
    earlier = (
        lax.broadcasted_iota(jnp.int32, (segs, segs), 0)
        < lax.broadcasted_iota(jnp.int32, (segs, segs), 1)
    )
    before = jnp.dot(
        hits_b, jnp.where(earlier, 1.0, 0.0).astype(BF16), preferred_element_type=F32
    )
    rank = jnp.sum(jnp.where(hits, before, 0.0), axis=0, keepdims=True).astype(jnp.int32)
    slot = part[...] * cap + rank
    slot_out[...] = slot
    place = jnp.where(
        lax.broadcasted_iota(jnp.int32, (width, segs), 0) == slot, 1.0, 0.0
    ).astype(BF16)
    p1 = payload.astype(BF16)
    rest = payload - p1.astype(F32)
    p2 = rest.astype(BF16)
    p3 = (rest - p2.astype(F32)).astype(BF16)
    out[...] = lax.dot_general(
        jnp.concatenate([place, place, place], axis=1),
        jnp.concatenate([p1, p2, p3], axis=1),
        (((1,), (1,)), ((), ())),
        preferred_element_type=F32,
    )


def master_kernel(incoming, disp, faces, mult_out, force_out, nodes_out, rows):
    own = disp.shape[1] // LO
    width = incoming.shape[0]
    n_dom = width // 8
    to_rows(disp, 0, own, rows, 0, own)
    first, second = pieces(rows[...])
    packed = jnp.concatenate([first, second], axis=1)
    got = incoming[...].T
    face = got[88:89, :].astype(jnp.int32)
    groups = faces.shape[1] // LO
    listing = jnp.concatenate([faces[:, g * LO : (g + 1) * LO] for g in range(groups)], axis=0)
    f_first = (listing >> 7).astype(F32).astype(BF16)
    f_second = (listing & 127).astype(F32).astype(BF16)
    hot = one_hot_lo(face)
    f_table = jnp.concatenate([f_first, f_second], axis=0)
    picked = jnp.dot(f_table, hot, preferred_element_type=F32)
    both = picked[: 8 * groups] * 128.0 + picked[8 * groups :]
    face_hi = face >> 8
    nodes = jnp.zeros((8, width), F32)
    for g in range(groups):
        nodes = nodes + jnp.where(face_hi == g, both[8 * g : 8 * (g + 1)], 0.0)
    nodes = nodes.astype(jnp.int32)
    nodes_out[...] = nodes
    vals = [gather_column(packed, nodes[j : j + 1, :], own) for j in range(8)]
    matrix = [got[24 + 8 * i : 32 + 8 * i, :] for i in range(8)]
    mults = []
    for c in range(3):
        master = jnp.concatenate([vals[j][c] for j in range(8)], axis=0)
        force = jnp.zeros((8, width), F32)
        for i in range(8):
            gap = got[8 * c + i : 8 * c + i + 1, :] - jnp.sum(
                matrix[i] * master, axis=0, keepdims=True
            )
            mult = penalty * gap
            mults.append(mult)
            force = force - matrix[i] * mult
        force_out[8 * c : 8 * c + 8, :] = force
    back = jnp.concatenate(mults + [jnp.zeros((8, width), F32)], axis=0).T
    back = back.reshape(n_dom, 8, 32)
    for k in range(8):
        mult_out[:, 0, 32 * k : 32 * (k + 1)] = back[:, k, :]


def master_scatter_kernel(force, nodes, out):
    own = out.shape[0] // 3
    total = jnp.zeros(out.shape, F32)
    for j in range(8):
        values = [force[8 * c + j : 8 * c + j + 1, :] for c in range(3)]
        total = total + scatter_column(values, nodes[j : j + 1, :], own)
    out[...] = total


def slave_kernel(returned, slot, dual, slave, owned, master, upper, lower, out):
    own = owned.shape[0] // 3
    ghost = upper.shape[0] // 3
    segs = slot.shape[1]
    n_dom = returned.shape[0]
    mult_rows = returned[...].reshape(n_dom, 256).T
    m1 = mult_rows.astype(BF16)
    rest = mult_rows - m1.astype(F32)
    m2 = rest.astype(BF16)
    m3 = (rest - m2.astype(F32)).astype(BF16)
    hot = jnp.where(
        lax.broadcasted_iota(jnp.int32, (n_dom, segs), 0) == (slot[...] >> 3), 1.0, 0.0
    ).astype(BF16)
    picked = jnp.dot(
        jnp.concatenate([m1, m2, m3], axis=1),
        jnp.concatenate([hot, hot, hot], axis=0),
        preferred_element_type=F32,
    )
    rank = slot[...] & 7
    mult = jnp.zeros((32, segs), F32)
    for k in range(8):
        mult = mult + jnp.where(rank == k, picked[32 * k : 32 * (k + 1)], 0.0)
    total = owned[...] + master[...]
    for i in range(8):
        values = [dual[i : i + 1, :] * mult[8 * c + i : 8 * c + i + 1, :] for c in range(3)]
        total = total + scatter_column(values, slave[i : i + 1, :], own)
    quarters = out.shape[0]
    per = own // quarters
    for c in range(3):
        block = total[c * own : (c + 1) * own]
        for q in range(quarters):
            part = block[q * per : (q + 1) * per]
            if q == 0:
                part = jnp.concatenate(
                    [part[:ghost] + lower[c * ghost : (c + 1) * ghost, :], part[ghost:]], axis=0
                )
            if q == quarters - 1:
                part = jnp.concatenate(
                    [part[:-ghost], part[-ghost:] + upper[c * ghost : (c + 1) * ghost, :]], axis=0
                )
            out[q, c * per : (c + 1) * per, :] = part


def finish_kernel(own_part, a, b, d, out):
    per = own_part.shape[0] // 3
    total = own_part[...] + a[...] + b[...] + d[...]
    for c in range(3):
        for h in range(per):
            out[c : c + 1, h * LO : (h + 1) * LO] = total[c * per + h : c * per + h + 1, :]


def call(kernel, outs, *args, scratch=(), smem=()):
    specs = [
        pl.BlockSpec(memory_space=pltpu.SMEM if i in smem else pltpu.VMEM)
        for i in range(len(args))
    ]
    many = isinstance(outs, list)
    return pl.pallas_call(
        kernel,
        out_shape=outs,
        in_specs=specs,
        out_specs=[pl.BlockSpec(memory_space=pltpu.VMEM)] * len(outs)
        if many
        else pl.BlockSpec(memory_space=pltpu.VMEM),
        scratch_shapes=list(scratch),
        compiler_params=pltpu.CompilerParams(vmem_limit_bytes=48 * 1024 * 1024),
    )(*args)


def shape(*dims):
    return jax.ShapeDtypeStruct(dims, F32)


def element_forces(displacement, before, after, connect, shear, bulk, k_shear, k_bulk):
    nodes = displacement.shape[1]
    rows = nodes // LO + 2 * GHOST // LO
    elems = connect.shape[1]
    k_shear = jnp.pad(k_shear.T, ((0, 4), (0, 4)))
    k_bulk = jnp.pad(k_bulk.T, ((0, 4), (0, 4)))
    return call(
        forces_kernel,
        shape(64, elems),
        displacement,
        before,
        after,
        connect,
        shear[None],
        bulk[None],
        k_shear,
        k_bulk,
        scratch=[
            pltpu.VMEM((3 * rows, LO), F32),
            pltpu.VMEM((3 * rows, 2 * LO), BF16),
            pltpu.VMEM((64, elems), F32),
        ],
    )


def element_scatter(forces, connect, nodes):
    own = nodes // LO
    ghost = GHOST // LO
    return call(
        element_scatter_kernel,
        [shape(3 * own, LO), shape(3 * ghost, LO), shape(3 * ghost, LO)],
        forces,
        connect,
        scratch=[pltpu.VMEM((3 * (own + 2 * ghost), LO), F32)],
    )


def pack(displacement, seg_slave, dual, mortar, seg_face, seg_part, seg_count, n_dom):
    own = displacement.shape[1] // LO
    segs = seg_face.shape[0]
    return call(
        pack_kernel,
        [shape(n_dom * 8, 128), jax.ShapeDtypeStruct((1, segs), jnp.int32)],
        displacement,
        seg_slave,
        dual,
        mortar,
        seg_face[None],
        seg_part.reshape(1, segs),
        seg_count.reshape(1, 1),
        smem=(6,),
        scratch=[pltpu.VMEM((3 * own, LO), F32), pltpu.VMEM((3 * own, 2 * LO), BF16)],
    )


def master(incoming, displacement, face_nodes):
    own = displacement.shape[1] // LO
    width = incoming.shape[0]
    return call(
        master_kernel,
        [
            shape(width // 8, 1, 256),
            shape(24, width),
            jax.ShapeDtypeStruct((8, width), jnp.int32),
        ],
        incoming,
        displacement,
        face_nodes,
        scratch=[pltpu.VMEM((3 * own, LO), F32)],
    )


def slave_side(returned, slot, dual, seg_slave, owned, master_part, upper, lower, n_sub):
    own = owned.shape[0] // 3
    return call(
        slave_kernel,
        shape(n_sub, 3 * own // n_sub, LO),
        returned,
        slot,
        dual,
        seg_slave,
        owned,
        master_part,
        upper,
        lower,
    )


def on_device(
    displacement,
    connect,
    shear,
    bulk,
    stiff_shear,
    stiff_bulk,
    seg_slave,
    seg_part,
    seg_face,
    face_nodes,
    dual,
    mortar,
    seg_count,
):
    nodes = displacement.shape[1]
    n_dom, n_sub = lax.axis_size("dom"), lax.axis_size("sub")
    up = [(i, i + 1) for i in range(n_dom - 1)]
    down = [(i + 1, i) for i in range(n_dom - 1)]
    before = lax.ppermute(displacement[:, nodes - GHOST :], "dom", up)
    after = lax.ppermute(displacement[:, :GHOST], "dom", down)
    outgoing, slot = pack(
        displacement, seg_slave, dual, mortar, seg_face, seg_part, seg_count, n_dom
    )
    incoming = lax.all_to_all(
        outgoing.reshape(n_dom, 8, 128), "dom", split_axis=0, concat_axis=0, tiled=True
    )
    forces = element_forces(
        displacement, before, after, connect, shear, bulk, stiff_shear, stiff_bulk
    )
    mult, master_force, master_nodes = master(
        incoming.reshape(n_dom * 8, 128), displacement, face_nodes
    )
    returned = lax.all_to_all(mult, "dom", split_axis=0, concat_axis=0, tiled=True)
    owned, low, high = element_scatter(forces, connect, nodes)
    upper = lax.ppermute(low, "dom", down)
    lower = lax.ppermute(high, "dom", up)
    master_part = call(
        master_scatter_kernel, shape(3 * nodes // LO, LO), master_force, master_nodes
    )
    blocks = slave_side(
        returned, slot, dual, seg_slave, owned, master_part, upper, lower, n_sub
    )
    me = lax.axis_index("sub")
    sent = [
        lax.ppermute(
            lax.dynamic_index_in_dim(blocks, (me + k) % n_sub, 0, keepdims=False),
            "sub",
            [(s, (s + k) % n_sub) for s in range(n_sub)],
        )
        for k in range(1, n_sub)
    ]
    mine = lax.dynamic_index_in_dim(blocks, me, 0, keepdims=False)
    return call(finish_kernel, shape(3, nodes // n_sub), mine, *sent)


def solution(mesh):
    placed = (
        P(None, "dom"),
        P(None, ("dom", "sub")),
        P(("dom", "sub")),
        P(("dom", "sub")),
        P(),
        P(),
        P(None, ("dom", "sub")),
        P(("dom", "sub"), None),
        P(("dom", "sub")),
        P(None, "dom"),
        P(None, ("dom", "sub")),
        P(None, ("dom", "sub")),
        P(("dom", "sub")),
    )
    return jax.shard_map(
        on_device, mesh=mesh, in_specs=placed, out_specs=P(None, ("dom", "sub")), check_vma=False
    )
```

time: 420 us -> 89.5 us (0.21)
  other arithmetic: 139 us -> 0 us
  local copies, waits for them, and re-layouts: 135 us -> 5.02 us
  waiting for transfers between devices: 87.2 us -> 6.91 us
  Pallas kernels: 0 us -> 25 us
  blocking collectives: 0 us -> 23.6 us
  between operations: 14.6 us -> 0.94 us
  matrix products: 9.91 us -> 0 us
  starting transfers between devices: 32.8 us -> 27.4 us
    scatter-add x4 -> x0, other arithmetic: 134 us -> none  [the longest x1 86.8 us: on_device(): jnp.zeros(extended.shape, jnp.float32).at[:, connect]]
    gather x8 -> x0, local copies, waits for them, and re-layouts: 88.7 us -> none  [the longest x2 60.4 us: on_device(): element_dofs = extended[:, connect].reshape(60, -1)]
    reduce_scatter x1 -> x0, waiting for transfers between devices: 83.5 us -> none  [on_device(): return lax.psum_scatter(owned, 'sub', scatter_dimension=1, tiled=True)]
    pallas_call x0 -> x7, Pallas kernels: none -> 25 us  [call(): pl.pallas_call(kernel, out_shape=outs, in_specs=specs, out_specs=[pl.Bloc...]
    all_to_all x0 -> x1, blocking collectives: none -> 23.6 us  [on_device(): lax.all_to_all(outgoing.reshape(n_dom, 8, 128), 'dom', split_axis=0, conc...]
    slice x7 -> x1, local copies, waits for them, and re-layouts: 11.6 us -> 0.01 us  [on_device(): after = lax.ppermute(displacement[:, :GHOST], 'dom', down)]
    all_to_all x2 -> x1, starting transfers between devices: 17.2 us -> 6.49 us  [on_device(): lax.all_to_all(mult, 'dom', split_axis=0, concat_axis=0, tiled=True)]
    dot_general x4 -> x0, matrix products: 9.91 us -> none  [the longest x1 4.65 us: on_device(): jnp.einsum('ijs,cis->cjs', matrix_in, mult_in, precision=highest)]
  transfers between devices with their start and end apart: 7 -> 8, of which waited for: 3 -> 4; matrix products, arithmetic and copies ran while one was open for 48% -> 0% of each run, Pallas kernels for 0% -> 21%
where the time goes in v1:
time: 89.5 us; the launch traced here: 88.8 us
  starting transfers between devices  27.4 us (31%)
  Pallas kernels  25 us (28%)
  blocking collectives  23.6 us (26%)
  waiting for transfers between devices  6.91 us (8%)
  local copies, waits for them, and re-layouts  5.02 us (6%)
  between operations  0.94 us (1%)
    pallas_call x7, Pallas kernels, call(): pl.pallas_call(kernel, out_shape=outs, in_specs=specs, out_specs=[pl.Bloc...  25 us
    all_to_all x1, blocking collectives, on_device(): lax.all_to_all(outgoing.reshape(n_dom, 8, 128), 'dom', split_axis=0, conc...  23.6 us
    all_to_all x1, starting transfers between devices, on_device(): lax.all_to_all(mult, 'dom', split_axis=0, concat_axis=0, tiled=True)  6.49 us
    ppermute x3, starting transfers between devices, on_device(): lax.ppermute(lax.dynamic_index_in_dim(blocks, (me + k) % n_sub, 0, keepdi...  5.73 us
    ppermute x1, starting transfers between devices, on_device(): after = lax.ppermute(displacement[:, :GHOST], 'dom', down)  5.61 us
    ppermute x1, starting transfers between devices, on_device(): upper = lax.ppermute(low, 'dom', down)  5.54 us
    unnamed x32, local copies, waits for them, and re-layouts  4.97 us
    ppermute x1, waiting for transfers between devices, on_device(): lower = lax.ppermute(high, 'dom', up)  3.63 us
  transfers between devices with their start and end apart: 8, of which 4 were waited for; matrix products, arithmetic and copies ran while one was open for 0% of the time, Pallas kernels for 21%

profile of v1, /device:TPU:8, one launch (start us, length us, event | category | flops | bytes accessed | tf_op | source)
XLA Modules:
  0.0 88.8 jit_solution(10490996560487437068)
XLA Ops:
  0.7 0.0 copy-start.10
  0.7 0.0 copy-start.9
  0.7 0.7 copy-done.10
  1.3 0.0 copy-done.9
  1.3 0.0 copy-start
  1.4 0.9 %copy-done = f32[3,16384]{1,0:T(4,128)S(1)} copy-done((f32[3,16384]{1,0:T(4,128)S(1)}, f32[3,16384]{1,0:T(4,128)}, u32[]{:S(2)}) %copy-start) | copy-done | bytes 196632
  2.3 0.0 copy-start.4
  2.3 0.8 copy-done.4
  3.1 0.0 copy-start.5
  3.1 0.7 copy-done.5
  3.8 0.0 copy-start.7
  3.8 0.7 copy-done.7
  4.5 1.3 %shard_map.127 = (f32[512,128]{1,0:T(8,128)S(1)}, s32[1,256]{1,0:T(1,128)S(1)}) custom-call(f32[3,16384]{1,0:T(4,128)S(1)} %copy-done, s32[8,256]{1,0:T(8,128)S(1)} %copy-done.5, f32[8,256]{1,0:T(8,128)S(1)} %copy-done.7, f32[64,256]{1,0:T(8,128)S(1)} %copy-done.4, s32[1,256]{1,0:T(1,128)S(1)} %bitcast.18, s32[1,256]{1,0:T(1,128)S(1)} %bitcast.19, ...), custom_call_target="tpu_custom_call" | custom-call | tf_op jit(solution)/shard_map/pallas_call | solution.py:275
  5.8 0.0 copy-start.3
  5.8 23.6 %all_to_all.10 = f32[64,8,128]{2,1,0:T(8,128)S(1)} all-to-all(f32[64,8,128]{2,1,0:T(8,128)S(1)} %bitcast.17), channel_id=1, replica_groups=mesh['dom'=64,'sub'=4] {'dom'}, dimensions={0} | all-to-all | bytes 524288 | tf_op jit(solution)/shard_map/all_to_all | solution.py:403
  29.4 0.0 copy-done.3
  29.4 0.0 copy-start.1
  29.4 3.2 %shard_map.128 = (f32[64,1,256]{2,1,0:T(1,128)}, f32[24,512]{1,0:T(8,128)S(1)}, s32[8,512]{1,0:T(8,128)S(1)}) custom-call(f32[512,128]{1,0:T(8,128)S(1)} %bitcast.16, f32[3,16384]{1,0:T(4,128)S(1)} %copy-done, s32[8,2048]{1,0:T(8,128)S(1)} %copy-done.3), custom_call_target="tpu_custom_call" | custom-call | tf_op jit(solution)/shard_map/pallas_call | solution.py:275
  32.6 6.5 %all-to-all-start.1 = ((f32[64,1,256]{2,1,0:T(1,128)}), f32[64,1,256]{2,1,0:T(1,128)S(1)}, u32[]{:S(2)}, u32[]{:S(2)}) async-start(f32[64,1,256]{2,1,0:T(1,128)} %get-tuple-element.14), calls=%async_computation.1 | async-start | bytes 131072 | tf_op jit(solution)/shard_map/all_to_all | solution.py:412
  39.1 0.0 copy-done.1
  39.1 0.0 copy-start.13
  39.1 0.0 copy-start.11
  39.1 0.0 copy-start.14
  39.1 2.1 %collective-permute-start = (f32[3,2048]{1,0:T(4,128)S(1)}, f32[3,2048]{1,0:T(4,128)S(1)}, u32[]{:S(2)}, u32[]{:S(2)}) collective-permute-start(f32[3,2048]{1,0:T(4,128)S(1)} %get-tuple-element.22), channel_id=1, source_target_pairs={{0,4},{4,8},{8,12},{12,16},{16,20},{20,24},{24,28},{28,32},{32,36}... | collective-permute-start | bytes 73736 | tf_op jit(solution)/shard_map/ppermute | solution.py:398
  41.2 5.6 %collective-permute-start.1 = (f32[3,2048]{1,0:T(4,128)S(1)}, f32[3,2048]{1,0:T(4,128)S(1)}, u32[]{:S(2)}, u32[]{:S(2)}) collective-permute-start(f32[3,2048]{1,0:T(4,128)S(1)} %get-tuple-element.21), channel_id=1, source_target_pairs={{4,0},{8,4},{12,8},{16,12},{20,16},{24,20},{28,24},{32,28},{36,32}... | collective-permute-start | bytes 73736 | tf_op jit(solution)/shard_map/ppermute | solution.py:399
  46.8 0.0 copy-done.13
  46.8 0.0 copy-done.14
  46.9 0.0 copy-done.11
  46.9 0.0 copy-start.12
  46.9 0.1 copy.14
  47.0 0.7 copy-done.12
  47.6 0.1 copy.15
  47.7 0.0 copy-start.2
  47.8 0.0 collective-permute-done.before
  47.8 0.6 collective-permute-done.1.after
  48.4 0.2 copy-done.2
  48.6 8.5 %shard_map.129.forces = f32[64,768]{1,0:T(8,128)S(1)} custom-call(f32[3,16384]{1,0:T(4,128)S(1)} %copy-done.1, f32[3,2048]{1,0:T(4,128)S(1)} %collective-permute-done.before, f32[3,2048]{1,0:T(4,128)S(1)} %collective-permute-done.1.after, s32[20,768]{1,0:T(8,128)S(1)} %copy-done.2, f32[1,768]{1,0:T(1,128)S(1)} %broadcast_in_dim.10.shear, ...), custom_call_target="tpu_custom_call" | custom-call | tf_op jit(solution)/shard_map/pallas_call | solution.py:275
  57.1 8.6 %shard_map.130 = (f32[192,256]{1,0:T(8,128)S(1)}, f32[24,256]{1,0:T(8,128)S(1)}, f32[24,256]{1,0:T(8,128)S(1)}) custom-call(f32[64,768]{1,0:T(8,128)S(1)} %shard_map.129.forces, s32[20,768]{1,0:T(8,128)S(1)} %copy-done.2), custom_call_target="tpu_custom_call" | custom-call | tf_op jit(solution)/shard_map/pallas_call | solution.py:275
  65.7 5.5 %collective-permute-start.2 = (f32[24,256]{1,0:T(8,128)S(1)}, f32[24,256]{1,0:T(8,128)S(1)}, u32[]{:S(2)}, u32[]{:S(2)}) collective-permute-start(f32[24,256]{1,0:T(8,128)S(1)} %get-tuple-element.19), channel_id=1, source_target_pairs={{4,0},{8,4},{12,8},{16,12},{20,16},{24,20},{28,24},{32,28},{36,32}... | collective-permute-start | bytes 73736 | tf_op jit(solution)/shard_map/ppermute | solution.py:414
  71.3 1.9 %collective-permute-start.3 = (f32[24,256]{1,0:T(8,128)S(1)}, f32[24,256]{1,0:T(8,128)S(1)}, u32[]{:S(2)}, u32[]{:S(2)}) collective-permute-start(f32[24,256]{1,0:T(8,128)S(1)} %get-tuple-element.20), channel_id=1, source_target_pairs={{0,4},{4,8},{8,12},{12,16},{16,20},{20,24},{24,28},{28,32},{32,36}... | collective-permute-start | bytes 73736 | tf_op jit(solution)/shard_map/ppermute | solution.py:415
  73.2 0.0 copy-start.6
  73.2 0.0 copy-start.8
  73.3 1.6 %shard_map.131.master = f32[192,256]{1,0:T(8,128)S(1)} custom-call(f32[24,512]{1,0:T(8,128)S(1)} %get-tuple-element.17.force, s32[8,512]{1,0:T(8,128)S(1)} %get-tuple-element.18.nodes), custom_call_target="tpu_custom_call" | custom-call | tf_op jit(solution)/shard_map/pallas_call | solution.py:275
  74.9 0.0 collective-permute-done.2.upper
  74.9 3.6 %collective-permute-done.3.lower = f32[24,256]{1,0:T(8,128)S(1)} collective-permute-done((f32[24,256]{1,0:T(8,128)S(1)}, f32[24,256]{1,0:T(8,128)S(1)}, u32[]{:S(2)}, u32[]{:S(2)}) %collective-permute-start.3) | collective-permute-done | bytes 24608 | tf_op jit(solution)/shard_map/ppermute | solution.py:415
  78.5 0.0 all-to-all-done.1.returned
  78.5 0.0 copy-done.6
  78.5 0.0 copy-done.8
  78.5 1.2 %shard_map.132 = f32[4,48,256]{2,1,0:T(8,128)S(1)} custom-call(f32[64,1,256]{2,1,0:T(1,128)S(1)} %all-to-all-done.1.returned, s32[1,256]{1,0:T(1,128)S(1)} %get-tuple-element.15.slot, f32[8,256]{1,0:T(8,128)S(1)} %copy-done.8, s32[8,256]{1,0:T(8,128)S(1)} %copy-done.6, f32[192,256]{1,0:T(8,128)S(1)} %get-tuple-element.16.owned, ...), custom_call_target="tpu_custom_call" | custom-call | tf_op jit(solution)/shard_map/pallas_call | solution.py:275
  79.8 1.6 %collective-permute-start.4 = (f32[48,256]{1,0:T(8,128)S(1)}, f32[48,256]{1,0:T(8,128)S(1)}, u32[]{:S(2)}, u32[]{:S(2)}) collective-permute-start(f32[48,256]{1,0:T(8,128)S(1)} %get-tuple-element.25), channel_id=1, source_target_pairs={{0,1},{1,2},{2,3},{3,0},{4,5},{5,6},{6,7},{7,4},{8,9},{9,10},{10,1... | collective-permute-start | bytes 147464 | tf_op jit(solution)/shard_map/ppermute | solution.py:424
  81.3 2.7 %collective-permute-start.5 = (f32[48,256]{1,0:T(8,128)S(1)}, f32[48,256]{1,0:T(8,128)S(1)}, u32[]{:S(2)}, u32[]{:S(2)}) collective-permute-start(f32[48,256]{1,0:T(8,128)S(1)} %get-tuple-element.24), channel_id=1, source_target_pairs={{0,2},{1,3},{2,0},{3,1},{4,6},{5,7},{6,4},{7,5},{8,10},{9,11},{10,... | collective-permute-start | bytes 147464 | tf_op jit(solution)/shard_map/ppermute | solution.py:424
  84.1 1.4 %collective-permute-start.6 = (f32[48,256]{1,0:T(8,128)S(1)}, f32[48,256]{1,0:T(8,128)S(1)}, u32[]{:S(2)}, u32[]{:S(2)}) collective-permute-start(f32[48,256]{1,0:T(8,128)S(1)} %get-tuple-element.23), channel_id=1, source_target_pairs={{0,3},{1,0},{2,1},{3,2},{4,7},{5,4},{6,5},{7,6},{8,11},{9,8},{10,9... | collective-permute-start | bytes 147464 | tf_op jit(solution)/shard_map/ppermute | solution.py:424
  85.5 0.0 collective-permute-done.4.a
  85.5 1.4 %collective-permute-done.5.b = f32[48,256]{1,0:T(8,128)S(1)} collective-permute-done((f32[48,256]{1,0:T(8,128)S(1)}, f32[48,256]{1,0:T(8,128)S(1)}, u32[]{:S(2)}, u32[]{:S(2)}) %collective-permute-start.5) | collective-permute-done | bytes 49184 | tf_op jit(solution)/shard_map/ppermute | solution.py:424
  86.9 1.2 %collective-permute-done.6.d = f32[48,256]{1,0:T(8,128)S(1)} collective-permute-done((f32[48,256]{1,0:T(8,128)S(1)}, f32[48,256]{1,0:T(8,128)S(1)}, u32[]{:S(2)}, u32[]{:S(2)}) %collective-permute-start.6) | collective-permute-done | bytes 49184 | tf_op jit(solution)/shard_map/ppermute | solution.py:424
  88.2 0.7 shard_map.133
  (6 shorter events, 0.1 us)
Async XLA Ops:
  0.7 0.7 copy-start.10
  0.7 0.7 copy-start.9
  1.3 0.9 %copy-start = (f32[3,16384]{1,0:T(4,128)S(1)}, f32[3,16384]{1,0:T(4,128)}, u32[]{:S(2)}) copy-start(f32[3,16384]{1,0:T(4,128)} %disp.5) | copy-start | bytes 589828
  2.3 0.8 copy-start.4
  3.1 0.7 copy-start.5
  3.8 0.7 copy-start.7
  5.8 23.6 %copy-start.3 = (s32[8,2048]{1,0:T(8,128)S(1)}, s32[8,2048]{1,0:T(8,128)}, u32[]{:S(2)}) copy-start(s32[8,2048]{1,0:T(8,128)} %faces.1) | copy-start | bytes 196612
  29.4 9.7 %copy-start.1 = (f32[3,16384]{1,0:T(4,128)S(1)}, f32[3,16384]{1,0:T(4,128)}, u32[]{:S(2)}) copy-start(f32[3,16384]{1,0:T(4,128)} %disp.5) | copy-start | bytes 589828
  32.6 45.9 %all-to-all-start.1 = ((f32[64,1,256]{2,1,0:T(1,128)}), f32[64,1,256]{2,1,0:T(1,128)S(1)}, u32[]{:S(2)}, u32[]{:S(2)}) async-start(f32[64,1,256]{2,1,0:T(1,128)} %get-tuple-element.14), calls=%async_computation.1 | async-start | bytes 131072 | tf_op jit(solution)/shard_map/all_to_all | solution.py:412
  39.1 7.7 %copy-start.13 = (f32[768]{0:T(1024)S(1)}, f32[768]{0:T(1024)}, u32[]{:S(2)}) copy-start(f32[768]{0:T(1024)} %param.15) | copy-start | bytes 9220
  39.1 7.8 %copy-start.11 = (f32[60,60]{1,0:T(8,128)S(1)}, f32[60,60]{1,0:T(8,128)}, u32[]{:S(2)}) copy-start(f32[60,60]{1,0:T(8,128)} %param.17) | copy-start | bytes 43204
  39.1 7.7 %copy-start.14 = (f32[768]{0:T(1024)S(1)}, f32[768]{0:T(1024)}, u32[]{:S(2)}) copy-start(f32[768]{0:T(1024)} %param.16) | copy-start | bytes 9220
  39.1 8.6 %collective-permute-start = (f32[3,2048]{1,0:T(4,128)S(1)}, f32[3,2048]{1,0:T(4,128)S(1)}, u32[]{:S(2)}, u32[]{:S(2)}) collective-permute-start(f32[3,2048]{1,0:T(4,128)S(1)} %get-tuple-element.22), channel_id=1, source_target_pairs={{0,4},{4,8},{8,12},{12,16},{16,20},{20,24},{24,28},{28,32},{32,36}... | collective-permute-start | bytes 73736 | tf_op jit(solution)/shard_map/ppermute | solution.py:398
  41.2 7.2 %collective-permute-start.1 = (f32[3,2048]{1,0:T(4,128)S(1)}, f32[3,2048]{1,0:T(4,128)S(1)}, u32[]{:S(2)}, u32[]{:S(2)}) collective-permute-start(f32[3,2048]{1,0:T(4,128)S(1)} %get-tuple-element.21), channel_id=1, source_target_pairs={{4,0},{8,4},{12,8},{16,12},{20,16},{24,20},{28,24},{32,28},{36,32}... | collective-permute-start | bytes 73736 | tf_op jit(solution)/shard_map/ppermute | solution.py:399
  46.9 0.8 copy-start.12
  47.7 0.9 copy-start.2
  65.7 9.2 %collective-permute-start.2 = (f32[24,256]{1,0:T(8,128)S(1)}, f32[24,256]{1,0:T(8,128)S(1)}, u32[]{:S(2)}, u32[]{:S(2)}) collective-permute-start(f32[24,256]{1,0:T(8,128)S(1)} %get-tuple-element.19), channel_id=1, source_target_pairs={{4,0},{8,4},{12,8},{16,12},{20,16},{24,20},{28,24},{32,28},{36,32}... | collective-permute-start | bytes 73736 | tf_op jit(solution)/shard_map/ppermute | solution.py:414
  71.3 7.3 %collective-permute-start.3 = (f32[24,256]{1,0:T(8,128)S(1)}, f32[24,256]{1,0:T(8,128)S(1)}, u32[]{:S(2)}, u32[]{:S(2)}) collective-permute-start(f32[24,256]{1,0:T(8,128)S(1)} %get-tuple-element.20), channel_id=1, source_target_pairs={{0,4},{4,8},{8,12},{12,16},{16,20},{20,24},{24,28},{28,32},{32,36}... | collective-permute-start | bytes 73736 | tf_op jit(solution)/shard_map/ppermute | solution.py:415
  73.2 5.3 %copy-start.6 = (s32[8,256]{1,0:T(8,128)S(1)}, s32[8,256]{1,0:T(8,128)}, u32[]{:S(2)}) copy-start(s32[8,256]{1,0:T(8,128)} %slave.3) | copy-start | bytes 24580
  73.2 5.3 %copy-start.8 = (f32[8,256]{1,0:T(8,128)S(1)}, f32[8,256]{1,0:T(8,128)}, u32[]{:S(2)}) copy-start(f32[8,256]{1,0:T(8,128)} %dual.3) | copy-start | bytes 24580
  79.8 5.7 %collective-permute-start.4 = (f32[48,256]{1,0:T(8,128)S(1)}, f32[48,256]{1,0:T(8,128)S(1)}, u32[]{:S(2)}, u32[]{:S(2)}) collective-permute-start(f32[48,256]{1,0:T(8,128)S(1)} %get-tuple-element.25), channel_id=1, source_target_pairs={{0,1},{1,2},{2,3},{3,0},{4,5},{5,6},{6,7},{7,4},{8,9},{9,10},{10,1... | collective-permute-start | bytes 147464 | tf_op jit(solution)/shard_map/ppermute | solution.py:424
  81.3 5.6 %collective-permute-start.5 = (f32[48,256]{1,0:T(8,128)S(1)}, f32[48,256]{1,0:T(8,128)S(1)}, u32[]{:S(2)}, u32[]{:S(2)}) collective-permute-start(f32[48,256]{1,0:T(8,128)S(1)} %get-tuple-element.24), channel_id=1, source_target_pairs={{0,2},{1,3},{2,0},{3,1},{4,6},{5,7},{6,4},{7,5},{8,10},{9,11},{10,... | collective-permute-start | bytes 147464 | tf_op jit(solution)/shard_map/ppermute | solution.py:424
  84.1 4.1 %collective-permute-start.6 = (f32[48,256]{1,0:T(8,128)S(1)}, f32[48,256]{1,0:T(8,128)S(1)}, u32[]{:S(2)}, u32[]{:S(2)}) collective-permute-start(f32[48,256]{1,0:T(8,128)S(1)} %get-tuple-element.23), channel_id=1, source_target_pairs={{0,3},{1,0},{2,1},{3,2},{4,7},{5,4},{6,5},{7,6},{8,11},{9,8},{10,9... | collective-permute-start | bytes 147464 | tf_op jit(solution)/shard_map/ppermute | solution.py:424

commit v2 on v1

--- a/solution.py
+++ b/solution.py
@@ -20,8 +20,9 @@
 
 def one_hot_lo(index):
     n = index.shape[1]
-    rows = lax.broadcasted_iota(jnp.int32, (LO, n), 0)
-    return jnp.where(rows == (index & (LO - 1)), 1.0, 0.0).astype(BF16)
+    rows = lax.broadcasted_iota(jnp.int16, (LO, n), 0)
+    low = (index & (LO - 1)).astype(jnp.int16)
+    return jnp.where(rows == low, jnp.bfloat16(1), jnp.bfloat16(0))
 
 
 def hi_mask(index, rows):
@@ -65,16 +66,18 @@
     )
 
 
-def forces_kernel(disp, before, after, connect, shear, bulk, k_shear, k_bulk, out, rows, table, dofs):
-    nodes = disp.shape[1]
-    ghost = GHOST // LO
-    total = nodes // LO + 2 * ghost
-    to_rows(before, 0, ghost, rows, 0, total)
-    to_rows(disp, 0, nodes // LO, rows, ghost, total)
-    to_rows(after, 0, ghost, rows, total - ghost, total)
-    first, second = pieces(rows[...])
-    table[:, :LO] = first
-    table[:, LO:] = second
+def forces_kernel(own, before, after, connect, shear, bulk, k_shear, k_bulk, out, table, dofs, k_pad):
+    ghost = before.shape[0] // 3
+    count = own.shape[0] // 3
+    total = count + 2 * ghost
+    for source, first_row, rows in ((before, 0, ghost), (after, total - ghost, ghost)):
+        first, second = pieces(source[...])
+        for c in range(3):
+            here = slice(c * total + first_row, c * total + first_row + rows)
+            table[here, :LO] = first[c * rows : (c + 1) * rows]
+            table[here, LO:] = second[c * rows : (c + 1) * rows]
+    for c in range(3):
+        table[c * total + ghost : c * total + ghost + count, :] = own[c * count : (c + 1) * count, :]
     dofs[...] = jnp.zeros_like(dofs)
 
     def step(a, carry):
@@ -83,12 +86,14 @@
             dofs[pl.ds(20 * c + a, 1), :] = got[c]
         return carry
 
-    lax.fori_loop(0, 20, step, 0)
+    lax.fori_loop(0, 20, step, 0, unroll=True)
     g_first, g_second = pieces(dofs[...])
     g = jnp.concatenate([g_first, g_first, g_second, g_second], axis=0)
 
     def product(k):
-        k_first, k_second = pieces(k[...])
+        k_pad[...] = jnp.zeros_like(k_pad)
+        k_pad[: k.shape[0], : k.shape[1]] = k[...]
+        k_first, k_second = pieces(k_pad[...].T)
         wide = jnp.concatenate([k_first, k_second, k_first, k_second], axis=1)
         return jnp.dot(wide, g, preferred_element_type=F32)
 
@@ -105,7 +110,7 @@
         total[...] += scatter_column(values, connect[pl.ds(a, 1), :], all_rows)
         return carry
 
-    lax.fori_loop(0, 20, step, 0)
+    lax.fori_loop(0, 20, step, 0, unroll=True)
     own = all_rows - 2 * ghost
     for c in range(3):
         base = c * all_rows
@@ -114,12 +119,25 @@
         high[c * ghost : (c + 1) * ghost, :] = total[base + ghost + own : base + all_rows, :]
 
 
-def pack_kernel(disp, slave, dual, mortar, face, part, count, out, slot_out, rows, table):
+def pack_kernel(*refs):
+    given, (count, out, slot_out, table, head, tail, rows) = refs[:6], refs[6:13]
+    held, sems = refs[13:19], refs[19]
+    copies = [pltpu.make_async_copy(a, b, sems.at[i]) for i, (a, b) in enumerate(zip(given, held))]
+    for copy in copies:
+        copy.start()
+    for copy in copies:
+        copy.wait()
+    disp, slave, dual, mortar, face, part = held
     segs = slave.shape[1]
     own = disp.shape[1] // LO
     to_rows(disp, 0, own, rows, 0, own)
     first, second = pieces(rows[...])
     packed = jnp.concatenate([first, second], axis=1)
+    table[...] = packed
+    ghost = GHOST // LO
+    for c in range(3):
+        head[c * ghost : (c + 1) * ghost, :] = rows[c * own : c * own + ghost, :]
+        tail[c * ghost : (c + 1) * ghost, :] = rows[(c + 1) * own - ghost : (c + 1) * own, :]
     cap = 8
     width = out.shape[0]
     n_dom = width // cap
@@ -163,13 +181,11 @@
     )
 
 
-def master_kernel(incoming, disp, faces, mult_out, force_out, nodes_out, rows):
-    own = disp.shape[1] // LO
+def master_kernel(incoming, table, faces, mult_out, force_out, nodes_out):
+    own = table.shape[0] // 3
     width = incoming.shape[0]
     n_dom = width // 8
-    to_rows(disp, 0, own, rows, 0, own)
-    first, second = pieces(rows[...])
-    packed = jnp.concatenate([first, second], axis=1)
+    packed = table[...]
     got = incoming[...].T
     face = got[88:89, :].astype(jnp.int32)
     groups = faces.shape[1] // LO
@@ -266,11 +282,14 @@
             out[c : c + 1, h * LO : (h + 1) * LO] = total[c * per + h : c * per + h + 1, :]
 
 
-def call(kernel, outs, *args, scratch=(), smem=()):
+def call(kernel, outs, *args, scratch=(), smem=(), hbm=(), flops=10**8):
     specs = [
-        pl.BlockSpec(memory_space=pltpu.SMEM if i in smem else pltpu.VMEM)
+        pl.BlockSpec(
+            memory_space=pltpu.SMEM if i in smem else pltpu.HBM if i in hbm else pltpu.VMEM
+        )
         for i in range(len(args))
     ]
+    moved = sum(a.size * 4 for a in args)
     many = isinstance(outs, list)
     return pl.pallas_call(
         kernel,
@@ -280,24 +299,22 @@
         if many
         else pl.BlockSpec(memory_space=pltpu.VMEM),
         scratch_shapes=list(scratch),
+        cost_estimate=pl.CostEstimate(flops=flops, transcendentals=0, bytes_accessed=moved),
         compiler_params=pltpu.CompilerParams(vmem_limit_bytes=48 * 1024 * 1024),
-    )(*args)
+    )(*[pltpu.with_memory_space_constraint(a, pltpu.HBM) if i in hbm else a for i, a in enumerate(args)])
 
 
 def shape(*dims):
     return jax.ShapeDtypeStruct(dims, F32)
 
 
-def element_forces(displacement, before, after, connect, shear, bulk, k_shear, k_bulk):
-    nodes = displacement.shape[1]
-    rows = nodes // LO + 2 * GHOST // LO
+def element_forces(table, before, after, connect, shear, bulk, k_shear, k_bulk):
+    rows = table.shape[0] + before.shape[0] + after.shape[0]
     elems = connect.shape[1]
-    k_shear = jnp.pad(k_shear.T, ((0, 4), (0, 4)))
-    k_bulk = jnp.pad(k_bulk.T, ((0, 4), (0, 4)))
     return call(
         forces_kernel,
         shape(64, elems),
-        displacement,
+        table,
         before,
         after,
         connect,
@@ -306,10 +323,11 @@
         k_shear,
         k_bulk,
         scratch=[
-            pltpu.VMEM((3 * rows, LO), F32),
-            pltpu.VMEM((3 * rows, 2 * LO), BF16),
+            pltpu.VMEM((rows, 2 * LO), BF16),
             pltpu.VMEM((64, elems), F32),
+            pltpu.VMEM((64, 64), F32),
         ],
+        flops=8 * 10**9,
     )
 
 
@@ -322,6 +340,7 @@
         forces,
         connect,
         scratch=[pltpu.VMEM((3 * (own + 2 * ghost), LO), F32)],
+        flops=8 * 10**9,
     )
 
 
@@ -330,7 +349,13 @@
     segs = seg_face.shape[0]
     return call(
         pack_kernel,
-        [shape(n_dom * 8, 128), jax.ShapeDtypeStruct((1, segs), jnp.int32)],
+        [
+            shape(n_dom * 8, 128),
+            jax.ShapeDtypeStruct((1, segs), jnp.int32),
+            jax.ShapeDtypeStruct((3 * own, 2 * LO), BF16),
+            shape(3 * GHOST // LO, LO),
+            shape(3 * GHOST // LO, LO),
+        ],
         displacement,
         seg_slave,
         dual,
@@ -339,12 +364,21 @@
         seg_part.reshape(1, segs),
         seg_count.reshape(1, 1),
         smem=(6,),
-        scratch=[pltpu.VMEM((3 * own, LO), F32), pltpu.VMEM((3 * own, 2 * LO), BF16)],
-    )
-
-
-def master(incoming, displacement, face_nodes):
-    own = displacement.shape[1] // LO
+        hbm=(0, 1, 2, 3, 4, 5),
+        scratch=[
+            pltpu.VMEM((3 * own, LO), F32),
+            pltpu.VMEM(displacement.shape, F32),
+            pltpu.VMEM(seg_slave.shape, jnp.int32),
+            pltpu.VMEM(dual.shape, F32),
+            pltpu.VMEM(mortar.shape, F32),
+            pltpu.VMEM((1, segs), jnp.int32),
+            pltpu.VMEM((1, segs), jnp.int32),
+            pltpu.SemaphoreType.DMA((6,)),
+        ],
+    )
+
+
+def master(incoming, table, face_nodes):
     width = incoming.shape[0]
     return call(
         master_kernel,
@@ -354,9 +388,8 @@
             jax.ShapeDtypeStruct((8, width), jnp.int32),
         ],
         incoming,
-        displacement,
+        table,
         face_nodes,
-        scratch=[pltpu.VMEM((3 * own, LO), F32)],
     )
 
 
@@ -395,21 +428,21 @@
     n_dom, n_sub = lax.axis_size("dom"), lax.axis_size("sub")
     up = [(i, i + 1) for i in range(n_dom - 1)]
     down = [(i + 1, i) for i in range(n_dom - 1)]
-    before = lax.ppermute(displacement[:, nodes - GHOST :], "dom", up)
-    after = lax.ppermute(displacement[:, :GHOST], "dom", down)
-    outgoing, slot = pack(
+    outgoing, slot, table, head, tail = pack(
         displacement, seg_slave, dual, mortar, seg_face, seg_part, seg_count, n_dom
     )
     incoming = lax.all_to_all(
         outgoing.reshape(n_dom, 8, 128), "dom", split_axis=0, concat_axis=0, tiled=True
     )
-    forces = element_forces(
-        displacement, before, after, connect, shear, bulk, stiff_shear, stiff_bulk
-    )
+    before = lax.ppermute(tail, "dom", up)
+    after = lax.ppermute(head, "dom", down)
+    forces = element_forces(table, before, after, connect, shear, bulk, stiff_shear, stiff_bulk)
+    incoming, forces = lax.optimization_barrier((incoming, forces))
     mult, master_force, master_nodes = master(
-        incoming.reshape(n_dom * 8, 128), displacement, face_nodes
+        incoming.reshape(n_dom * 8, 128), table, face_nodes
     )
     returned = lax.all_to_all(mult, "dom", split_axis=0, concat_axis=0, tiled=True)
+    forces, _ = lax.optimization_barrier((forces, mult))
     owned, low, high = element_scatter(forces, connect, nodes)
     upper = lax.ppermute(low, "dom", down)
     lower = lax.ppermute(high, "dom", up)

time: 89.5 us -> 70 us (0.78)
  blocking collectives: 23.6 us -> 0 us
  starting transfers between devices: 27.4 us -> 37.5 us
  Pallas kernels: 25 us -> 17.7 us
  waiting for transfers between devices: 6.91 us -> 12.5 us
  local copies, waits for them, and re-layouts: 5.02 us -> 0.74 us
    all_to_all x1 -> x0, blocking collectives: 23.6 us -> none  [on_device(): lax.all_to_all(outgoing.reshape(n_dom, 8, 128), 'dom', split_axis=0, conc...]
    all_to_all x0 -> x1, starting transfers between devices: none -> 10 us  [on_device(): lax.all_to_all(outgoing.reshape(n_dom, 8, 128), 'dom', split_axis=0, conc...]
    pallas_call x7, Pallas kernels: 25 us -> 17.7 us  [call(): pl.pallas_call(kernel, out_shape=outs, in_specs=specs, out_specs=[pl.Bloc...]
    all_to_all x0 -> x1, waiting for transfers between devices: none -> 6.11 us  [on_device(): lax.all_to_all(outgoing.reshape(n_dom, 8, 128), 'dom', split_axis=0, conc...]
    unnamed x32 -> x16, local copies, waits for them, and re-layouts: 4.97 us -> 0.71 us
    ppermute x2, starting transfers between devices: 7.67 us -> 9.01 us  [the longest x1 7.09 us: on_device(): after = lax.ppermute(head, 'dom', down)]
    ppermute x1, starting transfers between devices: 5.54 us -> 4.33 us  [on_device(): upper = lax.ppermute(low, 'dom', down)]
  transfers between devices with their start and end apart: 8 -> 9, of which waited for: 4 -> 4; matrix products, arithmetic and copies ran while one was open for 0% -> 0% of each run, Pallas kernels for 21% -> 15%
where the time goes in v2:
time: 70 us; the launch traced here: 69.4 us
  starting transfers between devices  37.5 us (54%)
  Pallas kernels  17.7 us (25%)
  waiting for transfers between devices  12.5 us (18%)
  between operations  0.91 us (1%)
  local copies, waits for them, and re-layouts  0.74 us (1%)
    pallas_call x7, Pallas kernels, call(): pl.pallas_call(kernel, out_shape=outs, in_specs=specs, out_specs=[pl.Bloc...  17.7 us
    all_to_all x1, starting transfers between devices, on_device(): lax.all_to_all(outgoing.reshape(n_dom, 8, 128), 'dom', split_axis=0, conc...  10 us
    ppermute x1, starting transfers between devices, on_device(): after = lax.ppermute(head, 'dom', down)  7.09 us
    all_to_all x1, starting transfers between devices, on_device(): lax.all_to_all(mult, 'dom', split_axis=0, concat_axis=0, tiled=True)  6.49 us
    all_to_all x1, waiting for transfers between devices, on_device(): lax.all_to_all(outgoing.reshape(n_dom, 8, 128), 'dom', split_axis=0, conc...  6.11 us
    ppermute x3, starting transfers between devices, on_device(): lax.ppermute(lax.dynamic_index_in_dim(blocks, (me + k) % n_sub, 0, keepdi...  5.74 us
    ppermute x1, starting transfers between devices, on_device(): upper = lax.ppermute(low, 'dom', down)  4.33 us
    ppermute x1, waiting for transfers between devices, on_device(): lower = lax.ppermute(high, 'dom', up)  3.74 us
  transfers between devices with their start and end apart: 9, of which 4 were waited for; matrix products, arithmetic and copies ran while one was open for 0% of the time, Pallas kernels for 15%

profile of v2, /device:TPU:8, one launch (start us, length us, event | category | flops | bytes accessed | tf_op | source)
XLA Modules:
  0.0 69.4 jit_solution(1997138763150093402)
XLA Ops:
  0.7 2.8 %shard_map.127 = (f32[512,128]{1,0:T(8,128)}, s32[1,256]{1,0:T(1,128)S(1)}, bf16[192,512]{1,0:T(8,128)(2,1)S(1)}, f32[24,256]{1,0:T(8,128)S(1)}, f32[24,256]{1,0:T(8,128)S(1)}) custom-call(f32[3,16384]{1,0:T(4,128)} %refs_0_.1, s32[8,256]{1,0:T(8,128)} %slave.1, f32[8,256]{1,0:T(8,128)} %dual.1, f32[64,256]{1,0:T(8,128)} %refs_3_.1, s32[1,256]{1,0:T(1,128)} %bitcast.15, ...), custom_call_target="tpu_custom_call" | custom-call | flops 100000000 | bytes 280580 | tf_op jit(solution)/shard_map/pallas_call | solution.py:294
  3.4 1.9 %collective-permute-start = (f32[24,256]{1,0:T(8,128)S(1)}, f32[24,256]{1,0:T(8,128)S(1)}, u32[]{:S(2)}, u32[]{:S(2)}) collective-permute-start(f32[24,256]{1,0:T(8,128)S(1)} %get-tuple-element.21), channel_id=1, source_target_pairs={{0,4},{4,8},{8,12},{12,16},{16,20},{20,24},{24,28},{28,32},{32,36}... | collective-permute-start | bytes 73736 | tf_op jit(solution)/shard_map/ppermute | solution.py:437
  5.4 7.1 %collective-permute-start.1 = (f32[24,256]{1,0:T(8,128)S(1)}, f32[24,256]{1,0:T(8,128)S(1)}, u32[]{:S(2)}, u32[]{:S(2)}) collective-permute-start(f32[24,256]{1,0:T(8,128)S(1)} %get-tuple-element.22), channel_id=1, source_target_pairs={{4,0},{8,4},{12,8},{16,12},{20,16},{24,20},{28,24},{32,28},{36,32}... | collective-permute-start | bytes 73736 | tf_op jit(solution)/shard_map/ppermute | solution.py:438
  12.5 0.0 copy-start.6
  12.5 0.0 copy-start.3
  12.5 0.0 copy-start.4
  12.5 0.0 copy-start.5
  12.5 10.0 %all-to-all-start = ((f32[64,8,128]{2,1,0:T(8,128)}), f32[64,8,128]{2,1,0:T(8,128)S(1)}, u32[]{:S(2)}, u32[]{:S(2)}) async-start(f32[64,8,128]{2,1,0:T(8,128)} %bitcast.3), calls=%async_computation | async-start | bytes 524288 | tf_op jit(solution)/shard_map/all_to_all | solution.py:434
  22.5 0.0 copy-done.6
  22.5 0.0 copy-start.7
  22.6 0.7 copy-done.7
  23.2 0.0 collective-permute-done.before
  23.2 0.0 collective-permute-done.1.after
  23.2 0.0 copy-done.3
  23.2 0.0 copy-done.4
  23.3 0.0 copy-done.5
  23.3 0.0 copy-start
  23.3 4.7 %shard_map.128.forces = f32[64,768]{1,0:T(8,128)S(1)} custom-call(bf16[192,512]{1,0:T(8,128)(2,1)S(1)} %get-tuple-element.20.own.table, f32[24,256]{1,0:T(8,128)S(1)} %collective-permute-done.before, f32[24,256]{1,0:T(8,128)S(1)} %collective-permute-done.1.after, s32[20,768]{1,0:T(8,128)S(1)} %copy-done.3, f32[1,768]{1,0:T(1,128)S(1)} %broadcast_in_dim.10.shear, ...), custom_call_target="tpu_custom_call" | custom-call | flops 8000000000 | bytes 538752 | tf_op jit(solution)/shard_map/pallas_call | solution.py:294
  28.0 6.1 %all-to-all-done = f32[64,8,128]{2,1,0:T(8,128)S(1)} async-done(((f32[64,8,128]{2,1,0:T(8,128)}), f32[64,8,128]{2,1,0:T(8,128)S(1)}, u32[]{:S(2)}, u32[]{:S(2)}) %all-to-all-start) | async-done | bytes 262176 | tf_op jit(solution)/shard_map/all_to_all | solution.py:434
  34.1 0.0 copy-done
  34.1 2.6 %shard_map.129 = (f32[64,1,256]{2,1,0:T(1,128)}, f32[24,512]{1,0:T(8,128)S(1)}, s32[8,512]{1,0:T(8,128)S(1)}) custom-call(f32[512,128]{1,0:T(8,128)S(1)} %bitcast.14, bf16[192,512]{1,0:T(8,128)(2,1)S(1)} %get-tuple-element.20.own.table, s32[8,2048]{1,0:T(8,128)S(1)} %copy-done), custom_call_target="tpu_custom_call" | custom-call | flops 100000000 | bytes 720896 | tf_op jit(solution)/shard_map/pallas_call | solution.py:294
  36.7 6.5 %all-to-all-start.1 = ((f32[64,1,256]{2,1,0:T(1,128)}), f32[64,1,256]{2,1,0:T(1,128)S(1)}, u32[]{:S(2)}, u32[]{:S(2)}) async-start(f32[64,1,256]{2,1,0:T(1,128)} %get-tuple-element.24), calls=%async_computation.1 | async-start | bytes 131072 | tf_op jit(solution)/shard_map/all_to_all | solution.py:444
  43.2 4.3 %shard_map.130 = (f32[192,256]{1,0:T(8,128)S(1)}, f32[24,256]{1,0:T(8,128)S(1)}, f32[24,256]{1,0:T(8,128)S(1)}) custom-call(f32[64,768]{1,0:T(8,128)S(1)} %shard_map.128.forces, s32[20,768]{1,0:T(8,128)S(1)} %copy-done.3), custom_call_target="tpu_custom_call" | custom-call | flops 8000000000 | bytes 258048 | tf_op jit(solution)/shard_map/pallas_call | solution.py:294
  47.5 4.3 %collective-permute-start.2 = (f32[24,256]{1,0:T(8,128)S(1)}, f32[24,256]{1,0:T(8,128)S(1)}, u32[]{:S(2)}, u32[]{:S(2)}) collective-permute-start(f32[24,256]{1,0:T(8,128)S(1)} %get-tuple-element.31), channel_id=1, source_target_pairs={{4,0},{8,4},{12,8},{16,12},{20,16},{24,20},{28,24},{32,28},{36,32}... | collective-permute-start | bytes 73736 | tf_op jit(solution)/shard_map/ppermute | solution.py:447
  51.8 1.9 %collective-permute-start.3 = (f32[24,256]{1,0:T(8,128)S(1)}, f32[24,256]{1,0:T(8,128)S(1)}, u32[]{:S(2)}, u32[]{:S(2)}) collective-permute-start(f32[24,256]{1,0:T(8,128)S(1)} %get-tuple-element.32), channel_id=1, source_target_pairs={{0,4},{4,8},{8,12},{12,16},{16,20},{20,24},{24,28},{28,32},{32,36}... | collective-permute-start | bytes 73736 | tf_op jit(solution)/shard_map/ppermute | solution.py:448
  53.8 0.0 copy-start.1
  53.8 0.0 copy-start.2
  53.8 1.5 %shard_map.131.master = f32[192,256]{1,0:T(8,128)S(1)} custom-call(f32[24,512]{1,0:T(8,128)S(1)} %get-tuple-element.29.force, s32[8,512]{1,0:T(8,128)S(1)} %get-tuple-element.30.nodes), custom_call_target="tpu_custom_call" | custom-call | flops 100000000 | bytes 65536 | tf_op jit(solution)/shard_map/pallas_call | solution.py:294
  55.3 0.0 collective-permute-done.2.upper
  55.3 3.7 %collective-permute-done.3.lower = f32[24,256]{1,0:T(8,128)S(1)} collective-permute-done((f32[24,256]{1,0:T(8,128)S(1)}, f32[24,256]{1,0:T(8,128)S(1)}, u32[]{:S(2)}, u32[]{:S(2)}) %collective-permute-start.3) | collective-permute-done | bytes 24608 | tf_op jit(solution)/shard_map/ppermute | solution.py:448
  59.1 0.0 all-to-all-done.1.returned
  59.1 0.0 copy-done.1
  59.1 0.0 copy-done.2
  59.1 1.2 %shard_map.132 = f32[4,48,256]{2,1,0:T(8,128)S(1)} custom-call(f32[64,1,256]{2,1,0:T(1,128)S(1)} %all-to-all-done.1.returned, s32[1,256]{1,0:T(1,128)S(1)} %get-tuple-element.25.slot, f32[8,256]{1,0:T(8,128)S(1)} %copy-done.2, s32[8,256]{1,0:T(8,128)S(1)} %copy-done.1, f32[192,256]{1,0:T(8,128)S(1)} %get-tuple-element.28.owned, ...), custom_call_target="tpu_custom_call" | custom-call | flops 100000000 | bytes 525312 | tf_op jit(solution)/shard_map/pallas_call | solution.py:294
  60.3 1.6 %collective-permute-start.4 = (f32[48,256]{1,0:T(8,128)S(1)}, f32[48,256]{1,0:T(8,128)S(1)}, u32[]{:S(2)}, u32[]{:S(2)}) collective-permute-start(f32[48,256]{1,0:T(8,128)S(1)} %get-tuple-element.35), channel_id=1, source_target_pairs={{0,1},{1,2},{2,3},{3,0},{4,5},{5,6},{6,7},{7,4},{8,9},{9,10},{10,1... | collective-permute-start | bytes 147464 | tf_op jit(solution)/shard_map/ppermute | solution.py:457
  61.9 2.7 %collective-permute-start.5 = (f32[48,256]{1,0:T(8,128)S(1)}, f32[48,256]{1,0:T(8,128)S(1)}, u32[]{:S(2)}, u32[]{:S(2)}) collective-permute-start(f32[48,256]{1,0:T(8,128)S(1)} %get-tuple-element.34), channel_id=1, source_target_pairs={{0,2},{1,3},{2,0},{3,1},{4,6},{5,7},{6,4},{7,5},{8,10},{9,11},{10,... | collective-permute-start | bytes 147464 | tf_op jit(solution)/shard_map/ppermute | solution.py:457
  64.6 1.4 %collective-permute-start.6 = (f32[48,256]{1,0:T(8,128)S(1)}, f32[48,256]{1,0:T(8,128)S(1)}, u32[]{:S(2)}, u32[]{:S(2)}) collective-permute-start(f32[48,256]{1,0:T(8,128)S(1)} %get-tuple-element.33), channel_id=1, source_target_pairs={{0,3},{1,0},{2,1},{3,2},{4,7},{5,4},{6,5},{7,6},{8,11},{9,8},{10,9... | collective-permute-start | bytes 147464 | tf_op jit(solution)/shard_map/ppermute | solution.py:457
  66.1 0.0 collective-permute-done.4.a
  66.1 1.4 %collective-permute-done.5.b = f32[48,256]{1,0:T(8,128)S(1)} collective-permute-done((f32[48,256]{1,0:T(8,128)S(1)}, f32[48,256]{1,0:T(8,128)S(1)}, u32[]{:S(2)}, u32[]{:S(2)}) %collective-permute-start.5) | collective-permute-done | bytes 49184 | tf_op jit(solution)/shard_map/ppermute | solution.py:457
  67.5 1.2 %collective-permute-done.6.d = f32[48,256]{1,0:T(8,128)S(1)} collective-permute-done((f32[48,256]{1,0:T(8,128)S(1)}, f32[48,256]{1,0:T(8,128)S(1)}, u32[]{:S(2)}, u32[]{:S(2)}) %collective-permute-start.6) | collective-permute-done | bytes 49184 | tf_op jit(solution)/shard_map/ppermute | solution.py:457
  68.7 0.7 shard_map.133
  (3 shorter events, 0.0 us)
Async XLA Ops:
  3.4 19.8 %collective-permute-start = (f32[24,256]{1,0:T(8,128)S(1)}, f32[24,256]{1,0:T(8,128)S(1)}, u32[]{:S(2)}, u32[]{:S(2)}) collective-permute-start(f32[24,256]{1,0:T(8,128)S(1)} %get-tuple-element.21), channel_id=1, source_target_pairs={{0,4},{4,8},{8,12},{12,16},{16,20},{20,24},{24,28},{28,32},{32,36}... | collective-permute-start | bytes 73736 | tf_op jit(solution)/shard_map/ppermute | solution.py:437
  5.4 17.9 %collective-permute-start.1 = (f32[24,256]{1,0:T(8,128)S(1)}, f32[24,256]{1,0:T(8,128)S(1)}, u32[]{:S(2)}, u32[]{:S(2)}) collective-permute-start(f32[24,256]{1,0:T(8,128)S(1)} %get-tuple-element.22), channel_id=1, source_target_pairs={{4,0},{8,4},{12,8},{16,12},{20,16},{24,20},{28,24},{32,28},{36,32}... | collective-permute-start | bytes 73736 | tf_op jit(solution)/shard_map/ppermute | solution.py:438
  12.5 10.1 %copy-start.6 = (f32[768]{0:T(1024)S(1)}, f32[768]{0:T(1024)}, u32[]{:S(2)}) copy-start(f32[768]{0:T(1024)} %param.15) | copy-start | bytes 9220
  12.5 10.8 %copy-start.3 = (s32[20,768]{1,0:T(8,128)S(1)}, s32[20,768]{1,0:T(8,128)}, u32[]{:S(2)}) copy-start(s32[20,768]{1,0:T(8,128)} %connect.3) | copy-start | bytes 184324
  12.5 10.8 %copy-start.4 = (f32[60,60]{1,0:T(8,128)S(1)}, f32[60,60]{1,0:T(8,128)}, u32[]{:S(2)}) copy-start(f32[60,60]{1,0:T(8,128)} %k_shear.1) | copy-start | bytes 43204
  12.5 10.8 %copy-start.5 = (f32[60,60]{1,0:T(8,128)S(1)}, f32[60,60]{1,0:T(8,128)}, u32[]{:S(2)}) copy-start(f32[60,60]{1,0:T(8,128)} %k_bulk.1) | copy-start | bytes 43204
  12.5 21.6 %all-to-all-start = ((f32[64,8,128]{2,1,0:T(8,128)}), f32[64,8,128]{2,1,0:T(8,128)S(1)}, u32[]{:S(2)}, u32[]{:S(2)}) async-start(f32[64,8,128]{2,1,0:T(8,128)} %bitcast.3), calls=%async_computation | async-start | bytes 524288 | tf_op jit(solution)/shard_map/all_to_all | solution.py:434
  22.5 0.7 copy-start.7
  23.3 10.8 %copy-start = (s32[8,2048]{1,0:T(8,128)S(1)}, s32[8,2048]{1,0:T(8,128)}, u32[]{:S(2)}) copy-start(s32[8,2048]{1,0:T(8,128)} %faces.1) | copy-start | bytes 196612
  36.7 22.4 %all-to-all-start.1 = ((f32[64,1,256]{2,1,0:T(1,128)}), f32[64,1,256]{2,1,0:T(1,128)S(1)}, u32[]{:S(2)}, u32[]{:S(2)}) async-start(f32[64,1,256]{2,1,0:T(1,128)} %get-tuple-element.24), calls=%async_computation.1 | async-start | bytes 131072 | tf_op jit(solution)/shard_map/all_to_all | solution.py:444
  47.5 7.8 %collective-permute-start.2 = (f32[24,256]{1,0:T(8,128)S(1)}, f32[24,256]{1,0:T(8,128)S(1)}, u32[]{:S(2)}, u32[]{:S(2)}) collective-permute-start(f32[24,256]{1,0:T(8,128)S(1)} %get-tuple-element.31), channel_id=1, source_target_pairs={{4,0},{8,4},{12,8},{16,12},{20,16},{24,20},{28,24},{32,28},{36,32}... | collective-permute-start | bytes 73736 | tf_op jit(solution)/shard_map/ppermute | solution.py:447
  51.8 7.3 %collective-permute-start.3 = (f32[24,256]{1,0:T(8,128)S(1)}, f32[24,256]{1,0:T(8,128)S(1)}, u32[]{:S(2)}, u32[]{:S(2)}) collective-permute-start(f32[24,256]{1,0:T(8,128)S(1)} %get-tuple-element.32), channel_id=1, source_target_pairs={{0,4},{4,8},{8,12},{12,16},{16,20},{20,24},{24,28},{28,32},{32,36}... | collective-permute-start | bytes 73736 | tf_op jit(solution)/shard_map/ppermute | solution.py:448
  53.8 5.3 %copy-start.1 = (s32[8,256]{1,0:T(8,128)S(1)}, s32[8,256]{1,0:T(8,128)}, u32[]{:S(2)}) copy-start(s32[8,256]{1,0:T(8,128)} %slave.1) | copy-start | bytes 24580
  53.8 5.3 %copy-start.2 = (f32[8,256]{1,0:T(8,128)S(1)}, f32[8,256]{1,0:T(8,128)}, u32[]{:S(2)}) copy-start(f32[8,256]{1,0:T(8,128)} %dual.1) | copy-start | bytes 24580
  60.3 5.7 %collective-permute-start.4 = (f32[48,256]{1,0:T(8,128)S(1)}, f32[48,256]{1,0:T(8,128)S(1)}, u32[]{:S(2)}, u32[]{:S(2)}) collective-permute-start(f32[48,256]{1,0:T(8,128)S(1)} %get-tuple-element.35), channel_id=1, source_target_pairs={{0,1},{1,2},{2,3},{3,0},{4,5},{5,6},{6,7},{7,4},{8,9},{9,10},{10,1... | collective-permute-start | bytes 147464 | tf_op jit(solution)/shard_map/ppermute | solution.py:457
  61.9 5.6 %collective-permute-start.5 = (f32[48,256]{1,0:T(8,128)S(1)}, f32[48,256]{1,0:T(8,128)S(1)}, u32[]{:S(2)}, u32[]{:S(2)}) collective-permute-start(f32[48,256]{1,0:T(8,128)S(1)} %get-tuple-element.34), channel_id=1, source_target_pairs={{0,2},{1,3},{2,0},{3,1},{4,6},{5,7},{6,4},{7,5},{8,10},{9,11},{10,... | collective-permute-start | bytes 147464 | tf_op jit(solution)/shard_map/ppermute | solution.py:457
  64.6 4.1 %collective-permute-start.6 = (f32[48,256]{1,0:T(8,128)S(1)}, f32[48,256]{1,0:T(8,128)S(1)}, u32[]{:S(2)}, u32[]{:S(2)}) collective-permute-start(f32[48,256]{1,0:T(8,128)S(1)} %get-tuple-element.33), channel_id=1, source_target_pairs={{0,3},{1,0},{2,1},{3,2},{4,7},{5,4},{6,5},{7,6},{8,11},{9,8},{10,9... | collective-permute-start | bytes 147464 | tf_op jit(solution)/shard_map/ppermute | solution.py:457

commit v3 on v2

--- a/solution.py
+++ b/solution.py
@@ -8,6 +8,7 @@
 GHOST = 2048
 LO = 256
 penalty = 2.0
+ELEMENT_FLOPS = 8 * 10**9
 F32 = jnp.float32
 BF16 = jnp.bfloat16
 
@@ -37,19 +38,16 @@
             target[row : row + 1, :] = source[c : c + 1, offset + h * LO : offset + (h + 1) * LO]
 
 
-def gather_column(table, index, rows):
-    hot = one_hot_lo(index)
+def gather_column(table, hot, mask):
+    rows = mask.shape[0]
     picked = jnp.dot(table, jnp.concatenate([hot, hot], axis=0), preferred_element_type=F32)
-    mask = hi_mask(index, rows)
     return [
         jnp.sum(jnp.where(mask, picked[c * rows : (c + 1) * rows], 0.0), axis=0, keepdims=True)
         for c in range(3)
     ]
 
 
-def scatter_column(values, index, rows):
-    hot = one_hot_lo(index)
-    mask = hi_mask(index, rows)
+def scatter_column(values, hot, mask):
     firsts, seconds = [], []
     for c in range(3):
         first, second = pieces(values[c])
@@ -66,27 +64,45 @@
     )
 
 
-def forces_kernel(own, before, after, connect, shear, bulk, k_shear, k_bulk, out, table, dofs, k_pad):
-    ghost = before.shape[0] // 3
+def gather(table, index, rows):
+    return gather_column(table, one_hot_lo(index), hi_mask(index, rows))
+
+
+def scatter(values, index, rows):
+    return scatter_column(values, one_hot_lo(index), hi_mask(index, rows))
+
+
+def by_side(near, far):
+    here_dom, n_dom = lax.axis_index("dom"), lax.axis_size("dom")
+    even = here_dom % 2 == 0
+    below = jnp.where(here_dom == 0, 0.0, jnp.where(even, far, near))
+    above = jnp.where(here_dom == n_dom - 1, 0.0, jnp.where(even, near, far))
+    return below, above
+
+
+def element_kernel(
+    own, near, far, connect, shear, bulk, k_shear, k_bulk,
+    owned, near_out, far_out, table, dofs, k_pad, hots, total,
+):
+    ghost = near.shape[0] // 3
     count = own.shape[0] // 3
-    total = count + 2 * ghost
-    for source, first_row, rows in ((before, 0, ghost), (after, total - ghost, ghost)):
-        first, second = pieces(source[...])
+    rows = count + 2 * ghost
+    for source, first_row in zip(by_side(near[...], far[...]), (0, rows - ghost)):
+        first, second = pieces(source)
         for c in range(3):
-            here = slice(c * total + first_row, c * total + first_row + rows)
-            table[here, :LO] = first[c * rows : (c + 1) * rows]
-            table[here, LO:] = second[c * rows : (c + 1) * rows]
-    for c in range(3):
-        table[c * total + ghost : c * total + ghost + count, :] = own[c * count : (c + 1) * count, :]
+            here = slice(c * rows + first_row, c * rows + first_row + ghost)
+            table[here, :LO] = first[c * ghost : (c + 1) * ghost]
+            table[here, LO:] = second[c * ghost : (c + 1) * ghost]
+    for c in range(3):
+        table[c * rows + ghost : c * rows + ghost + count, :] = own[c * count : (c + 1) * count, :]
     dofs[...] = jnp.zeros_like(dofs)
-
-    def step(a, carry):
-        got = gather_column(table[...], connect[pl.ds(a, 1), :], total)
+    for a in range(20):
+        index = connect[a : a + 1, :]
+        hot = one_hot_lo(index)
+        hots[a] = hot
+        got = gather_column(table[...], hot, hi_mask(index, rows))
         for c in range(3):
-            dofs[pl.ds(20 * c + a, 1), :] = got[c]
-        return carry
-
-    lax.fori_loop(0, 20, step, 0, unroll=True)
+            dofs[20 * c + a : 20 * c + a + 1, :] = got[c]
     g_first, g_second = pieces(dofs[...])
     g = jnp.concatenate([g_first, g_first, g_second, g_second], axis=0)
 
@@ -97,30 +113,24 @@
         wide = jnp.concatenate([k_first, k_second, k_first, k_second], axis=1)
         return jnp.dot(wide, g, preferred_element_type=F32)
 
-    out[...] = shear[...] * product(k_shear) + bulk[...] * product(k_bulk)
-
-
-def element_scatter_kernel(forces, connect, owned, low, high, total):
-    ghost = GHOST // LO
-    all_rows = total.shape[0] // 3
+    dofs[...] = shear[...] * product(k_shear) + bulk[...] * product(k_bulk)
     total[...] = jnp.zeros_like(total)
-
-    def step(a, carry):
-        values = [forces[pl.ds(20 * c + a, 1), :] for c in range(3)]
-        total[...] += scatter_column(values, connect[pl.ds(a, 1), :], all_rows)
-        return carry
-
-    lax.fori_loop(0, 20, step, 0, unroll=True)
-    own = all_rows - 2 * ghost
-    for c in range(3):
-        base = c * all_rows
-        low[c * ghost : (c + 1) * ghost, :] = total[base : base + ghost, :]
-        owned[c * own : (c + 1) * own, :] = total[base + ghost : base + ghost + own, :]
-        high[c * ghost : (c + 1) * ghost, :] = total[base + ghost + own : base + all_rows, :]
+    for a in range(20):
+        values = [dofs[20 * c + a : 20 * c + a + 1, :] for c in range(3)]
+        total[...] += scatter_column(values, hots[a], hi_mask(connect[a : a + 1, :], rows))
+    even = lax.axis_index("dom") % 2 == 0
+    for c in range(3):
+        base = c * rows
+        here = slice(c * ghost, (c + 1) * ghost)
+        low = total[base : base + ghost, :]
+        high = total[base + ghost + count : base + rows, :]
+        near_out[here, :] = jnp.where(even, high, low)
+        far_out[here, :] = jnp.where(even, low, high)
+        owned[c * count : (c + 1) * count, :] = total[base + ghost : base + ghost + count, :]
 
 
 def pack_kernel(*refs):
-    given, (count, out, slot_out, table, head, tail, rows) = refs[:6], refs[6:13]
+    given, (count, out, slot_out, table, near, far, rows) = refs[:6], refs[6:13]
     held, sems = refs[13:19], refs[19]
     copies = [pltpu.make_async_copy(a, b, sems.at[i]) for i, (a, b) in enumerate(zip(given, held))]
     for copy in copies:
@@ -135,9 +145,12 @@
     packed = jnp.concatenate([first, second], axis=1)
     table[...] = packed
     ghost = GHOST // LO
-    for c in range(3):
-        head[c * ghost : (c + 1) * ghost, :] = rows[c * own : c * own + ghost, :]
-        tail[c * ghost : (c + 1) * ghost, :] = rows[(c + 1) * own - ghost : (c + 1) * own, :]
+    even = lax.axis_index("dom") % 2 == 0
+    for c in range(3):
+        head = rows[c * own : c * own + ghost, :]
+        tail = rows[(c + 1) * own - ghost : (c + 1) * own, :]
+        near[c * ghost : (c + 1) * ghost, :] = jnp.where(even, tail, head)
+        far[c * ghost : (c + 1) * ghost, :] = jnp.where(even, head, tail)
     cap = 8
     width = out.shape[0]
     n_dom = width // cap
@@ -145,7 +158,7 @@
     live = jnp.where(lanes < count[0, 0], 1.0, 0.0)
     vals = []
     for i in range(8):
-        vals.append(gather_column(packed, slave[i : i + 1, :], own))
+        vals.append(gather(packed, slave[i : i + 1, :], own))
     slave_part = [
         (dual[i : i + 1, :] * live) * vals[i][c] for c in range(3) for i in range(8)
     ]
@@ -202,7 +215,7 @@
         nodes = nodes + jnp.where(face_hi == g, both[8 * g : 8 * (g + 1)], 0.0)
     nodes = nodes.astype(jnp.int32)
     nodes_out[...] = nodes
-    vals = [gather_column(packed, nodes[j : j + 1, :], own) for j in range(8)]
+    vals = [gather(packed, nodes[j : j + 1, :], own) for j in range(8)]
     matrix = [got[24 + 8 * i : 32 + 8 * i, :] for i in range(8)]
     mults = []
     for c in range(3):
@@ -227,13 +240,14 @@
     total = jnp.zeros(out.shape, F32)
     for j in range(8):
         values = [force[8 * c + j : 8 * c + j + 1, :] for c in range(3)]
-        total = total + scatter_column(values, nodes[j : j + 1, :], own)
+        total = total + scatter(values, nodes[j : j + 1, :], own)
     out[...] = total
 
 
-def slave_kernel(returned, slot, dual, slave, owned, master, upper, lower, out):
+def slave_kernel(returned, slot, dual, slave, owned, master, near, far, out):
+    lower, upper = by_side(near[...], far[...])
     own = owned.shape[0] // 3
-    ghost = upper.shape[0] // 3
+    ghost = near.shape[0] // 3
     segs = slot.shape[1]
     n_dom = returned.shape[0]
     mult_rows = returned[...].reshape(n_dom, 256).T
@@ -256,7 +270,7 @@
     total = owned[...] + master[...]
     for i in range(8):
         values = [dual[i : i + 1, :] * mult[8 * c + i : 8 * c + i + 1, :] for c in range(3)]
-        total = total + scatter_column(values, slave[i : i + 1, :], own)
+        total = total + scatter(values, slave[i : i + 1, :], own)
     quarters = out.shape[0]
     per = own // quarters
     for c in range(3):
@@ -265,11 +279,11 @@
             part = block[q * per : (q + 1) * per]
             if q == 0:
                 part = jnp.concatenate(
-                    [part[:ghost] + lower[c * ghost : (c + 1) * ghost, :], part[ghost:]], axis=0
+                    [part[:ghost] + lower[c * ghost : (c + 1) * ghost], part[ghost:]], axis=0
                 )
             if q == quarters - 1:
                 part = jnp.concatenate(
-                    [part[:-ghost], part[-ghost:] + upper[c * ghost : (c + 1) * ghost, :]], axis=0
+                    [part[:-ghost], part[-ghost:] + upper[c * ghost : (c + 1) * ghost]], axis=0
                 )
             out[q, c * per : (c + 1) * per, :] = part
 
@@ -308,15 +322,15 @@
     return jax.ShapeDtypeStruct(dims, F32)
 
 
-def element_forces(table, before, after, connect, shear, bulk, k_shear, k_bulk):
-    rows = table.shape[0] + before.shape[0] + after.shape[0]
+def elements(table, near, far, connect, shear, bulk, k_shear, k_bulk):
+    rows = table.shape[0] + near.shape[0] + far.shape[0]
     elems = connect.shape[1]
     return call(
-        forces_kernel,
-        shape(64, elems),
+        element_kernel,
+        [shape(table.shape[0], LO), shape(*near.shape), shape(*far.shape)],
         table,
-        before,
-        after,
+        near,
+        far,
         connect,
         shear[None],
         bulk[None],
@@ -326,21 +340,10 @@
             pltpu.VMEM((rows, 2 * LO), BF16),
             pltpu.VMEM((64, elems), F32),
             pltpu.VMEM((64, 64), F32),
+            pltpu.VMEM((20, LO, elems), BF16),
+            pltpu.VMEM((rows, LO), F32),
         ],
-        flops=8 * 10**9,
-    )
-
-
-def element_scatter(forces, connect, nodes):
-    own = nodes // LO
-    ghost = GHOST // LO
-    return call(
-        element_scatter_kernel,
-        [shape(3 * own, LO), shape(3 * ghost, LO), shape(3 * ghost, LO)],
-        forces,
-        connect,
-        scratch=[pltpu.VMEM((3 * (own + 2 * ghost), LO), F32)],
-        flops=8 * 10**9,
+        flops=ELEMENT_FLOPS,
     )
 
 
@@ -393,7 +396,7 @@
     )
 
 
-def slave_side(returned, slot, dual, seg_slave, owned, master_part, upper, lower, n_sub):
+def slave_side(returned, slot, dual, seg_slave, owned, master_part, near, far, n_sub):
     own = owned.shape[0] // 3
     return call(
         slave_kernel,
@@ -404,8 +407,8 @@
         seg_slave,
         owned,
         master_part,
-        upper,
-        lower,
+        near,
+        far,
     )
 
 
@@ -426,31 +429,31 @@
 ):
     nodes = displacement.shape[1]
     n_dom, n_sub = lax.axis_size("dom"), lax.axis_size("sub")
-    up = [(i, i + 1) for i in range(n_dom - 1)]
-    down = [(i + 1, i) for i in range(n_dom - 1)]
-    outgoing, slot, table, head, tail = pack(
+    near_pairs = [(i, i ^ 1) for i in range(n_dom)]
+    far_pairs = [(i, min(max(((i + 1) ^ 1) - 1, 0), n_dom - 1)) for i in range(n_dom)]
+    outgoing, slot, table, near, far = pack(
         displacement, seg_slave, dual, mortar, seg_face, seg_part, seg_count, n_dom
     )
     incoming = lax.all_to_all(
         outgoing.reshape(n_dom, 8, 128), "dom", split_axis=0, concat_axis=0, tiled=True
     )
-    before = lax.ppermute(tail, "dom", up)
-    after = lax.ppermute(head, "dom", down)
-    forces = element_forces(table, before, after, connect, shear, bulk, stiff_shear, stiff_bulk)
-    incoming, forces = lax.optimization_barrier((incoming, forces))
+    near = lax.ppermute(near, "dom", near_pairs)
+    far = lax.ppermute(far, "dom", far_pairs)
+    owned, near, far = elements(
+        table, near, far, connect, shear, bulk, stiff_shear, stiff_bulk
+    )
+    incoming, owned = lax.optimization_barrier((incoming, owned))
     mult, master_force, master_nodes = master(
         incoming.reshape(n_dom * 8, 128), table, face_nodes
     )
     returned = lax.all_to_all(mult, "dom", split_axis=0, concat_axis=0, tiled=True)
-    forces, _ = lax.optimization_barrier((forces, mult))
-    owned, low, high = element_scatter(forces, connect, nodes)
-    upper = lax.ppermute(low, "dom", down)
-    lower = lax.ppermute(high, "dom", up)
+    near = lax.ppermute(near, "dom", near_pairs)
+    far = lax.ppermute(far, "dom", far_pairs)
     master_part = call(
         master_scatter_kernel, shape(3 * nodes // LO, LO), master_force, master_nodes
     )
     blocks = slave_side(
-        returned, slot, dual, seg_slave, owned, master_part, upper, lower, n_sub
+        returned, slot, dual, seg_slave, owned, master_part, near, far, n_sub
     )
     me = lax.axis_index("sub")
     sent = [

time: 70 us -> 61.4 us (0.88)
  waiting for transfers between devices: 12.5 us -> 6.73 us
  starting transfers between devices: 37.5 us -> 34.2 us
    all_to_all x1, waiting for transfers between devices: 6.11 us -> 1.82 us  [on_device(): lax.all_to_all(outgoing.reshape(n_dom, 8, 128), 'dom', split_axis=0, conc...]
    all_to_all x1, starting transfers between devices: 10 us -> 7.17 us  [on_device(): lax.all_to_all(outgoing.reshape(n_dom, 8, 128), 'dom', split_axis=0, conc...]
    ppermute x4, waiting for transfers between devices: 3.75 us -> 0.93 us  [the longest x2 0.93 us: on_device(): far = lax.ppermute(far, 'dom', far_pairs)]
    ppermute x4, starting transfers between devices: 15.3 us -> 12.8 us  [the longest x2 12.5 us: on_device(): far = lax.ppermute(far, 'dom', far_pairs)]
    all_to_all x1, starting transfers between devices: 6.49 us -> 8.53 us  [on_device(): lax.all_to_all(mult, 'dom', split_axis=0, concat_axis=0, tiled=True)]
    all_to_all x1, waiting for transfers between devices: 0.01 us -> 1.32 us  [on_device(): lax.all_to_all(mult, 'dom', split_axis=0, concat_axis=0, tiled=True)]
    pallas_call x7 -> x6, Pallas kernels: 17.7 us -> 17.7 us  [call(): pl.pallas_call(kernel, out_shape=outs, in_specs=specs, out_specs=[pl.Bloc...]
  transfers between devices with their start and end apart: 9 -> 9, of which waited for: 4 -> 5; matrix products, arithmetic and copies ran while one was open for 0% -> 0% of each run, Pallas kernels for 15% -> 17%
where the time goes in v3:
time: 61.4 us; the launch traced here: 60.3 us
  starting transfers between devices  34.2 us (56%)
  Pallas kernels  17.7 us (29%)
  waiting for transfers between devices  6.73 us (11%)
  between operations  0.89 us (1%)
  local copies, waits for them, and re-layouts  0.74 us (1%)
    pallas_call x6, Pallas kernels, call(): pl.pallas_call(kernel, out_shape=outs, in_specs=specs, out_specs=[pl.Bloc...  17.7 us
    ppermute x2, starting transfers between devices, on_device(): far = lax.ppermute(far, 'dom', far_pairs)  12.5 us
    all_to_all x1, starting transfers between devices, on_device(): lax.all_to_all(mult, 'dom', split_axis=0, concat_axis=0, tiled=True)  8.53 us
    all_to_all x1, starting transfers between devices, on_device(): lax.all_to_all(outgoing.reshape(n_dom, 8, 128), 'dom', split_axis=0, conc...  7.17 us
    ppermute x3, starting transfers between devices, on_device(): lax.ppermute(lax.dynamic_index_in_dim(blocks, (me + k) % n_sub, 0, keepdi...  5.73 us
    ppermute x3, waiting for transfers between devices, on_device(): lax.ppermute(lax.dynamic_index_in_dim(blocks, (me + k) % n_sub, 0, keepdi...  2.66 us
    all_to_all x1, waiting for transfers between devices, on_device(): lax.all_to_all(outgoing.reshape(n_dom, 8, 128), 'dom', split_axis=0, conc...  1.82 us
    all_to_all x1, waiting for transfers between devices, on_device(): lax.all_to_all(mult, 'dom', split_axis=0, concat_axis=0, tiled=True)  1.32 us
  transfers between devices with their start and end apart: 9, of which 5 were waited for; matrix products, arithmetic and copies ran while one was open for 0% of the time, Pallas kernels for 17%

profile of v3, /device:TPU:8, one launch (start us, length us, event | category | flops | bytes accessed | tf_op | source)
XLA Modules:
  0.0 60.3 jit_solution(6215658472349043530)
XLA Ops:
  0.7 2.8 %shard_map.127 = (f32[512,128]{1,0:T(8,128)}, s32[1,256]{1,0:T(1,128)S(1)}, bf16[192,512]{1,0:T(8,128)(2,1)S(1)}, f32[24,256]{1,0:T(8,128)S(1)}, f32[24,256]{1,0:T(8,128)S(1)}) custom-call(f32[3,16384]{1,0:T(4,128)} %refs_0_.1, s32[8,256]{1,0:T(8,128)} %slave.1, f32[8,256]{1,0:T(8,128)} %dual.1, f32[64,256]{1,0:T(8,128)} %refs_3_.1, s32[1,256]{1,0:T(1,128)} %bitcast.15, ...), custom_call_target="tpu_custom_call" | custom-call | flops 100000000 | bytes 280580 | tf_op jit(solution)/shard_map/pallas_call | solution.py:308
  3.4 0.1 collective-permute-start
  3.5 7.7 %collective-permute-start.1 = (f32[24,256]{1,0:T(8,128)S(1)}, f32[24,256]{1,0:T(8,128)S(1)}, u32[]{:S(2)}, u32[]{:S(2)}) collective-permute-start(f32[24,256]{1,0:T(8,128)S(1)} %get-tuple-element.21), channel_id=1, source_target_pairs={{0,0},{4,8},{8,4},{12,16},{16,12},{20,24},{24,20},{28,32},{32,28},... | collective-permute-start | bytes 73736 | tf_op jit(solution)/shard_map/ppermute | solution.py:441
  11.3 0.0 copy-start.6
  11.3 0.0 copy-start.3
  11.3 0.0 copy-start.4
  11.3 0.0 copy-start.5
  11.3 7.2 %all-to-all-start = ((f32[64,8,128]{2,1,0:T(8,128)}), f32[64,8,128]{2,1,0:T(8,128)S(1)}, u32[]{:S(2)}, u32[]{:S(2)}) async-start(f32[64,8,128]{2,1,0:T(8,128)} %bitcast.3), calls=%async_computation | async-start | bytes 524288 | tf_op jit(solution)/shard_map/all_to_all | solution.py:437
  18.5 0.0 copy-done.6
  18.5 0.0 copy-start.7
  18.5 0.7 %copy-done.7 = f32[768]{0:T(1024)S(1)} copy-done((f32[768]{0:T(1024)S(1)}, f32[768]{0:T(1024)}, u32[]{:S(2)}) %copy-start.7) | copy-done | bytes 3096
  19.2 0.0 collective-permute-done.near
  19.2 0.0 collective-permute-done.1.far
  19.2 0.0 copy-done.3
  19.2 0.0 copy-done.4
  19.2 0.0 copy-done.5
  19.3 0.0 copy-start
  19.3 9.0 %shard_map.128 = (f32[192,256]{1,0:T(8,128)S(1)}, f32[24,256]{1,0:T(8,128)S(1)}, f32[24,256]{1,0:T(8,128)S(1)}) custom-call(bf16[192,512]{1,0:T(8,128)(2,1)S(1)} %get-tuple-element.19.own.table, f32[24,256]{1,0:T(8,128)S(1)} %collective-permute-done.near, f32[24,256]{1,0:T(8,128)S(1)} %collective-permute-done.1.far, s32[20,768]{1,0:T(8,128)S(1)} %copy-done.3, ...), custom_call_target="tpu_custom_call" | custom-call | flops 8000000000 | bytes 538752 | tf_op jit(solution)/shard_map/pallas_call | solution.py:308
  28.2 1.8 %all-to-all-done = f32[64,8,128]{2,1,0:T(8,128)S(1)} async-done(((f32[64,8,128]{2,1,0:T(8,128)}), f32[64,8,128]{2,1,0:T(8,128)S(1)}, u32[]{:S(2)}, u32[]{:S(2)}) %all-to-all-start) | async-done | bytes 262176 | tf_op jit(solution)/shard_map/all_to_all | solution.py:437
  30.0 0.0 copy-done
  30.0 2.6 %shard_map.129 = (f32[64,1,256]{2,1,0:T(1,128)}, f32[24,512]{1,0:T(8,128)S(1)}, s32[8,512]{1,0:T(8,128)S(1)}) custom-call(f32[512,128]{1,0:T(8,128)S(1)} %bitcast.14, bf16[192,512]{1,0:T(8,128)(2,1)S(1)} %get-tuple-element.19.own.table, s32[8,2048]{1,0:T(8,128)S(1)} %copy-done), custom_call_target="tpu_custom_call" | custom-call | flops 100000000 | bytes 720896 | tf_op jit(solution)/shard_map/pallas_call | solution.py:308
  32.7 8.5 %all-to-all-start.1 = ((f32[64,1,256]{2,1,0:T(1,128)}), f32[64,1,256]{2,1,0:T(1,128)S(1)}, u32[]{:S(2)}, u32[]{:S(2)}) async-start(f32[64,1,256]{2,1,0:T(1,128)} %get-tuple-element.24), calls=%async_computation.1 | async-start | bytes 131072 | tf_op jit(solution)/shard_map/all_to_all | solution.py:449
  41.2 0.2 collective-permute-start.2
  41.4 4.8 %collective-permute-start.3 = (f32[24,256]{1,0:T(8,128)S(1)}, f32[24,256]{1,0:T(8,128)S(1)}, u32[]{:S(2)}, u32[]{:S(2)}) collective-permute-start(f32[24,256]{1,0:T(8,128)S(1)} %get-tuple-element.30), channel_id=1, source_target_pairs={{0,0},{4,8},{8,4},{12,16},{16,12},{20,24},{24,20},{28,32},{32,28},... | collective-permute-start | bytes 73736 | tf_op jit(solution)/shard_map/ppermute | solution.py:451
  46.2 0.0 copy-start.1
  46.3 0.0 copy-start.2
  46.3 1.5 %shard_map.130.master = f32[192,256]{1,0:T(8,128)S(1)} custom-call(f32[24,512]{1,0:T(8,128)S(1)} %get-tuple-element.27.force, s32[8,512]{1,0:T(8,128)S(1)} %get-tuple-element.28.nodes), custom_call_target="tpu_custom_call" | custom-call | flops 100000000 | bytes 65536 | tf_op jit(solution)/shard_map/pallas_call | solution.py:308
  47.8 0.0 collective-permute-done.2.near
  47.8 0.9 %collective-permute-done.3.far = f32[24,256]{1,0:T(8,128)S(1)} collective-permute-done((f32[24,256]{1,0:T(8,128)S(1)}, f32[24,256]{1,0:T(8,128)S(1)}, u32[]{:S(2)}, u32[]{:S(2)}) %collective-permute-start.3) | collective-permute-done | bytes 24608 | tf_op jit(solution)/shard_map/ppermute | solution.py:451
  48.7 1.3 %all-to-all-done.1.returned = f32[64,1,256]{2,1,0:T(1,128)S(1)} async-done(((f32[64,1,256]{2,1,0:T(1,128)}), f32[64,1,256]{2,1,0:T(1,128)S(1)}, u32[]{:S(2)}, u32[]{:S(2)}) %all-to-all-start.1) | async-done | bytes 65568 | tf_op jit(solution)/shard_map/all_to_all | solution.py:449
  50.0 0.0 copy-done.1
  50.0 0.0 copy-done.2
  50.0 1.2 %shard_map.131 = f32[4,48,256]{2,1,0:T(8,128)S(1)} custom-call(f32[64,1,256]{2,1,0:T(1,128)S(1)} %all-to-all-done.1.returned, s32[1,256]{1,0:T(1,128)S(1)} %get-tuple-element.25.slot, f32[8,256]{1,0:T(8,128)S(1)} %copy-done.2, s32[8,256]{1,0:T(8,128)S(1)} %copy-done.1, f32[192,256]{1,0:T(8,128)S(1)} %get-tuple-element.26.owned, ...), custom_call_target="tpu_custom_call" | custom-call | flops 100000000 | bytes 525312 | tf_op jit(solution)/shard_map/pallas_call | solution.py:308
  51.3 1.6 %collective-permute-start.4 = (f32[48,256]{1,0:T(8,128)S(1)}, f32[48,256]{1,0:T(8,128)S(1)}, u32[]{:S(2)}, u32[]{:S(2)}) collective-permute-start(f32[48,256]{1,0:T(8,128)S(1)} %get-tuple-element.33), channel_id=1, source_target_pairs={{0,1},{1,2},{2,3},{3,0},{4,5},{5,6},{6,7},{7,4},{8,9},{9,10},{10,1... | collective-permute-start | bytes 147464 | tf_op jit(solution)/shard_map/ppermute | solution.py:460
  52.8 2.7 %collective-permute-start.5 = (f32[48,256]{1,0:T(8,128)S(1)}, f32[48,256]{1,0:T(8,128)S(1)}, u32[]{:S(2)}, u32[]{:S(2)}) collective-permute-start(f32[48,256]{1,0:T(8,128)S(1)} %get-tuple-element.32), channel_id=1, source_target_pairs={{0,2},{1,3},{2,0},{3,1},{4,6},{5,7},{6,4},{7,5},{8,10},{9,11},{10,... | collective-permute-start | bytes 147464 | tf_op jit(solution)/shard_map/ppermute | solution.py:460
  55.6 1.4 %collective-permute-start.6 = (f32[48,256]{1,0:T(8,128)S(1)}, f32[48,256]{1,0:T(8,128)S(1)}, u32[]{:S(2)}, u32[]{:S(2)}) collective-permute-start(f32[48,256]{1,0:T(8,128)S(1)} %get-tuple-element.31), channel_id=1, source_target_pairs={{0,3},{1,0},{2,1},{3,2},{4,7},{5,4},{6,5},{7,6},{8,11},{9,8},{10,9... | collective-permute-start | bytes 147464 | tf_op jit(solution)/shard_map/ppermute | solution.py:460
  57.0 0.0 collective-permute-done.4.a
  57.0 1.4 %collective-permute-done.5.b = f32[48,256]{1,0:T(8,128)S(1)} collective-permute-done((f32[48,256]{1,0:T(8,128)S(1)}, f32[48,256]{1,0:T(8,128)S(1)}, u32[]{:S(2)}, u32[]{:S(2)}) %collective-permute-start.5) | collective-permute-done | bytes 49184 | tf_op jit(solution)/shard_map/ppermute | solution.py:460
  58.4 1.2 %collective-permute-done.6.d = f32[48,256]{1,0:T(8,128)S(1)} collective-permute-done((f32[48,256]{1,0:T(8,128)S(1)}, f32[48,256]{1,0:T(8,128)S(1)}, u32[]{:S(2)}, u32[]{:S(2)}) %collective-permute-start.6) | collective-permute-done | bytes 49184 | tf_op jit(solution)/shard_map/ppermute | solution.py:460
  59.7 0.7 %shard_map.132 = f32[3,4096]{1,0:T(4,128)} custom-call(f32[48,256]{1,0:T(8,128)S(1)} %get-tuple-element.34.own_part, f32[48,256]{1,0:T(8,128)S(1)} %collective-permute-done.4.a, f32[48,256]{1,0:T(8,128)S(1)} %collective-permute-done.5.b, f32[48,256]{1,0:T(8,128)S(1)} %collective-permute-done.6.d), custom_call_target="tpu_custom_call" | custom-call | flops 100000000 | bytes 196608 | tf_op jit(solution)/shard_map/pallas_call | solution.py:308
  (3 shorter events, 0.0 us)
Async XLA Ops:
  3.4 15.8 %collective-permute-start = (f32[24,256]{1,0:T(8,128)S(1)}, f32[24,256]{1,0:T(8,128)S(1)}, u32[]{:S(2)}, u32[]{:S(2)}) collective-permute-start(f32[24,256]{1,0:T(8,128)S(1)} %get-tuple-element.20), channel_id=1, source_target_pairs={{0,4},{4,0},{8,12},{12,8},{16,20},{20,16},{24,28},{28,24},{32,36},... | collective-permute-start | bytes 73736 | tf_op jit(solution)/shard_map/ppermute | solution.py:440
  3.5 15.7 %collective-permute-start.1 = (f32[24,256]{1,0:T(8,128)S(1)}, f32[24,256]{1,0:T(8,128)S(1)}, u32[]{:S(2)}, u32[]{:S(2)}) collective-permute-start(f32[24,256]{1,0:T(8,128)S(1)} %get-tuple-element.21), channel_id=1, source_target_pairs={{0,0},{4,8},{8,4},{12,16},{16,12},{20,24},{24,20},{28,32},{32,28},... | collective-permute-start | bytes 73736 | tf_op jit(solution)/shard_map/ppermute | solution.py:441
  11.3 7.2 %copy-start.6 = (f32[768]{0:T(1024)S(1)}, f32[768]{0:T(1024)}, u32[]{:S(2)}) copy-start(f32[768]{0:T(1024)} %param.15) | copy-start | bytes 9220
  11.3 7.9 %copy-start.3 = (s32[20,768]{1,0:T(8,128)S(1)}, s32[20,768]{1,0:T(8,128)}, u32[]{:S(2)}) copy-start(s32[20,768]{1,0:T(8,128)} %connect.1) | copy-start | bytes 184324
  11.3 7.9 %copy-start.4 = (f32[60,60]{1,0:T(8,128)S(1)}, f32[60,60]{1,0:T(8,128)}, u32[]{:S(2)}) copy-start(f32[60,60]{1,0:T(8,128)} %k_shear.1) | copy-start | bytes 43204
  11.3 7.9 %copy-start.5 = (f32[60,60]{1,0:T(8,128)S(1)}, f32[60,60]{1,0:T(8,128)}, u32[]{:S(2)}) copy-start(f32[60,60]{1,0:T(8,128)} %k_bulk.1) | copy-start | bytes 43204
  11.3 18.7 %all-to-all-start = ((f32[64,8,128]{2,1,0:T(8,128)}), f32[64,8,128]{2,1,0:T(8,128)S(1)}, u32[]{:S(2)}, u32[]{:S(2)}) async-start(f32[64,8,128]{2,1,0:T(8,128)} %bitcast.3), calls=%async_computation | async-start | bytes 524288 | tf_op jit(solution)/shard_map/all_to_all | solution.py:437
  18.5 0.7 %copy-start.7 = (f32[768]{0:T(1024)S(1)}, f32[768]{0:T(1024)}, u32[]{:S(2)}) copy-start(f32[768]{0:T(1024)} %param.16) | copy-start | bytes 9220
  19.3 10.8 %copy-start = (s32[8,2048]{1,0:T(8,128)S(1)}, s32[8,2048]{1,0:T(8,128)}, u32[]{:S(2)}) copy-start(s32[8,2048]{1,0:T(8,128)} %faces.1) | copy-start | bytes 196612
  32.7 17.4 %all-to-all-start.1 = ((f32[64,1,256]{2,1,0:T(1,128)}), f32[64,1,256]{2,1,0:T(1,128)S(1)}, u32[]{:S(2)}, u32[]{:S(2)}) async-start(f32[64,1,256]{2,1,0:T(1,128)} %get-tuple-element.24), calls=%async_computation.1 | async-start | bytes 131072 | tf_op jit(solution)/shard_map/all_to_all | solution.py:449
  41.2 6.6 %collective-permute-start.2 = (f32[24,256]{1,0:T(8,128)S(1)}, f32[24,256]{1,0:T(8,128)S(1)}, u32[]{:S(2)}, u32[]{:S(2)}) collective-permute-start(f32[24,256]{1,0:T(8,128)S(1)} %get-tuple-element.29), channel_id=1, source_target_pairs={{0,4},{4,0},{8,12},{12,8},{16,20},{20,16},{24,28},{28,24},{32,36},... | collective-permute-start | bytes 73736 | tf_op jit(solution)/shard_map/ppermute | solution.py:450
  41.4 7.3 %collective-permute-start.3 = (f32[24,256]{1,0:T(8,128)S(1)}, f32[24,256]{1,0:T(8,128)S(1)}, u32[]{:S(2)}, u32[]{:S(2)}) collective-permute-start(f32[24,256]{1,0:T(8,128)S(1)} %get-tuple-element.30), channel_id=1, source_target_pairs={{0,0},{4,8},{8,4},{12,16},{16,12},{20,24},{24,20},{28,32},{32,28},... | collective-permute-start | bytes 73736 | tf_op jit(solution)/shard_map/ppermute | solution.py:451
  46.2 3.8 %copy-start.1 = (s32[8,256]{1,0:T(8,128)S(1)}, s32[8,256]{1,0:T(8,128)}, u32[]{:S(2)}) copy-start(s32[8,256]{1,0:T(8,128)} %slave.1) | copy-start | bytes 24580
  46.3 3.8 %copy-start.2 = (f32[8,256]{1,0:T(8,128)S(1)}, f32[8,256]{1,0:T(8,128)}, u32[]{:S(2)}) copy-start(f32[8,256]{1,0:T(8,128)} %dual.1) | copy-start | bytes 24580
  51.3 5.7 %collective-permute-start.4 = (f32[48,256]{1,0:T(8,128)S(1)}, f32[48,256]{1,0:T(8,128)S(1)}, u32[]{:S(2)}, u32[]{:S(2)}) collective-permute-start(f32[48,256]{1,0:T(8,128)S(1)} %get-tuple-element.33), channel_id=1, source_target_pairs={{0,1},{1,2},{2,3},{3,0},{4,5},{5,6},{6,7},{7,4},{8,9},{9,10},{10,1... | collective-permute-start | bytes 147464 | tf_op jit(solution)/shard_map/ppermute | solution.py:460
  52.8 5.6 %collective-permute-start.5 = (f32[48,256]{1,0:T(8,128)S(1)}, f32[48,256]{1,0:T(8,128)S(1)}, u32[]{:S(2)}, u32[]{:S(2)}) collective-permute-start(f32[48,256]{1,0:T(8,128)S(1)} %get-tuple-element.32), channel_id=1, source_target_pairs={{0,2},{1,3},{2,0},{3,1},{4,6},{5,7},{6,4},{7,5},{8,10},{9,11},{10,... | collective-permute-start | bytes 147464 | tf_op jit(solution)/shard_map/ppermute | solution.py:460
  55.6 4.1 %collective-permute-start.6 = (f32[48,256]{1,0:T(8,128)S(1)}, f32[48,256]{1,0:T(8,128)S(1)}, u32[]{:S(2)}, u32[]{:S(2)}) collective-permute-start(f32[48,256]{1,0:T(8,128)S(1)} %get-tuple-element.31), channel_id=1, source_target_pairs={{0,3},{1,0},{2,1},{3,2},{4,7},{5,4},{6,5},{7,6},{8,11},{9,8},{10,9... | collective-permute-start | bytes 147464 | tf_op jit(solution)/shard_map/ppermute | solution.py:460

commit v4 on v3

--- a/solution.py
+++ b/solution.py
@@ -8,6 +8,7 @@
 GHOST = 2048
 LO = 256
 penalty = 2.0
+WORDS = 96
 ELEMENT_FLOPS = 8 * 10**9
 F32 = jnp.float32
 BF16 = jnp.bfloat16
@@ -87,6 +88,7 @@
     ghost = near.shape[0] // 3
     count = own.shape[0] // 3
     rows = count + 2 * ghost
+    elems = connect.shape[1]
     for source, first_row in zip(by_side(near[...], far[...]), (0, rows - ghost)):
         first, second = pieces(source)
         for c in range(3):
@@ -113,7 +115,8 @@
         wide = jnp.concatenate([k_first, k_second, k_first, k_second], axis=1)
         return jnp.dot(wide, g, preferred_element_type=F32)
 
-    dofs[...] = shear[...] * product(k_shear) + bulk[...] * product(k_bulk)
+    by_shear, by_bulk = (m[...].reshape(1, elems) for m in (shear, bulk))
+    dofs[...] = by_shear * product(k_shear) + by_bulk * product(k_bulk)
     total[...] = jnp.zeros_like(total)
     for a in range(20):
         values = [dofs[20 * c + a : 20 * c + a + 1, :] for c in range(3)]
@@ -127,6 +130,12 @@
         near_out[here, :] = jnp.where(even, high, low)
         far_out[here, :] = jnp.where(even, low, high)
         owned[c * count : (c + 1) * count, :] = total[base + ghost : base + ghost + count, :]
+
+
+def place_in_group(part, n_dom):
+    ny, nz = 4, n_dom // 8
+    y, z, core = part // (2 * nz), (part // 2) % nz, part % 2
+    return n_dom - 1 - (z * (2 * ny) + y * 2 + core)
 
 
 def pack_kernel(*refs):
@@ -152,8 +161,8 @@
         near[c * ghost : (c + 1) * ghost, :] = jnp.where(even, tail, head)
         far[c * ghost : (c + 1) * ghost, :] = jnp.where(even, head, tail)
     cap = 8
-    width = out.shape[0]
-    n_dom = width // cap
+    n_dom = out.shape[0]
+    width = n_dom * cap
     lanes = lax.broadcasted_iota(jnp.int32, (1, segs), 1)
     live = jnp.where(lanes < count[0, 0], 1.0, 0.0)
     vals = []
@@ -164,7 +173,7 @@
     ]
     payload = jnp.concatenate(
         slave_part
-        + [mortar[...] * live, face[...].astype(F32), jnp.zeros((39, segs), F32)],
+        + [mortar[...] * live, face[...].astype(F32), jnp.zeros((WORDS - 89, segs), F32)],
         axis=0,
     )
     hits = lax.broadcasted_iota(jnp.int32, (n_dom, segs), 0) == part[...]
@@ -177,8 +186,10 @@
         hits_b, jnp.where(earlier, 1.0, 0.0).astype(BF16), preferred_element_type=F32
     )
     rank = jnp.sum(jnp.where(hits, before, 0.0), axis=0, keepdims=True).astype(jnp.int32)
-    slot = part[...] * cap + rank
-    slot_out[...] = slot
+    place_of = place_in_group(part[...], n_dom)
+    slot = rank * n_dom + place_of
+    slot_out[0:1, :] = place_of
+    slot_out[1:2, :] = rank
     place = jnp.where(
         lax.broadcasted_iota(jnp.int32, (width, segs), 0) == slot, 1.0, 0.0
     ).astype(BF16)
@@ -186,20 +197,24 @@
     rest = payload - p1.astype(F32)
     p2 = rest.astype(BF16)
     p3 = (rest - p2.astype(F32)).astype(BF16)
-    out[...] = lax.dot_general(
+    placed = lax.dot_general(
         jnp.concatenate([place, place, place], axis=1),
         jnp.concatenate([p1, p2, p3], axis=1),
         (((1,), (1,)), ((), ())),
         preferred_element_type=F32,
     )
+    for k in range(cap):
+        out[:, 0, WORDS * k : WORDS * (k + 1)] = placed[n_dom * k : n_dom * (k + 1), :]
 
 
 def master_kernel(incoming, table, faces, mult_out, force_out, nodes_out):
     own = table.shape[0] // 3
-    width = incoming.shape[0]
-    n_dom = width // 8
+    n_dom = incoming.shape[0]
+    width = n_dom * 8
     packed = table[...]
-    got = incoming[...].T
+    got = jnp.concatenate(
+        [incoming[:, 0, WORDS * k : WORDS * (k + 1)] for k in range(8)], axis=0
+    ).T
     face = got[88:89, :].astype(jnp.int32)
     groups = faces.shape[1] // LO
     listing = jnp.concatenate([faces[:, g * LO : (g + 1) * LO] for g in range(groups)], axis=0)
@@ -230,9 +245,8 @@
             force = force - matrix[i] * mult
         force_out[8 * c : 8 * c + 8, :] = force
     back = jnp.concatenate(mults + [jnp.zeros((8, width), F32)], axis=0).T
-    back = back.reshape(n_dom, 8, 32)
     for k in range(8):
-        mult_out[:, 0, 32 * k : 32 * (k + 1)] = back[:, k, :]
+        mult_out[:, 0, 32 * k : 32 * (k + 1)] = back[n_dom * k : n_dom * (k + 1), :]
 
 
 def master_scatter_kernel(force, nodes, out):
@@ -256,14 +270,14 @@
     m2 = rest.astype(BF16)
     m3 = (rest - m2.astype(F32)).astype(BF16)
     hot = jnp.where(
-        lax.broadcasted_iota(jnp.int32, (n_dom, segs), 0) == (slot[...] >> 3), 1.0, 0.0
+        lax.broadcasted_iota(jnp.int32, (n_dom, segs), 0) == slot[0:1, :], 1.0, 0.0
     ).astype(BF16)
     picked = jnp.dot(
         jnp.concatenate([m1, m2, m3], axis=1),
         jnp.concatenate([hot, hot, hot], axis=0),
         preferred_element_type=F32,
     )
-    rank = slot[...] & 7
+    rank = slot[1:2, :]
     mult = jnp.zeros((32, segs), F32)
     for k in range(8):
         mult = mult + jnp.where(rank == k, picked[32 * k : 32 * (k + 1)], 0.0)
@@ -332,8 +346,8 @@
         near,
         far,
         connect,
-        shear[None],
-        bulk[None],
+        shear,
+        bulk,
         k_shear,
         k_bulk,
         scratch=[
@@ -353,8 +367,8 @@
     return call(
         pack_kernel,
         [
-            shape(n_dom * 8, 128),
-            jax.ShapeDtypeStruct((1, segs), jnp.int32),
+            shape(n_dom, 1, 8 * WORDS),
+            jax.ShapeDtypeStruct((2, segs), jnp.int32),
             jax.ShapeDtypeStruct((3 * own, 2 * LO), BF16),
             shape(3 * GHOST // LO, LO),
             shape(3 * GHOST // LO, LO),
@@ -382,7 +396,7 @@
 
 
 def master(incoming, table, face_nodes):
-    width = incoming.shape[0]
+    width = incoming.shape[0] * 8
     return call(
         master_kernel,
         [
@@ -429,24 +443,21 @@
 ):
     nodes = displacement.shape[1]
     n_dom, n_sub = lax.axis_size("dom"), lax.axis_size("sub")
+    group = sorted(range(n_dom), key=lambda part: place_in_group(part, n_dom))
     near_pairs = [(i, i ^ 1) for i in range(n_dom)]
     far_pairs = [(i, min(max(((i + 1) ^ 1) - 1, 0), n_dom - 1)) for i in range(n_dom)]
     outgoing, slot, table, near, far = pack(
         displacement, seg_slave, dual, mortar, seg_face, seg_part, seg_count, n_dom
     )
-    incoming = lax.all_to_all(
-        outgoing.reshape(n_dom, 8, 128), "dom", split_axis=0, concat_axis=0, tiled=True
-    )
+    incoming = lax.all_to_all(outgoing, "dom", 0, 0, axis_index_groups=[group], tiled=True)
     near = lax.ppermute(near, "dom", near_pairs)
     far = lax.ppermute(far, "dom", far_pairs)
     owned, near, far = elements(
         table, near, far, connect, shear, bulk, stiff_shear, stiff_bulk
     )
     incoming, owned = lax.optimization_barrier((incoming, owned))
-    mult, master_force, master_nodes = master(
-        incoming.reshape(n_dom * 8, 128), table, face_nodes
-    )
-    returned = lax.all_to_all(mult, "dom", split_axis=0, concat_axis=0, tiled=True)
+    mult, master_force, master_nodes = master(incoming, table, face_nodes)
+    returned = lax.all_to_all(mult, "dom", 0, 0, axis_index_groups=[group], tiled=True)
     near = lax.ppermute(near, "dom", near_pairs)
     far = lax.ppermute(far, "dom", far_pairs)
     master_part = call(

time: 61.4 us -> 60.4 us (0.984); the launches traced: 60.3 us -> 60.1 us
  waiting for transfers between devices: 6.73 us -> 5.31 us
  starting transfers between devices: 34.2 us -> 35.5 us
  local copies, waits for them, and re-layouts: 0.74 us -> 0.07 us
    all_to_all x2, waiting for transfers between devices: 3.13 us -> 0.01 us  [the longest x1 0.01 us: on_device(): lax.all_to_all(outgoing, 'dom', 0, 0, axis_index_groups=[group], tiled=True)]
    all_to_all x2, starting transfers between devices: 15.7 us -> 18.8 us  [the longest x1 10.1 us: on_device(): lax.all_to_all(mult, 'dom', 0, 0, axis_index_groups=[group], tiled=True)]
    ppermute x2, starting transfers between devices: 12.5 us -> 10.8 us  [on_device(): far = lax.ppermute(far, 'dom', far_pairs)]
    ppermute x2, waiting for transfers between devices: 0.93 us -> 2.63 us  [on_device(): far = lax.ppermute(far, 'dom', far_pairs)]
    unnamed x16, local copies, waits for them, and re-layouts: 0.71 us -> 0.05 us
  transfers between devices with their start and end apart: 9 -> 9, of which waited for: 5 -> 3; matrix products, arithmetic and copies ran while one was open for 0% -> 0% of each run, Pallas kernels for 17% -> 17%
where the time goes in v4:
time: 60.4 us; the launch traced here: 60.1 us
  starting transfers between devices  35.5 us (59%)
  Pallas kernels  18.3 us (30%)
  waiting for transfers between devices  5.31 us (9%)
  between operations  0.92 us (2%)
    pallas_call x6, Pallas kernels, call(): pl.pallas_call(kernel, out_shape=outs, in_specs=specs, out_specs=[pl.Bloc...  18.3 us
    ppermute x2, starting transfers between devices, on_device(): far = lax.ppermute(far, 'dom', far_pairs)  10.8 us
    all_to_all x1, starting transfers between devices, on_device(): lax.all_to_all(mult, 'dom', 0, 0, axis_index_groups=[group], tiled=True)  10.1 us
    all_to_all x1, starting transfers between devices, on_device(): lax.all_to_all(outgoing, 'dom', 0, 0, axis_index_groups=[group], tiled=True)  8.75 us
    ppermute x3, starting transfers between devices, on_device(): lax.ppermute(lax.dynamic_index_in_dim(blocks, (me + k) % n_sub, 0, keepdi...  5.73 us
    ppermute x3, waiting for transfers between devices, on_device(): lax.ppermute(lax.dynamic_index_in_dim(blocks, (me + k) % n_sub, 0, keepdi...  2.67 us
    ppermute x2, waiting for transfers between devices, on_device(): far = lax.ppermute(far, 'dom', far_pairs)  2.63 us
  transfers between devices with their start and end apart: 9, of which 3 were waited for; matrix products, arithmetic and copies ran while one was open for 0% of the time, Pallas kernels for 17%

profile of v4, /device:TPU:8, one launch (start us, length us, event | category | flops | bytes accessed | tf_op | source)
XLA Modules:
  0.0 60.1 jit_solution(3386808942987336707)
XLA Ops:
  0.7 3.2 %shard_map.127 = (f32[64,1,768]{2,1,0:T(1,128)}, s32[2,256]{1,0:T(2,128)S(1)}, bf16[192,512]{1,0:T(8,128)(2,1)S(1)}, f32[24,256]{1,0:T(8,128)S(1)}, f32[24,256]{1,0:T(8,128)S(1)}) custom-call(f32[3,16384]{1,0:T(4,128)} %refs_0_.1, s32[8,256]{1,0:T(8,128)} %slave.1, f32[8,256]{1,0:T(8,128)} %dual.1, f32[64,256]{1,0:T(8,128)} %refs_3_.1, s32[1,256]{1,0:T(1,128)} %bitcast.12, ...), custom_call_target="tpu_custom_call" | custom-call | flops 100000000 | bytes 280580 | tf_op jit(solution)/shard_map/pallas_call | solution.py:322
  3.8 0.1 collective-permute-start
  3.9 7.7 %collective-permute-start.1 = (f32[24,256]{1,0:T(8,128)S(1)}, f32[24,256]{1,0:T(8,128)S(1)}, u32[]{:S(2)}, u32[]{:S(2)}) collective-permute-start(f32[24,256]{1,0:T(8,128)S(1)} %get-tuple-element.21), channel_id=1, source_target_pairs={{0,0},{4,8},{8,4},{12,16},{16,12},{20,24},{24,20},{28,32},{32,28},... | collective-permute-start | bytes 73736 | tf_op jit(solution)/shard_map/ppermute | solution.py:454
  11.7 0.0 copy-start.3
  11.7 0.0 copy-start.4
  11.7 0.0 copy-start.5
  11.7 0.0 copy-start.6
  11.7 0.0 copy-start.7
  11.7 8.7 %all-to-all-start = ((f32[64,1,768]{2,1,0:T(1,128)}), f32[64,1,768]{2,1,0:T(1,128)S(1)}, u32[]{:S(2)}, u32[]{:S(2)}) async-start(f32[64,1,768]{2,1,0:T(1,128)} %get-tuple-element.18), calls=%async_computation | async-start | bytes 393216 | tf_op jit(solution)/shard_map/all_to_all | solution.py:452
  20.5 0.0 collective-permute-done.near
  20.5 0.0 collective-permute-done.1.far
  20.5 0.0 copy-done.3
  20.5 0.0 copy-done.4
  20.5 0.0 copy-done.5
  20.5 0.0 copy-done.6
  20.5 0.0 copy-done.7
  20.6 0.0 copy-start
  20.6 9.0 %shard_map.128 = (f32[192,256]{1,0:T(8,128)S(1)}, f32[24,256]{1,0:T(8,128)S(1)}, f32[24,256]{1,0:T(8,128)S(1)}) custom-call(bf16[192,512]{1,0:T(8,128)(2,1)S(1)} %get-tuple-element.19.own.table, f32[24,256]{1,0:T(8,128)S(1)} %collective-permute-done.near, f32[24,256]{1,0:T(8,128)S(1)} %collective-permute-done.1.far, s32[20,768]{1,0:T(8,128)S(1)} %copy-done.3, ...), custom_call_target="tpu_custom_call" | custom-call | flops 8000000000 | bytes 538752 | tf_op jit(solution)/shard_map/pallas_call | solution.py:322
  29.5 0.0 all-to-all-done.incoming
  29.5 0.0 copy-done
  29.6 2.8 %shard_map.129 = (f32[64,1,256]{2,1,0:T(1,128)}, f32[24,512]{1,0:T(8,128)S(1)}, s32[8,512]{1,0:T(8,128)S(1)}) custom-call(f32[64,1,768]{2,1,0:T(1,128)S(1)} %all-to-all-done.incoming, bf16[192,512]{1,0:T(8,128)(2,1)S(1)} %get-tuple-element.19.own.table, s32[8,2048]{1,0:T(8,128)S(1)} %copy-done), custom_call_target="tpu_custom_call" | custom-call | flops 100000000 | bytes 655360 | tf_op jit(solution)/shard_map/pallas_call | solution.py:322
  32.3 10.1 %all-to-all-start.1 = ((f32[64,1,256]{2,1,0:T(1,128)}), f32[64,1,256]{2,1,0:T(1,128)S(1)}, u32[]{:S(2)}, u32[]{:S(2)}) async-start(f32[64,1,256]{2,1,0:T(1,128)} %get-tuple-element.24), calls=%async_computation.1 | async-start | bytes 131072 | tf_op jit(solution)/shard_map/all_to_all | solution.py:460
  42.4 0.2 collective-permute-start.2
  42.6 3.0 %collective-permute-start.3 = (f32[24,256]{1,0:T(8,128)S(1)}, f32[24,256]{1,0:T(8,128)S(1)}, u32[]{:S(2)}, u32[]{:S(2)}) collective-permute-start(f32[24,256]{1,0:T(8,128)S(1)} %get-tuple-element.30), channel_id=1, source_target_pairs={{0,0},{4,8},{8,4},{12,16},{16,12},{20,24},{24,20},{28,32},{32,28},... | collective-permute-start | bytes 73736 | tf_op jit(solution)/shard_map/ppermute | solution.py:462
  45.6 0.0 copy-start.1
  45.6 0.0 copy-start.2
  45.7 1.5 %shard_map.130.master = f32[192,256]{1,0:T(8,128)S(1)} custom-call(f32[24,512]{1,0:T(8,128)S(1)} %get-tuple-element.27.force, s32[8,512]{1,0:T(8,128)S(1)} %get-tuple-element.28.nodes), custom_call_target="tpu_custom_call" | custom-call | flops 100000000 | bytes 65536 | tf_op jit(solution)/shard_map/pallas_call | solution.py:322
  47.2 0.0 collective-permute-done.2.near
  47.2 2.6 %collective-permute-done.3.far = f32[24,256]{1,0:T(8,128)S(1)} collective-permute-done((f32[24,256]{1,0:T(8,128)S(1)}, f32[24,256]{1,0:T(8,128)S(1)}, u32[]{:S(2)}, u32[]{:S(2)}) %collective-permute-start.3) | collective-permute-done | bytes 24608 | tf_op jit(solution)/shard_map/ppermute | solution.py:462
  49.8 0.0 all-to-all-done.1.returned
  49.8 0.0 copy-done.1
  49.8 0.0 copy-done.2
  49.8 1.2 %shard_map.131 = f32[4,48,256]{2,1,0:T(8,128)S(1)} custom-call(f32[64,1,256]{2,1,0:T(1,128)S(1)} %all-to-all-done.1.returned, s32[2,256]{1,0:T(2,128)S(1)} %get-tuple-element.25.slot, f32[8,256]{1,0:T(8,128)S(1)} %copy-done.2, s32[8,256]{1,0:T(8,128)S(1)} %copy-done.1, f32[192,256]{1,0:T(8,128)S(1)} %get-tuple-element.26.owned, ...), custom_call_target="tpu_custom_call" | custom-call | flops 100000000 | bytes 526336 | tf_op jit(solution)/shard_map/pallas_call | solution.py:322
  51.0 1.6 %collective-permute-start.4 = (f32[48,256]{1,0:T(8,128)S(1)}, f32[48,256]{1,0:T(8,128)S(1)}, u32[]{:S(2)}, u32[]{:S(2)}) collective-permute-start(f32[48,256]{1,0:T(8,128)S(1)} %get-tuple-element.33), channel_id=1, source_target_pairs={{0,1},{1,2},{2,3},{3,0},{4,5},{5,6},{6,7},{7,4},{8,9},{9,10},{10,1... | collective-permute-start | bytes 147464 | tf_op jit(solution)/shard_map/ppermute | solution.py:471
  52.6 2.7 %collective-permute-start.5 = (f32[48,256]{1,0:T(8,128)S(1)}, f32[48,256]{1,0:T(8,128)S(1)}, u32[]{:S(2)}, u32[]{:S(2)}) collective-permute-start(f32[48,256]{1,0:T(8,128)S(1)} %get-tuple-element.32), channel_id=1, source_target_pairs={{0,2},{1,3},{2,0},{3,1},{4,6},{5,7},{6,4},{7,5},{8,10},{9,11},{10,... | collective-permute-start | bytes 147464 | tf_op jit(solution)/shard_map/ppermute | solution.py:471
  55.4 1.4 %collective-permute-start.6 = (f32[48,256]{1,0:T(8,128)S(1)}, f32[48,256]{1,0:T(8,128)S(1)}, u32[]{:S(2)}, u32[]{:S(2)}) collective-permute-start(f32[48,256]{1,0:T(8,128)S(1)} %get-tuple-element.31), channel_id=1, source_target_pairs={{0,3},{1,0},{2,1},{3,2},{4,7},{5,4},{6,5},{7,6},{8,11},{9,8},{10,9... | collective-permute-start | bytes 147464 | tf_op jit(solution)/shard_map/ppermute | solution.py:471
  56.8 0.0 collective-permute-done.4.a
  56.8 1.4 %collective-permute-done.5.b = f32[48,256]{1,0:T(8,128)S(1)} collective-permute-done((f32[48,256]{1,0:T(8,128)S(1)}, f32[48,256]{1,0:T(8,128)S(1)}, u32[]{:S(2)}, u32[]{:S(2)}) %collective-permute-start.5) | collective-permute-done | bytes 49184 | tf_op jit(solution)/shard_map/ppermute | solution.py:471
  58.2 1.2 %collective-permute-done.6.d = f32[48,256]{1,0:T(8,128)S(1)} collective-permute-done((f32[48,256]{1,0:T(8,128)S(1)}, f32[48,256]{1,0:T(8,128)S(1)}, u32[]{:S(2)}, u32[]{:S(2)}) %collective-permute-start.6) | collective-permute-done | bytes 49184 | tf_op jit(solution)/shard_map/ppermute | solution.py:471
  59.4 0.7 %shard_map.132 = f32[3,4096]{1,0:T(4,128)} custom-call(f32[48,256]{1,0:T(8,128)S(1)} %get-tuple-element.34.own_part, f32[48,256]{1,0:T(8,128)S(1)} %collective-permute-done.4.a, f32[48,256]{1,0:T(8,128)S(1)} %collective-permute-done.5.b, f32[48,256]{1,0:T(8,128)S(1)} %collective-permute-done.6.d), custom_call_target="tpu_custom_call" | custom-call | flops 100000000 | bytes 196608 | tf_op jit(solution)/shard_map/pallas_call | solution.py:322
  (1 shorter events, 0.0 us)
Async XLA Ops:
  3.8 16.7 %collective-permute-start = (f32[24,256]{1,0:T(8,128)S(1)}, f32[24,256]{1,0:T(8,128)S(1)}, u32[]{:S(2)}, u32[]{:S(2)}) collective-permute-start(f32[24,256]{1,0:T(8,128)S(1)} %get-tuple-element.20), channel_id=1, source_target_pairs={{0,4},{4,0},{8,12},{12,8},{16,20},{20,16},{24,28},{28,24},{32,36},... | collective-permute-start | bytes 73736 | tf_op jit(solution)/shard_map/ppermute | solution.py:453
  3.9 16.6 %collective-permute-start.1 = (f32[24,256]{1,0:T(8,128)S(1)}, f32[24,256]{1,0:T(8,128)S(1)}, u32[]{:S(2)}, u32[]{:S(2)}) collective-permute-start(f32[24,256]{1,0:T(8,128)S(1)} %get-tuple-element.21), channel_id=1, source_target_pairs={{0,0},{4,8},{8,4},{12,16},{16,12},{20,24},{24,20},{28,32},{32,28},... | collective-permute-start | bytes 73736 | tf_op jit(solution)/shard_map/ppermute | solution.py:454
  11.7 8.8 %copy-start.3 = (s32[20,768]{1,0:T(8,128)S(1)}, s32[20,768]{1,0:T(8,128)}, u32[]{:S(2)}) copy-start(s32[20,768]{1,0:T(8,128)} %connect.1) | copy-start | bytes 184324
  11.7 8.8 %copy-start.4 = (f32[60,60]{1,0:T(8,128)S(1)}, f32[60,60]{1,0:T(8,128)}, u32[]{:S(2)}) copy-start(f32[60,60]{1,0:T(8,128)} %k_shear.1) | copy-start | bytes 43204
  11.7 8.8 %copy-start.5 = (f32[60,60]{1,0:T(8,128)S(1)}, f32[60,60]{1,0:T(8,128)}, u32[]{:S(2)}) copy-start(f32[60,60]{1,0:T(8,128)} %k_bulk.1) | copy-start | bytes 43204
  11.7 8.8 %copy-start.6 = (f32[768]{0:T(1024)S(1)}, f32[768]{0:T(1024)}, u32[]{:S(2)}) copy-start(f32[768]{0:T(1024)} %shear.1) | copy-start | bytes 9220
  11.7 8.8 %copy-start.7 = (f32[768]{0:T(1024)S(1)}, f32[768]{0:T(1024)}, u32[]{:S(2)}) copy-start(f32[768]{0:T(1024)} %bulk.1) | copy-start | bytes 9220
  11.7 17.8 %all-to-all-start = ((f32[64,1,768]{2,1,0:T(1,128)}), f32[64,1,768]{2,1,0:T(1,128)S(1)}, u32[]{:S(2)}, u32[]{:S(2)}) async-start(f32[64,1,768]{2,1,0:T(1,128)} %get-tuple-element.18), calls=%async_computation | async-start | bytes 393216 | tf_op jit(solution)/shard_map/all_to_all | solution.py:452
  20.6 9.0 %copy-start = (s32[8,2048]{1,0:T(8,128)S(1)}, s32[8,2048]{1,0:T(8,128)}, u32[]{:S(2)}) copy-start(s32[8,2048]{1,0:T(8,128)} %faces.1) | copy-start | bytes 196612
  32.3 17.5 %all-to-all-start.1 = ((f32[64,1,256]{2,1,0:T(1,128)}), f32[64,1,256]{2,1,0:T(1,128)S(1)}, u32[]{:S(2)}, u32[]{:S(2)}) async-start(f32[64,1,256]{2,1,0:T(1,128)} %get-tuple-element.24), calls=%async_computation.1 | async-start | bytes 131072 | tf_op jit(solution)/shard_map/all_to_all | solution.py:460
  42.4 4.8 %collective-permute-start.2 = (f32[24,256]{1,0:T(8,128)S(1)}, f32[24,256]{1,0:T(8,128)S(1)}, u32[]{:S(2)}, u32[]{:S(2)}) collective-permute-start(f32[24,256]{1,0:T(8,128)S(1)} %get-tuple-element.29), channel_id=1, source_target_pairs={{0,4},{4,0},{8,12},{12,8},{16,20},{20,16},{24,28},{28,24},{32,36},... | collective-permute-start | bytes 73736 | tf_op jit(solution)/shard_map/ppermute | solution.py:461
  42.6 7.2 %collective-permute-start.3 = (f32[24,256]{1,0:T(8,128)S(1)}, f32[24,256]{1,0:T(8,128)S(1)}, u32[]{:S(2)}, u32[]{:S(2)}) collective-permute-start(f32[24,256]{1,0:T(8,128)S(1)} %get-tuple-element.30), channel_id=1, source_target_pairs={{0,0},{4,8},{8,4},{12,16},{16,12},{20,24},{24,20},{28,32},{32,28},... | collective-permute-start | bytes 73736 | tf_op jit(solution)/shard_map/ppermute | solution.py:462
  45.6 4.2 %copy-start.1 = (s32[8,256]{1,0:T(8,128)S(1)}, s32[8,256]{1,0:T(8,128)}, u32[]{:S(2)}) copy-start(s32[8,256]{1,0:T(8,128)} %slave.1) | copy-start | bytes 24580
  45.6 4.2 %copy-start.2 = (f32[8,256]{1,0:T(8,128)S(1)}, f32[8,256]{1,0:T(8,128)}, u32[]{:S(2)}) copy-start(f32[8,256]{1,0:T(8,128)} %dual.1) | copy-start | bytes 24580
  51.0 5.7 %collective-permute-start.4 = (f32[48,256]{1,0:T(8,128)S(1)}, f32[48,256]{1,0:T(8,128)S(1)}, u32[]{:S(2)}, u32[]{:S(2)}) collective-permute-start(f32[48,256]{1,0:T(8,128)S(1)} %get-tuple-element.33), channel_id=1, source_target_pairs={{0,1},{1,2},{2,3},{3,0},{4,5},{5,6},{6,7},{7,4},{8,9},{9,10},{10,1... | collective-permute-start | bytes 147464 | tf_op jit(solution)/shard_map/ppermute | solution.py:471
  52.6 5.6 %collective-permute-start.5 = (f32[48,256]{1,0:T(8,128)S(1)}, f32[48,256]{1,0:T(8,128)S(1)}, u32[]{:S(2)}, u32[]{:S(2)}) collective-permute-start(f32[48,256]{1,0:T(8,128)S(1)} %get-tuple-element.32), channel_id=1, source_target_pairs={{0,2},{1,3},{2,0},{3,1},{4,6},{5,7},{6,4},{7,5},{8,10},{9,11},{10,... | collective-permute-start | bytes 147464 | tf_op jit(solution)/shard_map/ppermute | solution.py:471
  55.4 4.1 %collective-permute-start.6 = (f32[48,256]{1,0:T(8,128)S(1)}, f32[48,256]{1,0:T(8,128)S(1)}, u32[]{:S(2)}, u32[]{:S(2)}) collective-permute-start(f32[48,256]{1,0:T(8,128)S(1)} %get-tuple-element.31), channel_id=1, source_target_pairs={{0,3},{1,0},{2,1},{3,2},{4,7},{5,4},{6,5},{7,6},{8,11},{9,8},{10,9... | collective-permute-start | bytes 147464 | tf_op jit(solution)/shard_map/ppermute | solution.py:471

commit v5 on v4

--- a/solution.py
+++ b/solution.py
@@ -82,8 +82,8 @@
 
 
 def element_kernel(
-    own, near, far, connect, shear, bulk, k_shear, k_bulk,
-    owned, near_out, far_out, table, dofs, k_pad, hots, total,
+    own, far, near, connect, shear, bulk, k_shear, k_bulk,
+    owned, far_out, near_out, table, dofs, k_pad, hots, total,
 ):
     ghost = near.shape[0] // 3
     count = own.shape[0] // 3
@@ -139,7 +139,7 @@
 
 
 def pack_kernel(*refs):
-    given, (count, out, slot_out, table, near, far, rows) = refs[:6], refs[6:13]
+    given, (count, out, slot_out, table, far, near, rows) = refs[:6], refs[6:13]
     held, sems = refs[13:19], refs[19]
     copies = [pltpu.make_async_copy(a, b, sems.at[i]) for i, (a, b) in enumerate(zip(given, held))]
     for copy in copies:
@@ -196,10 +196,9 @@
     p1 = payload.astype(BF16)
     rest = payload - p1.astype(F32)
     p2 = rest.astype(BF16)
-    p3 = (rest - p2.astype(F32)).astype(BF16)
     placed = lax.dot_general(
-        jnp.concatenate([place, place, place], axis=1),
-        jnp.concatenate([p1, p2, p3], axis=1),
+        jnp.concatenate([place, place], axis=1),
+        jnp.concatenate([p1, p2], axis=1),
         (((1,), (1,)), ((), ())),
         preferred_element_type=F32,
     )
@@ -258,7 +257,7 @@
     out[...] = total
 
 
-def slave_kernel(returned, slot, dual, slave, owned, master, near, far, out):
+def slave_kernel(returned, slot, dual, slave, owned, master, far, near, out):
     lower, upper = by_side(near[...], far[...])
     own = owned.shape[0] // 3
     ghost = near.shape[0] // 3
@@ -268,13 +267,12 @@
     m1 = mult_rows.astype(BF16)
     rest = mult_rows - m1.astype(F32)
     m2 = rest.astype(BF16)
-    m3 = (rest - m2.astype(F32)).astype(BF16)
     hot = jnp.where(
         lax.broadcasted_iota(jnp.int32, (n_dom, segs), 0) == slot[0:1, :], 1.0, 0.0
     ).astype(BF16)
     picked = jnp.dot(
-        jnp.concatenate([m1, m2, m3], axis=1),
-        jnp.concatenate([hot, hot, hot], axis=0),
+        jnp.concatenate([m1, m2], axis=1),
+        jnp.concatenate([hot, hot], axis=0),
         preferred_element_type=F32,
     )
     rank = slot[1:2, :]
@@ -343,8 +341,8 @@
         element_kernel,
         [shape(table.shape[0], LO), shape(*near.shape), shape(*far.shape)],
         table,
+        far,
         near,
-        far,
         connect,
         shear,
         bulk,
@@ -421,8 +419,8 @@
         seg_slave,
         owned,
         master_part,
+        far,
         near,
-        far,
     )
 
 
@@ -446,20 +444,20 @@
     group = sorted(range(n_dom), key=lambda part: place_in_group(part, n_dom))
     near_pairs = [(i, i ^ 1) for i in range(n_dom)]
     far_pairs = [(i, min(max(((i + 1) ^ 1) - 1, 0), n_dom - 1)) for i in range(n_dom)]
-    outgoing, slot, table, near, far = pack(
+    outgoing, slot, table, far, near = pack(
         displacement, seg_slave, dual, mortar, seg_face, seg_part, seg_count, n_dom
     )
     incoming = lax.all_to_all(outgoing, "dom", 0, 0, axis_index_groups=[group], tiled=True)
+    far = lax.ppermute(far, "dom", far_pairs)
     near = lax.ppermute(near, "dom", near_pairs)
-    far = lax.ppermute(far, "dom", far_pairs)
-    owned, near, far = elements(
+    owned, far, near = elements(
         table, near, far, connect, shear, bulk, stiff_shear, stiff_bulk
     )
     incoming, owned = lax.optimization_barrier((incoming, owned))
     mult, master_force, master_nodes = master(incoming, table, face_nodes)
     returned = lax.all_to_all(mult, "dom", 0, 0, axis_index_groups=[group], tiled=True)
+    far = lax.ppermute(far, "dom", far_pairs)
     near = lax.ppermute(near, "dom", near_pairs)
-    far = lax.ppermute(far, "dom", far_pairs)
     master_part = call(
         master_scatter_kernel, shape(3 * nodes // LO, LO), master_force, master_nodes
     )

time: 60.4 us -> 60.4 us (level)
  starting transfers between devices: 35.5 us -> 36.4 us
  waiting for transfers between devices: 5.31 us -> 4.68 us
    ppermute x2, starting transfers between devices: 10.8 us -> 9.57 us  [on_device(): far = lax.ppermute(far, 'dom', far_pairs)]
    ppermute x2, starting transfers between devices: 0.26 us -> 1.36 us  [on_device(): near = lax.ppermute(near, 'dom', near_pairs)]
    all_to_all x1, starting transfers between devices: 8.75 us -> 9.73 us  [on_device(): lax.all_to_all(outgoing, 'dom', 0, 0, axis_index_groups=[group], tiled=True)]
    ppermute x2, waiting for transfers between devices: 2.63 us -> 2 us  [on_device(): far = lax.ppermute(far, 'dom', far_pairs)]
where the time goes in v5:
time: 60.4 us; the launch traced here: 60.1 us
  starting transfers between devices  36.4 us (60%)
  Pallas kernels  18.1 us (30%)
  waiting for transfers between devices  4.68 us (8%)
  between operations  0.87 us (1%)
    pallas_call x6, Pallas kernels, call(): pl.pallas_call(kernel, out_shape=outs, in_specs=specs, out_specs=[pl.Bloc...  18.1 us
    all_to_all x1, starting transfers between devices, on_device(): lax.all_to_all(mult, 'dom', 0, 0, axis_index_groups=[group], tiled=True)  10.1 us
    all_to_all x1, starting transfers between devices, on_device(): lax.all_to_all(outgoing, 'dom', 0, 0, axis_index_groups=[group], tiled=True)  9.73 us
    ppermute x2, starting transfers between devices, on_device(): far = lax.ppermute(far, 'dom', far_pairs)  9.57 us
    ppermute x3, starting transfers between devices, on_device(): lax.ppermute(lax.dynamic_index_in_dim(blocks, (me + k) % n_sub, 0, keepdi...  5.73 us
    ppermute x3, waiting for transfers between devices, on_device(): lax.ppermute(lax.dynamic_index_in_dim(blocks, (me + k) % n_sub, 0, keepdi...  2.67 us
    ppermute x2, waiting for transfers between devices, on_device(): far = lax.ppermute(far, 'dom', far_pairs)  2 us
    ppermute x2, starting transfers between devices, on_device(): near = lax.ppermute(near, 'dom', near_pairs)  1.36 us
  transfers between devices with their start and end apart: 9, of which 3 were waited for; matrix products, arithmetic and copies ran while one was open for 0% of the time, Pallas kernels for 17%

profile of v5, /device:TPU:8, one launch (start us, length us, event | category | flops | bytes accessed | tf_op | source)
XLA Modules:
  0.0 60.1 jit_solution(776141352076708905)
XLA Ops:
  0.7 3.0 %shard_map.127 = (f32[64,1,768]{2,1,0:T(1,128)}, s32[2,256]{1,0:T(2,128)S(1)}, bf16[192,512]{1,0:T(8,128)(2,1)S(1)}, f32[24,256]{1,0:T(8,128)S(1)}, f32[24,256]{1,0:T(8,128)S(1)}) custom-call(f32[3,16384]{1,0:T(4,128)} %refs_0_.1, s32[8,256]{1,0:T(8,128)} %slave.1, f32[8,256]{1,0:T(8,128)} %dual.1, f32[64,256]{1,0:T(8,128)} %refs_3_.1, s32[1,256]{1,0:T(1,128)} %bitcast.12, ...), custom_call_target="tpu_custom_call" | custom-call | flops 100000000 | bytes 280580 | tf_op jit(solution)/shard_map/pallas_call | solution.py:320
  3.7 7.1 %collective-permute-start = (f32[24,256]{1,0:T(8,128)S(1)}, f32[24,256]{1,0:T(8,128)S(1)}, u32[]{:S(2)}, u32[]{:S(2)}) collective-permute-start(f32[24,256]{1,0:T(8,128)S(1)} %get-tuple-element.20), channel_id=1, source_target_pairs={{0,0},{4,8},{8,4},{12,16},{16,12},{20,24},{24,20},{28,32},{32,28},... | collective-permute-start | bytes 73736 | tf_op jit(solution)/shard_map/ppermute | solution.py:451
  10.8 0.1 collective-permute-start.1
  10.9 0.0 copy-start.3
  10.9 0.0 copy-start.4
  10.9 0.0 copy-start.5
  10.9 0.0 copy-start.6
  10.9 0.0 copy-start.7
  11.0 9.7 %all-to-all-start = ((f32[64,1,768]{2,1,0:T(1,128)}), f32[64,1,768]{2,1,0:T(1,128)S(1)}, u32[]{:S(2)}, u32[]{:S(2)}) async-start(f32[64,1,768]{2,1,0:T(1,128)} %get-tuple-element.18), calls=%async_computation | async-start | bytes 393216 | tf_op jit(solution)/shard_map/all_to_all | solution.py:450
  20.7 0.0 collective-permute-done.far
  20.7 0.0 collective-permute-done.1.near
  20.7 0.0 copy-done.3
  20.7 0.0 copy-done.4
  20.7 0.0 copy-done.5
  20.7 0.0 copy-done.6
  20.8 0.0 copy-done.7
  20.8 0.0 copy-start
  20.8 9.0 %shard_map.128 = (f32[192,256]{1,0:T(8,128)S(1)}, f32[24,256]{1,0:T(8,128)S(1)}, f32[24,256]{1,0:T(8,128)S(1)}) custom-call(bf16[192,512]{1,0:T(8,128)(2,1)S(1)} %get-tuple-element.19.own.table, f32[24,256]{1,0:T(8,128)S(1)} %collective-permute-done.far, f32[24,256]{1,0:T(8,128)S(1)} %collective-permute-done.1.near, s32[20,768]{1,0:T(8,128)S(1)} %copy-done.3, ...), custom_call_target="tpu_custom_call" | custom-call | flops 8000000000 | bytes 538752 | tf_op jit(solution)/shard_map/pallas_call | solution.py:320
  29.7 0.0 all-to-all-done.incoming
  29.7 0.0 copy-done
  29.8 2.8 %shard_map.129 = (f32[64,1,256]{2,1,0:T(1,128)}, f32[24,512]{1,0:T(8,128)S(1)}, s32[8,512]{1,0:T(8,128)S(1)}) custom-call(f32[64,1,768]{2,1,0:T(1,128)S(1)} %all-to-all-done.incoming, bf16[192,512]{1,0:T(8,128)(2,1)S(1)} %get-tuple-element.19.own.table, s32[8,2048]{1,0:T(8,128)S(1)} %copy-done), custom_call_target="tpu_custom_call" | custom-call | flops 100000000 | bytes 655360 | tf_op jit(solution)/shard_map/pallas_call | solution.py:320
  32.5 10.1 %all-to-all-start.1 = ((f32[64,1,256]{2,1,0:T(1,128)}), f32[64,1,256]{2,1,0:T(1,128)S(1)}, u32[]{:S(2)}, u32[]{:S(2)}) async-start(f32[64,1,256]{2,1,0:T(1,128)} %get-tuple-element.24), calls=%async_computation.1 | async-start | bytes 131072 | tf_op jit(solution)/shard_map/all_to_all | solution.py:458
  42.6 2.5 %collective-permute-start.2 = (f32[24,256]{1,0:T(8,128)S(1)}, f32[24,256]{1,0:T(8,128)S(1)}, u32[]{:S(2)}, u32[]{:S(2)}) collective-permute-start(f32[24,256]{1,0:T(8,128)S(1)} %get-tuple-element.29), channel_id=1, source_target_pairs={{0,0},{4,8},{8,4},{12,16},{16,12},{20,24},{24,20},{28,32},{32,28},... | collective-permute-start | bytes 73736 | tf_op jit(solution)/shard_map/ppermute | solution.py:459
  45.1 1.3 %collective-permute-start.3 = (f32[24,256]{1,0:T(8,128)S(1)}, f32[24,256]{1,0:T(8,128)S(1)}, u32[]{:S(2)}, u32[]{:S(2)}) collective-permute-start(f32[24,256]{1,0:T(8,128)S(1)} %get-tuple-element.30), channel_id=1, source_target_pairs={{0,4},{4,0},{8,12},{12,8},{16,20},{20,16},{24,28},{28,24},{32,36},... | collective-permute-start | bytes 73736 | tf_op jit(solution)/shard_map/ppermute | solution.py:460
  46.3 0.0 copy-start.1
  46.3 0.0 copy-start.2
  46.3 1.5 %shard_map.130.master = f32[192,256]{1,0:T(8,128)S(1)} custom-call(f32[24,512]{1,0:T(8,128)S(1)} %get-tuple-element.27.force, s32[8,512]{1,0:T(8,128)S(1)} %get-tuple-element.28.nodes), custom_call_target="tpu_custom_call" | custom-call | flops 100000000 | bytes 65536 | tf_op jit(solution)/shard_map/pallas_call | solution.py:320
  47.8 2.0 %collective-permute-done.2.far = f32[24,256]{1,0:T(8,128)S(1)} collective-permute-done((f32[24,256]{1,0:T(8,128)S(1)}, f32[24,256]{1,0:T(8,128)S(1)}, u32[]{:S(2)}, u32[]{:S(2)}) %collective-permute-start.2) | collective-permute-done | bytes 24608 | tf_op jit(solution)/shard_map/ppermute | solution.py:459
  49.8 0.0 collective-permute-done.3.near
  49.8 0.0 all-to-all-done.1.returned
  49.8 0.0 copy-done.1
  49.9 0.0 copy-done.2
  49.9 1.2 %shard_map.131 = f32[4,48,256]{2,1,0:T(8,128)S(1)} custom-call(f32[64,1,256]{2,1,0:T(1,128)S(1)} %all-to-all-done.1.returned, s32[2,256]{1,0:T(2,128)S(1)} %get-tuple-element.25.slot, f32[8,256]{1,0:T(8,128)S(1)} %copy-done.2, s32[8,256]{1,0:T(8,128)S(1)} %copy-done.1, f32[192,256]{1,0:T(8,128)S(1)} %get-tuple-element.26.owned, ...), custom_call_target="tpu_custom_call" | custom-call | flops 100000000 | bytes 526336 | tf_op jit(solution)/shard_map/pallas_call | solution.py:320
  51.1 1.6 %collective-permute-start.4 = (f32[48,256]{1,0:T(8,128)S(1)}, f32[48,256]{1,0:T(8,128)S(1)}, u32[]{:S(2)}, u32[]{:S(2)}) collective-permute-start(f32[48,256]{1,0:T(8,128)S(1)} %get-tuple-element.33), channel_id=1, source_target_pairs={{0,1},{1,2},{2,3},{3,0},{4,5},{5,6},{6,7},{7,4},{8,9},{9,10},{10,1... | collective-permute-start | bytes 147464 | tf_op jit(solution)/shard_map/ppermute | solution.py:469
  52.6 2.7 %collective-permute-start.5 = (f32[48,256]{1,0:T(8,128)S(1)}, f32[48,256]{1,0:T(8,128)S(1)}, u32[]{:S(2)}, u32[]{:S(2)}) collective-permute-start(f32[48,256]{1,0:T(8,128)S(1)} %get-tuple-element.32), channel_id=1, source_target_pairs={{0,2},{1,3},{2,0},{3,1},{4,6},{5,7},{6,4},{7,5},{8,10},{9,11},{10,... | collective-permute-start | bytes 147464 | tf_op jit(solution)/shard_map/ppermute | solution.py:469
  55.4 1.4 %collective-permute-start.6 = (f32[48,256]{1,0:T(8,128)S(1)}, f32[48,256]{1,0:T(8,128)S(1)}, u32[]{:S(2)}, u32[]{:S(2)}) collective-permute-start(f32[48,256]{1,0:T(8,128)S(1)} %get-tuple-element.31), channel_id=1, source_target_pairs={{0,3},{1,0},{2,1},{3,2},{4,7},{5,4},{6,5},{7,6},{8,11},{9,8},{10,9... | collective-permute-start | bytes 147464 | tf_op jit(solution)/shard_map/ppermute | solution.py:469
  56.8 0.0 collective-permute-done.4.a
  56.8 1.4 %collective-permute-done.5.b = f32[48,256]{1,0:T(8,128)S(1)} collective-permute-done((f32[48,256]{1,0:T(8,128)S(1)}, f32[48,256]{1,0:T(8,128)S(1)}, u32[]{:S(2)}, u32[]{:S(2)}) %collective-permute-start.5) | collective-permute-done | bytes 49184 | tf_op jit(solution)/shard_map/ppermute | solution.py:469
  58.2 1.2 %collective-permute-done.6.d = f32[48,256]{1,0:T(8,128)S(1)} collective-permute-done((f32[48,256]{1,0:T(8,128)S(1)}, f32[48,256]{1,0:T(8,128)S(1)}, u32[]{:S(2)}, u32[]{:S(2)}) %collective-permute-start.6) | collective-permute-done | bytes 49184 | tf_op jit(solution)/shard_map/ppermute | solution.py:469
  59.5 0.7 %shard_map.132 = f32[3,4096]{1,0:T(4,128)} custom-call(f32[48,256]{1,0:T(8,128)S(1)} %get-tuple-element.34.own_part, f32[48,256]{1,0:T(8,128)S(1)} %collective-permute-done.4.a, f32[48,256]{1,0:T(8,128)S(1)} %collective-permute-done.5.b, f32[48,256]{1,0:T(8,128)S(1)} %collective-permute-done.6.d), custom_call_target="tpu_custom_call" | custom-call | flops 100000000 | bytes 196608 | tf_op jit(solution)/shard_map/pallas_call | solution.py:320
  (1 shorter events, 0.0 us)
Async XLA Ops:
  3.7 17.0 %collective-permute-start = (f32[24,256]{1,0:T(8,128)S(1)}, f32[24,256]{1,0:T(8,128)S(1)}, u32[]{:S(2)}, u32[]{:S(2)}) collective-permute-start(f32[24,256]{1,0:T(8,128)S(1)} %get-tuple-element.20), channel_id=1, source_target_pairs={{0,0},{4,8},{8,4},{12,16},{16,12},{20,24},{24,20},{28,32},{32,28},... | collective-permute-start | bytes 73736 | tf_op jit(solution)/shard_map/ppermute | solution.py:451
  10.8 9.9 %collective-permute-start.1 = (f32[24,256]{1,0:T(8,128)S(1)}, f32[24,256]{1,0:T(8,128)S(1)}, u32[]{:S(2)}, u32[]{:S(2)}) collective-permute-start(f32[24,256]{1,0:T(8,128)S(1)} %get-tuple-element.21), channel_id=1, source_target_pairs={{0,4},{4,0},{8,12},{12,8},{16,20},{20,16},{24,28},{28,24},{32,36},... | collective-permute-start | bytes 73736 | tf_op jit(solution)/shard_map/ppermute | solution.py:452
  10.9 9.8 %copy-start.3 = (s32[20,768]{1,0:T(8,128)S(1)}, s32[20,768]{1,0:T(8,128)}, u32[]{:S(2)}) copy-start(s32[20,768]{1,0:T(8,128)} %connect.1) | copy-start | bytes 184324
  10.9 9.8 %copy-start.4 = (f32[60,60]{1,0:T(8,128)S(1)}, f32[60,60]{1,0:T(8,128)}, u32[]{:S(2)}) copy-start(f32[60,60]{1,0:T(8,128)} %k_shear.1) | copy-start | bytes 43204
  10.9 9.8 %copy-start.5 = (f32[60,60]{1,0:T(8,128)S(1)}, f32[60,60]{1,0:T(8,128)}, u32[]{:S(2)}) copy-start(f32[60,60]{1,0:T(8,128)} %k_bulk.1) | copy-start | bytes 43204
  10.9 9.8 %copy-start.6 = (f32[768]{0:T(1024)S(1)}, f32[768]{0:T(1024)}, u32[]{:S(2)}) copy-start(f32[768]{0:T(1024)} %shear.1) | copy-start | bytes 9220
  10.9 9.8 %copy-start.7 = (f32[768]{0:T(1024)S(1)}, f32[768]{0:T(1024)}, u32[]{:S(2)}) copy-start(f32[768]{0:T(1024)} %bulk.1) | copy-start | bytes 9220
  11.0 18.8 %all-to-all-start = ((f32[64,1,768]{2,1,0:T(1,128)}), f32[64,1,768]{2,1,0:T(1,128)S(1)}, u32[]{:S(2)}, u32[]{:S(2)}) async-start(f32[64,1,768]{2,1,0:T(1,128)} %get-tuple-element.18), calls=%async_computation | async-start | bytes 393216 | tf_op jit(solution)/shard_map/all_to_all | solution.py:450
  20.8 9.0 %copy-start = (s32[8,2048]{1,0:T(8,128)S(1)}, s32[8,2048]{1,0:T(8,128)}, u32[]{:S(2)}) copy-start(s32[8,2048]{1,0:T(8,128)} %faces.1) | copy-start | bytes 196612
  32.5 17.3 %all-to-all-start.1 = ((f32[64,1,256]{2,1,0:T(1,128)}), f32[64,1,256]{2,1,0:T(1,128)S(1)}, u32[]{:S(2)}, u32[]{:S(2)}) async-start(f32[64,1,256]{2,1,0:T(1,128)} %get-tuple-element.24), calls=%async_computation.1 | async-start | bytes 131072 | tf_op jit(solution)/shard_map/all_to_all | solution.py:458
  42.6 7.3 %collective-permute-start.2 = (f32[24,256]{1,0:T(8,128)S(1)}, f32[24,256]{1,0:T(8,128)S(1)}, u32[]{:S(2)}, u32[]{:S(2)}) collective-permute-start(f32[24,256]{1,0:T(8,128)S(1)} %get-tuple-element.29), channel_id=1, source_target_pairs={{0,0},{4,8},{8,4},{12,16},{16,12},{20,24},{24,20},{28,32},{32,28},... | collective-permute-start | bytes 73736 | tf_op jit(solution)/shard_map/ppermute | solution.py:459
  45.1 4.8 %collective-permute-start.3 = (f32[24,256]{1,0:T(8,128)S(1)}, f32[24,256]{1,0:T(8,128)S(1)}, u32[]{:S(2)}, u32[]{:S(2)}) collective-permute-start(f32[24,256]{1,0:T(8,128)S(1)} %get-tuple-element.30), channel_id=1, source_target_pairs={{0,4},{4,0},{8,12},{12,8},{16,20},{20,16},{24,28},{28,24},{32,36},... | collective-permute-start | bytes 73736 | tf_op jit(solution)/shard_map/ppermute | solution.py:460
  46.3 3.5 %copy-start.1 = (s32[8,256]{1,0:T(8,128)S(1)}, s32[8,256]{1,0:T(8,128)}, u32[]{:S(2)}) copy-start(s32[8,256]{1,0:T(8,128)} %slave.1) | copy-start | bytes 24580
  46.3 3.5 %copy-start.2 = (f32[8,256]{1,0:T(8,128)S(1)}, f32[8,256]{1,0:T(8,128)}, u32[]{:S(2)}) copy-start(f32[8,256]{1,0:T(8,128)} %dual.1) | copy-start | bytes 24580
  51.1 5.7 %collective-permute-start.4 = (f32[48,256]{1,0:T(8,128)S(1)}, f32[48,256]{1,0:T(8,128)S(1)}, u32[]{:S(2)}, u32[]{:S(2)}) collective-permute-start(f32[48,256]{1,0:T(8,128)S(1)} %get-tuple-element.33), channel_id=1, source_target_pairs={{0,1},{1,2},{2,3},{3,0},{4,5},{5,6},{6,7},{7,4},{8,9},{9,10},{10,1... | collective-permute-start | bytes 147464 | tf_op jit(solution)/shard_map/ppermute | solution.py:469
  52.6 5.6 %collective-permute-start.5 = (f32[48,256]{1,0:T(8,128)S(1)}, f32[48,256]{1,0:T(8,128)S(1)}, u32[]{:S(2)}, u32[]{:S(2)}) collective-permute-start(f32[48,256]{1,0:T(8,128)S(1)} %get-tuple-element.32), channel_id=1, source_target_pairs={{0,2},{1,3},{2,0},{3,1},{4,6},{5,7},{6,4},{7,5},{8,10},{9,11},{10,... | collective-permute-start | bytes 147464 | tf_op jit(solution)/shard_map/ppermute | solution.py:469
  55.4 4.1 %collective-permute-start.6 = (f32[48,256]{1,0:T(8,128)S(1)}, f32[48,256]{1,0:T(8,128)S(1)}, u32[]{:S(2)}, u32[]{:S(2)}) collective-permute-start(f32[48,256]{1,0:T(8,128)S(1)} %get-tuple-element.31), channel_id=1, source_target_pairs={{0,3},{1,0},{2,1},{3,2},{4,7},{5,4},{6,5},{7,6},{8,11},{9,8},{10,9... | collective-permute-start | bytes 147464 | tf_op jit(solution)/shard_map/ppermute | solution.py:469

commit v6 on v3

--- a/solution.py
+++ b/solution.py
@@ -87,6 +87,7 @@
     ghost = near.shape[0] // 3
     count = own.shape[0] // 3
     rows = count + 2 * ghost
+    elems = connect.shape[1]
     for source, first_row in zip(by_side(near[...], far[...]), (0, rows - ghost)):
         first, second = pieces(source)
         for c in range(3):
@@ -113,7 +114,8 @@
         wide = jnp.concatenate([k_first, k_second, k_first, k_second], axis=1)
         return jnp.dot(wide, g, preferred_element_type=F32)
 
-    dofs[...] = shear[...] * product(k_shear) + bulk[...] * product(k_bulk)
+    by_shear, by_bulk = (m[...].reshape(1, elems) for m in (shear, bulk))
+    dofs[...] = by_shear * product(k_shear) + by_bulk * product(k_bulk)
     total[...] = jnp.zeros_like(total)
     for a in range(20):
         values = [dofs[20 * c + a : 20 * c + a + 1, :] for c in range(3)]
@@ -127,6 +129,12 @@
         near_out[here, :] = jnp.where(even, high, low)
         far_out[here, :] = jnp.where(even, low, high)
         owned[c * count : (c + 1) * count, :] = total[base + ghost : base + ghost + count, :]
+
+
+def place_in_group(part, n_dom):
+    ny, nz = 4, n_dom // 8
+    y, z, core = part // (2 * nz), (part // 2) % nz, part % 2
+    return n_dom - 1 - (z * (2 * ny) + y * 2 + core)
 
 
 def pack_kernel(*refs):
@@ -177,7 +185,7 @@
         hits_b, jnp.where(earlier, 1.0, 0.0).astype(BF16), preferred_element_type=F32
     )
     rank = jnp.sum(jnp.where(hits, before, 0.0), axis=0, keepdims=True).astype(jnp.int32)
-    slot = part[...] * cap + rank
+    slot = place_in_group(part[...], n_dom) * cap + rank
     slot_out[...] = slot
     place = jnp.where(
         lax.broadcasted_iota(jnp.int32, (width, segs), 0) == slot, 1.0, 0.0
@@ -332,8 +340,8 @@
         near,
         far,
         connect,
-        shear[None],
-        bulk[None],
+        shear,
+        bulk,
         k_shear,
         k_bulk,
         scratch=[
@@ -429,13 +437,14 @@
 ):
     nodes = displacement.shape[1]
     n_dom, n_sub = lax.axis_size("dom"), lax.axis_size("sub")
+    group = sorted(range(n_dom), key=lambda part: place_in_group(part, n_dom))
     near_pairs = [(i, i ^ 1) for i in range(n_dom)]
     far_pairs = [(i, min(max(((i + 1) ^ 1) - 1, 0), n_dom - 1)) for i in range(n_dom)]
     outgoing, slot, table, near, far = pack(
         displacement, seg_slave, dual, mortar, seg_face, seg_part, seg_count, n_dom
     )
     incoming = lax.all_to_all(
-        outgoing.reshape(n_dom, 8, 128), "dom", split_axis=0, concat_axis=0, tiled=True
+        outgoing.reshape(n_dom, 8, 128), "dom", 0, 0, axis_index_groups=[group], tiled=True
     )
     near = lax.ppermute(near, "dom", near_pairs)
     far = lax.ppermute(far, "dom", far_pairs)
@@ -446,7 +455,7 @@
     mult, master_force, master_nodes = master(
         incoming.reshape(n_dom * 8, 128), table, face_nodes
     )
-    returned = lax.all_to_all(mult, "dom", split_axis=0, concat_axis=0, tiled=True)
+    returned = lax.all_to_all(mult, "dom", 0, 0, axis_index_groups=[group], tiled=True)
     near = lax.ppermute(near, "dom", near_pairs)
     far = lax.ppermute(far, "dom", far_pairs)
     master_part = call(

time: 61.4 us -> 59.9 us (0.976); the launches traced: 60.3 us -> 59.6 us
  waiting for transfers between devices: 6.73 us -> 5.3 us
  starting transfers between devices: 34.2 us -> 35.5 us
  local copies, waits for them, and re-layouts: 0.74 us -> 0.07 us
    all_to_all x2, waiting for transfers between devices: 3.13 us -> 0.01 us  [the longest x1 0.01 us: on_device(): lax.all_to_all(mult, 'dom', 0, 0, axis_index_groups=[group], tiled=True)]
    all_to_all x2, starting transfers between devices: 15.7 us -> 18.8 us  [the longest x1 10.1 us: on_device(): lax.all_to_all(mult, 'dom', 0, 0, axis_index_groups=[group], tiled=True)]
    ppermute x2, starting transfers between devices: 12.5 us -> 10.8 us  [on_device(): far = lax.ppermute(far, 'dom', far_pairs)]
    ppermute x2, waiting for transfers between devices: 0.93 us -> 2.63 us  [on_device(): far = lax.ppermute(far, 'dom', far_pairs)]
    unnamed x16, local copies, waits for them, and re-layouts: 0.71 us -> 0.05 us
  transfers between devices with their start and end apart: 9 -> 9, of which waited for: 5 -> 3; matrix products, arithmetic and copies ran while one was open for 0% -> 0% of each run, Pallas kernels for 17% -> 18%
where the time goes in v6:
time: 59.9 us; the launch traced here: 59.6 us
  starting transfers between devices  35.5 us (59%)
  Pallas kernels  17.7 us (30%)
  waiting for transfers between devices  5.3 us (9%)
  between operations  0.92 us (2%)
    pallas_call x6, Pallas kernels, call(): pl.pallas_call(kernel, out_shape=outs, in_specs=specs, out_specs=[pl.Bloc...  17.7 us
    ppermute x2, starting transfers between devices, on_device(): far = lax.ppermute(far, 'dom', far_pairs)  10.8 us
    all_to_all x1, starting transfers between devices, on_device(): lax.all_to_all(mult, 'dom', 0, 0, axis_index_groups=[group], tiled=True)  10.1 us
    all_to_all x1, starting transfers between devices, on_device(): lax.all_to_all(outgoing.reshape(n_dom, 8, 128), 'dom', 0, 0, axis_index_g...  8.75 us
    ppermute x3, starting transfers between devices, on_device(): lax.ppermute(lax.dynamic_index_in_dim(blocks, (me + k) % n_sub, 0, keepdi...  5.73 us
    ppermute x3, waiting for transfers between devices, on_device(): lax.ppermute(lax.dynamic_index_in_dim(blocks, (me + k) % n_sub, 0, keepdi...  2.66 us
    ppermute x2, waiting for transfers between devices, on_device(): far = lax.ppermute(far, 'dom', far_pairs)  2.63 us
  transfers between devices with their start and end apart: 9, of which 3 were waited for; matrix products, arithmetic and copies ran while one was open for 0% of the time, Pallas kernels for 18%

profile of v6, /device:TPU:8, one launch (start us, length us, event | category | flops | bytes accessed | tf_op | source)
XLA Modules:
  0.0 59.6 jit_solution(13847243713853901511)
XLA Ops:
  0.7 2.8 %shard_map.127 = (f32[512,128]{1,0:T(8,128)}, s32[1,256]{1,0:T(1,128)S(1)}, bf16[192,512]{1,0:T(8,128)(2,1)S(1)}, f32[24,256]{1,0:T(8,128)S(1)}, f32[24,256]{1,0:T(8,128)S(1)}) custom-call(f32[3,16384]{1,0:T(4,128)} %refs_0_.1, s32[8,256]{1,0:T(8,128)} %slave.1, f32[8,256]{1,0:T(8,128)} %dual.1, f32[64,256]{1,0:T(8,128)} %refs_3_.1, s32[1,256]{1,0:T(1,128)} %bitcast.15, ...), custom_call_target="tpu_custom_call" | custom-call | flops 100000000 | bytes 280580 | tf_op jit(solution)/shard_map/pallas_call | solution.py:316
  3.5 0.1 collective-permute-start
  3.6 7.7 %collective-permute-start.1 = (f32[24,256]{1,0:T(8,128)S(1)}, f32[24,256]{1,0:T(8,128)S(1)}, u32[]{:S(2)}, u32[]{:S(2)}) collective-permute-start(f32[24,256]{1,0:T(8,128)S(1)} %get-tuple-element.21), channel_id=1, source_target_pairs={{0,0},{4,8},{8,4},{12,16},{16,12},{20,24},{24,20},{28,32},{32,28},... | collective-permute-start | bytes 73736 | tf_op jit(solution)/shard_map/ppermute | solution.py:450
  11.3 0.0 copy-start.3
  11.3 0.0 copy-start.4
  11.3 0.0 copy-start.5
  11.3 0.0 copy-start.6
  11.3 0.0 copy-start.7
  11.3 8.7 %all-to-all-start = ((f32[64,8,128]{2,1,0:T(8,128)}), f32[64,8,128]{2,1,0:T(8,128)S(1)}, u32[]{:S(2)}, u32[]{:S(2)}) async-start(f32[64,8,128]{2,1,0:T(8,128)} %bitcast.3), calls=%async_computation | async-start | bytes 524288 | tf_op jit(solution)/shard_map/all_to_all | solution.py:446
  20.1 0.0 collective-permute-done.near
  20.1 0.0 collective-permute-done.1.far
  20.1 0.0 copy-done.3
  20.1 0.0 copy-done.4
  20.1 0.0 copy-done.5
  20.2 0.0 copy-done.6
  20.2 0.0 copy-done.7
  20.2 0.0 copy-start
  20.2 9.0 %shard_map.128 = (f32[192,256]{1,0:T(8,128)S(1)}, f32[24,256]{1,0:T(8,128)S(1)}, f32[24,256]{1,0:T(8,128)S(1)}) custom-call(bf16[192,512]{1,0:T(8,128)(2,1)S(1)} %get-tuple-element.19.own.table, f32[24,256]{1,0:T(8,128)S(1)} %collective-permute-done.near, f32[24,256]{1,0:T(8,128)S(1)} %collective-permute-done.1.far, s32[20,768]{1,0:T(8,128)S(1)} %copy-done.3, ...), custom_call_target="tpu_custom_call" | custom-call | flops 8000000000 | bytes 538752 | tf_op jit(solution)/shard_map/pallas_call | solution.py:316
  29.1 0.0 all-to-all-done
  29.2 0.0 copy-done
  29.2 2.6 %shard_map.129 = (f32[64,1,256]{2,1,0:T(1,128)}, f32[24,512]{1,0:T(8,128)S(1)}, s32[8,512]{1,0:T(8,128)S(1)}) custom-call(f32[512,128]{1,0:T(8,128)S(1)} %bitcast.14, bf16[192,512]{1,0:T(8,128)(2,1)S(1)} %get-tuple-element.19.own.table, s32[8,2048]{1,0:T(8,128)S(1)} %copy-done), custom_call_target="tpu_custom_call" | custom-call | flops 100000000 | bytes 720896 | tf_op jit(solution)/shard_map/pallas_call | solution.py:316
  31.8 10.1 %all-to-all-start.1 = ((f32[64,1,256]{2,1,0:T(1,128)}), f32[64,1,256]{2,1,0:T(1,128)S(1)}, u32[]{:S(2)}, u32[]{:S(2)}) async-start(f32[64,1,256]{2,1,0:T(1,128)} %get-tuple-element.24), calls=%async_computation.1 | async-start | bytes 131072 | tf_op jit(solution)/shard_map/all_to_all | solution.py:458
  41.8 0.2 collective-permute-start.2
  42.0 3.0 %collective-permute-start.3 = (f32[24,256]{1,0:T(8,128)S(1)}, f32[24,256]{1,0:T(8,128)S(1)}, u32[]{:S(2)}, u32[]{:S(2)}) collective-permute-start(f32[24,256]{1,0:T(8,128)S(1)} %get-tuple-element.30), channel_id=1, source_target_pairs={{0,0},{4,8},{8,4},{12,16},{16,12},{20,24},{24,20},{28,32},{32,28},... | collective-permute-start | bytes 73736 | tf_op jit(solution)/shard_map/ppermute | solution.py:460
  45.1 0.0 copy-start.1
  45.1 0.0 copy-start.2
  45.1 1.5 %shard_map.130.master = f32[192,256]{1,0:T(8,128)S(1)} custom-call(f32[24,512]{1,0:T(8,128)S(1)} %get-tuple-element.27.force, s32[8,512]{1,0:T(8,128)S(1)} %get-tuple-element.28.nodes), custom_call_target="tpu_custom_call" | custom-call | flops 100000000 | bytes 65536 | tf_op jit(solution)/shard_map/pallas_call | solution.py:316
  46.6 0.0 collective-permute-done.2.near
  46.6 2.6 %collective-permute-done.3.far = f32[24,256]{1,0:T(8,128)S(1)} collective-permute-done((f32[24,256]{1,0:T(8,128)S(1)}, f32[24,256]{1,0:T(8,128)S(1)}, u32[]{:S(2)}, u32[]{:S(2)}) %collective-permute-start.3) | collective-permute-done | bytes 24608 | tf_op jit(solution)/shard_map/ppermute | solution.py:460
  49.3 0.0 all-to-all-done.1.returned
  49.3 0.0 copy-done.1
  49.3 0.0 copy-done.2
  49.3 1.2 %shard_map.131 = f32[4,48,256]{2,1,0:T(8,128)S(1)} custom-call(f32[64,1,256]{2,1,0:T(1,128)S(1)} %all-to-all-done.1.returned, s32[1,256]{1,0:T(1,128)S(1)} %get-tuple-element.25.slot, f32[8,256]{1,0:T(8,128)S(1)} %copy-done.2, s32[8,256]{1,0:T(8,128)S(1)} %copy-done.1, f32[192,256]{1,0:T(8,128)S(1)} %get-tuple-element.26.owned, ...), custom_call_target="tpu_custom_call" | custom-call | flops 100000000 | bytes 525312 | tf_op jit(solution)/shard_map/pallas_call | solution.py:316
  50.5 1.6 %collective-permute-start.4 = (f32[48,256]{1,0:T(8,128)S(1)}, f32[48,256]{1,0:T(8,128)S(1)}, u32[]{:S(2)}, u32[]{:S(2)}) collective-permute-start(f32[48,256]{1,0:T(8,128)S(1)} %get-tuple-element.33), channel_id=1, source_target_pairs={{0,1},{1,2},{2,3},{3,0},{4,5},{5,6},{6,7},{7,4},{8,9},{9,10},{10,1... | collective-permute-start | bytes 147464 | tf_op jit(solution)/shard_map/ppermute | solution.py:469
  52.1 2.7 %collective-permute-start.5 = (f32[48,256]{1,0:T(8,128)S(1)}, f32[48,256]{1,0:T(8,128)S(1)}, u32[]{:S(2)}, u32[]{:S(2)}) collective-permute-start(f32[48,256]{1,0:T(8,128)S(1)} %get-tuple-element.32), channel_id=1, source_target_pairs={{0,2},{1,3},{2,0},{3,1},{4,6},{5,7},{6,4},{7,5},{8,10},{9,11},{10,... | collective-permute-start | bytes 147464 | tf_op jit(solution)/shard_map/ppermute | solution.py:469
  54.8 1.4 %collective-permute-start.6 = (f32[48,256]{1,0:T(8,128)S(1)}, f32[48,256]{1,0:T(8,128)S(1)}, u32[]{:S(2)}, u32[]{:S(2)}) collective-permute-start(f32[48,256]{1,0:T(8,128)S(1)} %get-tuple-element.31), channel_id=1, source_target_pairs={{0,3},{1,0},{2,1},{3,2},{4,7},{5,4},{6,5},{7,6},{8,11},{9,8},{10,9... | collective-permute-start | bytes 147464 | tf_op jit(solution)/shard_map/ppermute | solution.py:469
  56.2 0.0 collective-permute-done.4.a
  56.3 1.4 %collective-permute-done.5.b = f32[48,256]{1,0:T(8,128)S(1)} collective-permute-done((f32[48,256]{1,0:T(8,128)S(1)}, f32[48,256]{1,0:T(8,128)S(1)}, u32[]{:S(2)}, u32[]{:S(2)}) %collective-permute-start.5) | collective-permute-done | bytes 49184 | tf_op jit(solution)/shard_map/ppermute | solution.py:469
  57.7 1.2 %collective-permute-done.6.d = f32[48,256]{1,0:T(8,128)S(1)} collective-permute-done((f32[48,256]{1,0:T(8,128)S(1)}, f32[48,256]{1,0:T(8,128)S(1)}, u32[]{:S(2)}, u32[]{:S(2)}) %collective-permute-start.6) | collective-permute-done | bytes 49184 | tf_op jit(solution)/shard_map/ppermute | solution.py:469
  58.9 0.7 %shard_map.132 = f32[3,4096]{1,0:T(4,128)} custom-call(f32[48,256]{1,0:T(8,128)S(1)} %get-tuple-element.34.own_part, f32[48,256]{1,0:T(8,128)S(1)} %collective-permute-done.4.a, f32[48,256]{1,0:T(8,128)S(1)} %collective-permute-done.5.b, f32[48,256]{1,0:T(8,128)S(1)} %collective-permute-done.6.d), custom_call_target="tpu_custom_call" | custom-call | flops 100000000 | bytes 196608 | tf_op jit(solution)/shard_map/pallas_call | solution.py:316
  (1 shorter events, 0.0 us)
Async XLA Ops:
  3.5 16.7 %collective-permute-start = (f32[24,256]{1,0:T(8,128)S(1)}, f32[24,256]{1,0:T(8,128)S(1)}, u32[]{:S(2)}, u32[]{:S(2)}) collective-permute-start(f32[24,256]{1,0:T(8,128)S(1)} %get-tuple-element.20), channel_id=1, source_target_pairs={{0,4},{4,0},{8,12},{12,8},{16,20},{20,16},{24,28},{28,24},{32,36},... | collective-permute-start | bytes 73736 | tf_op jit(solution)/shard_map/ppermute | solution.py:449
  3.6 16.6 %collective-permute-start.1 = (f32[24,256]{1,0:T(8,128)S(1)}, f32[24,256]{1,0:T(8,128)S(1)}, u32[]{:S(2)}, u32[]{:S(2)}) collective-permute-start(f32[24,256]{1,0:T(8,128)S(1)} %get-tuple-element.21), channel_id=1, source_target_pairs={{0,0},{4,8},{8,4},{12,16},{16,12},{20,24},{24,20},{28,32},{32,28},... | collective-permute-start | bytes 73736 | tf_op jit(solution)/shard_map/ppermute | solution.py:450
  11.3 8.8 %copy-start.3 = (s32[20,768]{1,0:T(8,128)S(1)}, s32[20,768]{1,0:T(8,128)}, u32[]{:S(2)}) copy-start(s32[20,768]{1,0:T(8,128)} %connect.1) | copy-start | bytes 184324
  11.3 8.8 %copy-start.4 = (f32[60,60]{1,0:T(8,128)S(1)}, f32[60,60]{1,0:T(8,128)}, u32[]{:S(2)}) copy-start(f32[60,60]{1,0:T(8,128)} %k_shear.1) | copy-start | bytes 43204
  11.3 8.8 %copy-start.5 = (f32[60,60]{1,0:T(8,128)S(1)}, f32[60,60]{1,0:T(8,128)}, u32[]{:S(2)}) copy-start(f32[60,60]{1,0:T(8,128)} %k_bulk.1) | copy-start | bytes 43204
  11.3 8.8 %copy-start.6 = (f32[768]{0:T(1024)S(1)}, f32[768]{0:T(1024)}, u32[]{:S(2)}) copy-start(f32[768]{0:T(1024)} %shear.1) | copy-start | bytes 9220
  11.3 8.8 %copy-start.7 = (f32[768]{0:T(1024)S(1)}, f32[768]{0:T(1024)}, u32[]{:S(2)}) copy-start(f32[768]{0:T(1024)} %bulk.1) | copy-start | bytes 9220
  11.3 17.8 %all-to-all-start = ((f32[64,8,128]{2,1,0:T(8,128)}), f32[64,8,128]{2,1,0:T(8,128)S(1)}, u32[]{:S(2)}, u32[]{:S(2)}) async-start(f32[64,8,128]{2,1,0:T(8,128)} %bitcast.3), calls=%async_computation | async-start | bytes 524288 | tf_op jit(solution)/shard_map/all_to_all | solution.py:446
  20.2 9.0 %copy-start = (s32[8,2048]{1,0:T(8,128)S(1)}, s32[8,2048]{1,0:T(8,128)}, u32[]{:S(2)}) copy-start(s32[8,2048]{1,0:T(8,128)} %faces.1) | copy-start | bytes 196612
  31.8 17.5 %all-to-all-start.1 = ((f32[64,1,256]{2,1,0:T(1,128)}), f32[64,1,256]{2,1,0:T(1,128)S(1)}, u32[]{:S(2)}, u32[]{:S(2)}) async-start(f32[64,1,256]{2,1,0:T(1,128)} %get-tuple-element.24), calls=%async_computation.1 | async-start | bytes 131072 | tf_op jit(solution)/shard_map/all_to_all | solution.py:458
  41.8 4.8 %collective-permute-start.2 = (f32[24,256]{1,0:T(8,128)S(1)}, f32[24,256]{1,0:T(8,128)S(1)}, u32[]{:S(2)}, u32[]{:S(2)}) collective-permute-start(f32[24,256]{1,0:T(8,128)S(1)} %get-tuple-element.29), channel_id=1, source_target_pairs={{0,4},{4,0},{8,12},{12,8},{16,20},{20,16},{24,28},{28,24},{32,36},... | collective-permute-start | bytes 73736 | tf_op jit(solution)/shard_map/ppermute | solution.py:459
  42.0 7.2 %collective-permute-start.3 = (f32[24,256]{1,0:T(8,128)S(1)}, f32[24,256]{1,0:T(8,128)S(1)}, u32[]{:S(2)}, u32[]{:S(2)}) collective-permute-start(f32[24,256]{1,0:T(8,128)S(1)} %get-tuple-element.30), channel_id=1, source_target_pairs={{0,0},{4,8},{8,4},{12,16},{16,12},{20,24},{24,20},{28,32},{32,28},... | collective-permute-start | bytes 73736 | tf_op jit(solution)/shard_map/ppermute | solution.py:460
  45.1 4.2 %copy-start.1 = (s32[8,256]{1,0:T(8,128)S(1)}, s32[8,256]{1,0:T(8,128)}, u32[]{:S(2)}) copy-start(s32[8,256]{1,0:T(8,128)} %slave.1) | copy-start | bytes 24580
  45.1 4.2 %copy-start.2 = (f32[8,256]{1,0:T(8,128)S(1)}, f32[8,256]{1,0:T(8,128)}, u32[]{:S(2)}) copy-start(f32[8,256]{1,0:T(8,128)} %dual.1) | copy-start | bytes 24580
  50.5 5.7 %collective-permute-start.4 = (f32[48,256]{1,0:T(8,128)S(1)}, f32[48,256]{1,0:T(8,128)S(1)}, u32[]{:S(2)}, u32[]{:S(2)}) collective-permute-start(f32[48,256]{1,0:T(8,128)S(1)} %get-tuple-element.33), channel_id=1, source_target_pairs={{0,1},{1,2},{2,3},{3,0},{4,5},{5,6},{6,7},{7,4},{8,9},{9,10},{10,1... | collective-permute-start | bytes 147464 | tf_op jit(solution)/shard_map/ppermute | solution.py:469
  52.1 5.6 %collective-permute-start.5 = (f32[48,256]{1,0:T(8,128)S(1)}, f32[48,256]{1,0:T(8,128)S(1)}, u32[]{:S(2)}, u32[]{:S(2)}) collective-permute-start(f32[48,256]{1,0:T(8,128)S(1)} %get-tuple-element.32), channel_id=1, source_target_pairs={{0,2},{1,3},{2,0},{3,1},{4,6},{5,7},{6,4},{7,5},{8,10},{9,11},{10,... | collective-permute-start | bytes 147464 | tf_op jit(solution)/shard_map/ppermute | solution.py:469
  54.8 4.1 %collective-permute-start.6 = (f32[48,256]{1,0:T(8,128)S(1)}, f32[48,256]{1,0:T(8,128)S(1)}, u32[]{:S(2)}, u32[]{:S(2)}) collective-permute-start(f32[48,256]{1,0:T(8,128)S(1)} %get-tuple-element.31), channel_id=1, source_target_pairs={{0,3},{1,0},{2,1},{3,2},{4,7},{5,4},{6,5},{7,6},{8,11},{9,8},{10,9... | collective-permute-start | bytes 147464 | tf_op jit(solution)/shard_map/ppermute | solution.py:469

commit v7 on v6

--- a/solution.py
+++ b/solution.py
@@ -193,10 +193,9 @@
     p1 = payload.astype(BF16)
     rest = payload - p1.astype(F32)
     p2 = rest.astype(BF16)
-    p3 = (rest - p2.astype(F32)).astype(BF16)
     out[...] = lax.dot_general(
-        jnp.concatenate([place, place, place], axis=1),
-        jnp.concatenate([p1, p2, p3], axis=1),
+        jnp.concatenate([place, place], axis=1),
+        jnp.concatenate([p1, p2], axis=1),
         (((1,), (1,)), ((), ())),
         preferred_element_type=F32,
     )
@@ -262,13 +261,12 @@
     m1 = mult_rows.astype(BF16)
     rest = mult_rows - m1.astype(F32)
     m2 = rest.astype(BF16)
-    m3 = (rest - m2.astype(F32)).astype(BF16)
     hot = jnp.where(
         lax.broadcasted_iota(jnp.int32, (n_dom, segs), 0) == (slot[...] >> 3), 1.0, 0.0
     ).astype(BF16)
     picked = jnp.dot(
-        jnp.concatenate([m1, m2, m3], axis=1),
-        jnp.concatenate([hot, hot, hot], axis=0),
+        jnp.concatenate([m1, m2], axis=1),
+        jnp.concatenate([hot, hot], axis=0),
         preferred_element_type=F32,
     )
     rank = slot[...] & 7

time: 59.9 us -> 59.7 us (level)
  no operation moved by 1% of the time
where the time goes in v7:
time: 59.7 us; the launch traced here: 59.4 us
  starting transfers between devices  35.5 us (59%)
  Pallas kernels  17.6 us (29%)
  waiting for transfers between devices  5.3 us (9%)
  between operations  0.92 us (2%)
    pallas_call x6, Pallas kernels, call(): pl.pallas_call(kernel, out_shape=outs, in_specs=specs, out_specs=[pl.Bloc...  17.6 us
    ppermute x2, starting transfers between devices, on_device(): far = lax.ppermute(far, 'dom', far_pairs)  10.8 us
    all_to_all x1, starting transfers between devices, on_device(): lax.all_to_all(mult, 'dom', 0, 0, axis_index_groups=[group], tiled=True)  10 us
    all_to_all x1, starting transfers between devices, on_device(): lax.all_to_all(outgoing.reshape(n_dom, 8, 128), 'dom', 0, 0, axis_index_g...  8.75 us
    ppermute x3, starting transfers between devices, on_device(): lax.ppermute(lax.dynamic_index_in_dim(blocks, (me + k) % n_sub, 0, keepdi...  5.74 us
    ppermute x3, waiting for transfers between devices, on_device(): lax.ppermute(lax.dynamic_index_in_dim(blocks, (me + k) % n_sub, 0, keepdi...  2.66 us
    ppermute x2, waiting for transfers between devices, on_device(): far = lax.ppermute(far, 'dom', far_pairs)  2.63 us
  transfers between devices with their start and end apart: 9, of which 3 were waited for; matrix products, arithmetic and copies ran while one was open for 0% of the time, Pallas kernels for 18%

profile of v7, /device:TPU:8, one launch (start us, length us, event | category | flops | bytes accessed | tf_op | source)
XLA Modules:
  0.0 59.4 jit_solution(16257801188810863267)
XLA Ops:
  0.7 2.7 %shard_map.127 = (f32[512,128]{1,0:T(8,128)}, s32[1,256]{1,0:T(1,128)S(1)}, bf16[192,512]{1,0:T(8,128)(2,1)S(1)}, f32[24,256]{1,0:T(8,128)S(1)}, f32[24,256]{1,0:T(8,128)S(1)}) custom-call(f32[3,16384]{1,0:T(4,128)} %refs_0_.1, s32[8,256]{1,0:T(8,128)} %slave.1, f32[8,256]{1,0:T(8,128)} %dual.1, f32[64,256]{1,0:T(8,128)} %refs_3_.1, s32[1,256]{1,0:T(1,128)} %bitcast.15, ...), custom_call_target="tpu_custom_call" | custom-call | flops 100000000 | bytes 280580 | tf_op jit(solution)/shard_map/pallas_call | solution.py:314
  3.4 0.1 collective-permute-start
  3.5 7.7 %collective-permute-start.1 = (f32[24,256]{1,0:T(8,128)S(1)}, f32[24,256]{1,0:T(8,128)S(1)}, u32[]{:S(2)}, u32[]{:S(2)}) collective-permute-start(f32[24,256]{1,0:T(8,128)S(1)} %get-tuple-element.21), channel_id=1, source_target_pairs={{0,0},{4,8},{8,4},{12,16},{16,12},{20,24},{24,20},{28,32},{32,28},... | collective-permute-start | bytes 73736 | tf_op jit(solution)/shard_map/ppermute | solution.py:448
  11.2 0.0 copy-start.3
  11.2 0.0 copy-start.4
  11.2 0.0 copy-start.5
  11.2 0.0 copy-start.6
  11.2 0.0 copy-start.7
  11.3 8.7 %all-to-all-start = ((f32[64,8,128]{2,1,0:T(8,128)}), f32[64,8,128]{2,1,0:T(8,128)S(1)}, u32[]{:S(2)}, u32[]{:S(2)}) async-start(f32[64,8,128]{2,1,0:T(8,128)} %bitcast.3), calls=%async_computation | async-start | bytes 524288 | tf_op jit(solution)/shard_map/all_to_all | solution.py:444
  20.0 0.0 collective-permute-done.near
  20.0 0.0 collective-permute-done.1.far
  20.0 0.0 copy-done.3
  20.0 0.0 copy-done.4
  20.1 0.0 copy-done.5
  20.1 0.0 copy-done.6
  20.1 0.0 copy-done.7
  20.1 0.0 copy-start
  20.1 9.0 %shard_map.128 = (f32[192,256]{1,0:T(8,128)S(1)}, f32[24,256]{1,0:T(8,128)S(1)}, f32[24,256]{1,0:T(8,128)S(1)}) custom-call(bf16[192,512]{1,0:T(8,128)(2,1)S(1)} %get-tuple-element.19.own.table, f32[24,256]{1,0:T(8,128)S(1)} %collective-permute-done.near, f32[24,256]{1,0:T(8,128)S(1)} %collective-permute-done.1.far, s32[20,768]{1,0:T(8,128)S(1)} %copy-done.3, ...), custom_call_target="tpu_custom_call" | custom-call | flops 8000000000 | bytes 538752 | tf_op jit(solution)/shard_map/pallas_call | solution.py:314
  29.1 0.0 all-to-all-done
  29.1 0.0 copy-done
  29.1 2.6 %shard_map.129 = (f32[64,1,256]{2,1,0:T(1,128)}, f32[24,512]{1,0:T(8,128)S(1)}, s32[8,512]{1,0:T(8,128)S(1)}) custom-call(f32[512,128]{1,0:T(8,128)S(1)} %bitcast.14, bf16[192,512]{1,0:T(8,128)(2,1)S(1)} %get-tuple-element.19.own.table, s32[8,2048]{1,0:T(8,128)S(1)} %copy-done), custom_call_target="tpu_custom_call" | custom-call | flops 100000000 | bytes 720896 | tf_op jit(solution)/shard_map/pallas_call | solution.py:314
  31.7 10.0 %all-to-all-start.1 = ((f32[64,1,256]{2,1,0:T(1,128)}), f32[64,1,256]{2,1,0:T(1,128)S(1)}, u32[]{:S(2)}, u32[]{:S(2)}) async-start(f32[64,1,256]{2,1,0:T(1,128)} %get-tuple-element.24), calls=%async_computation.1 | async-start | bytes 131072 | tf_op jit(solution)/shard_map/all_to_all | solution.py:456
  41.8 0.2 collective-permute-start.2
  41.9 3.0 %collective-permute-start.3 = (f32[24,256]{1,0:T(8,128)S(1)}, f32[24,256]{1,0:T(8,128)S(1)}, u32[]{:S(2)}, u32[]{:S(2)}) collective-permute-start(f32[24,256]{1,0:T(8,128)S(1)} %get-tuple-element.30), channel_id=1, source_target_pairs={{0,0},{4,8},{8,4},{12,16},{16,12},{20,24},{24,20},{28,32},{32,28},... | collective-permute-start | bytes 73736 | tf_op jit(solution)/shard_map/ppermute | solution.py:458
  45.0 0.0 copy-start.1
  45.0 0.0 copy-start.2
  45.0 1.5 %shard_map.130.master = f32[192,256]{1,0:T(8,128)S(1)} custom-call(f32[24,512]{1,0:T(8,128)S(1)} %get-tuple-element.27.force, s32[8,512]{1,0:T(8,128)S(1)} %get-tuple-element.28.nodes), custom_call_target="tpu_custom_call" | custom-call | flops 100000000 | bytes 65536 | tf_op jit(solution)/shard_map/pallas_call | solution.py:314
  46.5 0.0 collective-permute-done.2.near
  46.5 2.6 %collective-permute-done.3.far = f32[24,256]{1,0:T(8,128)S(1)} collective-permute-done((f32[24,256]{1,0:T(8,128)S(1)}, f32[24,256]{1,0:T(8,128)S(1)}, u32[]{:S(2)}, u32[]{:S(2)}) %collective-permute-start.3) | collective-permute-done | bytes 24608 | tf_op jit(solution)/shard_map/ppermute | solution.py:458
  49.2 0.0 all-to-all-done.1.returned
  49.2 0.0 copy-done.1
  49.2 0.0 copy-done.2
  49.2 1.2 %shard_map.131 = f32[4,48,256]{2,1,0:T(8,128)S(1)} custom-call(f32[64,1,256]{2,1,0:T(1,128)S(1)} %all-to-all-done.1.returned, s32[1,256]{1,0:T(1,128)S(1)} %get-tuple-element.25.slot, f32[8,256]{1,0:T(8,128)S(1)} %copy-done.2, s32[8,256]{1,0:T(8,128)S(1)} %copy-done.1, f32[192,256]{1,0:T(8,128)S(1)} %get-tuple-element.26.owned, ...), custom_call_target="tpu_custom_call" | custom-call | flops 100000000 | bytes 525312 | tf_op jit(solution)/shard_map/pallas_call | solution.py:314
  50.4 1.6 %collective-permute-start.4 = (f32[48,256]{1,0:T(8,128)S(1)}, f32[48,256]{1,0:T(8,128)S(1)}, u32[]{:S(2)}, u32[]{:S(2)}) collective-permute-start(f32[48,256]{1,0:T(8,128)S(1)} %get-tuple-element.33), channel_id=1, source_target_pairs={{0,1},{1,2},{2,3},{3,0},{4,5},{5,6},{6,7},{7,4},{8,9},{9,10},{10,1... | collective-permute-start | bytes 147464 | tf_op jit(solution)/shard_map/ppermute | solution.py:467
  51.9 2.7 %collective-permute-start.5 = (f32[48,256]{1,0:T(8,128)S(1)}, f32[48,256]{1,0:T(8,128)S(1)}, u32[]{:S(2)}, u32[]{:S(2)}) collective-permute-start(f32[48,256]{1,0:T(8,128)S(1)} %get-tuple-element.32), channel_id=1, source_target_pairs={{0,2},{1,3},{2,0},{3,1},{4,6},{5,7},{6,4},{7,5},{8,10},{9,11},{10,... | collective-permute-start | bytes 147464 | tf_op jit(solution)/shard_map/ppermute | solution.py:467
  54.7 1.4 %collective-permute-start.6 = (f32[48,256]{1,0:T(8,128)S(1)}, f32[48,256]{1,0:T(8,128)S(1)}, u32[]{:S(2)}, u32[]{:S(2)}) collective-permute-start(f32[48,256]{1,0:T(8,128)S(1)} %get-tuple-element.31), channel_id=1, source_target_pairs={{0,3},{1,0},{2,1},{3,2},{4,7},{5,4},{6,5},{7,6},{8,11},{9,8},{10,9... | collective-permute-start | bytes 147464 | tf_op jit(solution)/shard_map/ppermute | solution.py:467
  56.1 0.0 collective-permute-done.4.a
  56.1 1.4 %collective-permute-done.5.b = f32[48,256]{1,0:T(8,128)S(1)} collective-permute-done((f32[48,256]{1,0:T(8,128)S(1)}, f32[48,256]{1,0:T(8,128)S(1)}, u32[]{:S(2)}, u32[]{:S(2)}) %collective-permute-start.5) | collective-permute-done | bytes 49184 | tf_op jit(solution)/shard_map/ppermute | solution.py:467
  57.5 1.2 %collective-permute-done.6.d = f32[48,256]{1,0:T(8,128)S(1)} collective-permute-done((f32[48,256]{1,0:T(8,128)S(1)}, f32[48,256]{1,0:T(8,128)S(1)}, u32[]{:S(2)}, u32[]{:S(2)}) %collective-permute-start.6) | collective-permute-done | bytes 49184 | tf_op jit(solution)/shard_map/ppermute | solution.py:467
  58.8 0.7 %shard_map.132 = f32[3,4096]{1,0:T(4,128)} custom-call(f32[48,256]{1,0:T(8,128)S(1)} %get-tuple-element.34.own_part, f32[48,256]{1,0:T(8,128)S(1)} %collective-permute-done.4.a, f32[48,256]{1,0:T(8,128)S(1)} %collective-permute-done.5.b, f32[48,256]{1,0:T(8,128)S(1)} %collective-permute-done.6.d), custom_call_target="tpu_custom_call" | custom-call | flops 100000000 | bytes 196608 | tf_op jit(solution)/shard_map/pallas_call | solution.py:314
  (1 shorter events, 0.0 us)
Async XLA Ops:
  3.4 16.7 %collective-permute-start = (f32[24,256]{1,0:T(8,128)S(1)}, f32[24,256]{1,0:T(8,128)S(1)}, u32[]{:S(2)}, u32[]{:S(2)}) collective-permute-start(f32[24,256]{1,0:T(8,128)S(1)} %get-tuple-element.20), channel_id=1, source_target_pairs={{0,4},{4,0},{8,12},{12,8},{16,20},{20,16},{24,28},{28,24},{32,36},... | collective-permute-start | bytes 73736 | tf_op jit(solution)/shard_map/ppermute | solution.py:447
  3.5 16.6 %collective-permute-start.1 = (f32[24,256]{1,0:T(8,128)S(1)}, f32[24,256]{1,0:T(8,128)S(1)}, u32[]{:S(2)}, u32[]{:S(2)}) collective-permute-start(f32[24,256]{1,0:T(8,128)S(1)} %get-tuple-element.21), channel_id=1, source_target_pairs={{0,0},{4,8},{8,4},{12,16},{16,12},{20,24},{24,20},{28,32},{32,28},... | collective-permute-start | bytes 73736 | tf_op jit(solution)/shard_map/ppermute | solution.py:448
  11.2 8.8 %copy-start.3 = (s32[20,768]{1,0:T(8,128)S(1)}, s32[20,768]{1,0:T(8,128)}, u32[]{:S(2)}) copy-start(s32[20,768]{1,0:T(8,128)} %connect.1) | copy-start | bytes 184324
  11.2 8.8 %copy-start.4 = (f32[60,60]{1,0:T(8,128)S(1)}, f32[60,60]{1,0:T(8,128)}, u32[]{:S(2)}) copy-start(f32[60,60]{1,0:T(8,128)} %k_shear.1) | copy-start | bytes 43204
  11.2 8.8 %copy-start.5 = (f32[60,60]{1,0:T(8,128)S(1)}, f32[60,60]{1,0:T(8,128)}, u32[]{:S(2)}) copy-start(f32[60,60]{1,0:T(8,128)} %k_bulk.1) | copy-start | bytes 43204
  11.2 8.8 %copy-start.6 = (f32[768]{0:T(1024)S(1)}, f32[768]{0:T(1024)}, u32[]{:S(2)}) copy-start(f32[768]{0:T(1024)} %shear.1) | copy-start | bytes 9220
  11.2 8.8 %copy-start.7 = (f32[768]{0:T(1024)S(1)}, f32[768]{0:T(1024)}, u32[]{:S(2)}) copy-start(f32[768]{0:T(1024)} %bulk.1) | copy-start | bytes 9220
  11.3 17.8 %all-to-all-start = ((f32[64,8,128]{2,1,0:T(8,128)}), f32[64,8,128]{2,1,0:T(8,128)S(1)}, u32[]{:S(2)}, u32[]{:S(2)}) async-start(f32[64,8,128]{2,1,0:T(8,128)} %bitcast.3), calls=%async_computation | async-start | bytes 524288 | tf_op jit(solution)/shard_map/all_to_all | solution.py:444
  20.1 9.0 %copy-start = (s32[8,2048]{1,0:T(8,128)S(1)}, s32[8,2048]{1,0:T(8,128)}, u32[]{:S(2)}) copy-start(s32[8,2048]{1,0:T(8,128)} %faces.1) | copy-start | bytes 196612
  31.7 17.5 %all-to-all-start.1 = ((f32[64,1,256]{2,1,0:T(1,128)}), f32[64,1,256]{2,1,0:T(1,128)S(1)}, u32[]{:S(2)}, u32[]{:S(2)}) async-start(f32[64,1,256]{2,1,0:T(1,128)} %get-tuple-element.24), calls=%async_computation.1 | async-start | bytes 131072 | tf_op jit(solution)/shard_map/all_to_all | solution.py:456
  41.8 4.8 %collective-permute-start.2 = (f32[24,256]{1,0:T(8,128)S(1)}, f32[24,256]{1,0:T(8,128)S(1)}, u32[]{:S(2)}, u32[]{:S(2)}) collective-permute-start(f32[24,256]{1,0:T(8,128)S(1)} %get-tuple-element.29), channel_id=1, source_target_pairs={{0,4},{4,0},{8,12},{12,8},{16,20},{20,16},{24,28},{28,24},{32,36},... | collective-permute-start | bytes 73736 | tf_op jit(solution)/shard_map/ppermute | solution.py:457
  41.9 7.2 %collective-permute-start.3 = (f32[24,256]{1,0:T(8,128)S(1)}, f32[24,256]{1,0:T(8,128)S(1)}, u32[]{:S(2)}, u32[]{:S(2)}) collective-permute-start(f32[24,256]{1,0:T(8,128)S(1)} %get-tuple-element.30), channel_id=1, source_target_pairs={{0,0},{4,8},{8,4},{12,16},{16,12},{20,24},{24,20},{28,32},{32,28},... | collective-permute-start | bytes 73736 | tf_op jit(solution)/shard_map/ppermute | solution.py:458
  45.0 4.2 %copy-start.1 = (s32[8,256]{1,0:T(8,128)S(1)}, s32[8,256]{1,0:T(8,128)}, u32[]{:S(2)}) copy-start(s32[8,256]{1,0:T(8,128)} %slave.1) | copy-start | bytes 24580
  45.0 4.2 %copy-start.2 = (f32[8,256]{1,0:T(8,128)S(1)}, f32[8,256]{1,0:T(8,128)}, u32[]{:S(2)}) copy-start(f32[8,256]{1,0:T(8,128)} %dual.1) | copy-start | bytes 24580
  50.4 5.7 %collective-permute-start.4 = (f32[48,256]{1,0:T(8,128)S(1)}, f32[48,256]{1,0:T(8,128)S(1)}, u32[]{:S(2)}, u32[]{:S(2)}) collective-permute-start(f32[48,256]{1,0:T(8,128)S(1)} %get-tuple-element.33), channel_id=1, source_target_pairs={{0,1},{1,2},{2,3},{3,0},{4,5},{5,6},{6,7},{7,4},{8,9},{9,10},{10,1... | collective-permute-start | bytes 147464 | tf_op jit(solution)/shard_map/ppermute | solution.py:467
  51.9 5.6 %collective-permute-start.5 = (f32[48,256]{1,0:T(8,128)S(1)}, f32[48,256]{1,0:T(8,128)S(1)}, u32[]{:S(2)}, u32[]{:S(2)}) collective-permute-start(f32[48,256]{1,0:T(8,128)S(1)} %get-tuple-element.32), channel_id=1, source_target_pairs={{0,2},{1,3},{2,0},{3,1},{4,6},{5,7},{6,4},{7,5},{8,10},{9,11},{10,... | collective-permute-start | bytes 147464 | tf_op jit(solution)/shard_map/ppermute | solution.py:467
  54.7 4.1 %collective-permute-start.6 = (f32[48,256]{1,0:T(8,128)S(1)}, f32[48,256]{1,0:T(8,128)S(1)}, u32[]{:S(2)}, u32[]{:S(2)}) collective-permute-start(f32[48,256]{1,0:T(8,128)S(1)} %get-tuple-element.31), channel_id=1, source_target_pairs={{0,3},{1,0},{2,1},{3,2},{4,7},{5,4},{6,5},{7,6},{8,11},{9,8},{10,9... | collective-permute-start | bytes 147464 | tf_op jit(solution)/shard_map/ppermute | solution.py:467
